TPU v7x, 256 devices: a whole 4x4x8 slice. The times are simulated.
256 devices in a mesh: dp: 8 (over z), tenant: 32 (over y, x, core).
Axes of the slice: x: 4, y: 4, z: 8, core: 2. Of those that a mesh axis runs over, the one named last changes fastest.
Arguments:
- tokens: bfloat16 [2048, 8192], P(('dp', 'tenant')), may hold values from -6 to 6
- tenant_ids: int32 [8, 256], P('dp', 'tenant'), may hold values from 0 to 31, never falling along the last dimension, each value on 1 to 16 neighbouring positions
- gate_weight: bfloat16 [8192, 16384], P('dp', 'tenant'), may hold values from -0.0625 to 0.0625
- up_weight: bfloat16 [8192, 16384], P('dp', 'tenant'), may hold values from -0.0625 to 0.0625
- adapter_in: bfloat16 [32, 32, 8192], P('tenant'), may hold values from -0.0625 to 0.0625
- adapter_out: bfloat16 [32, 2, 16, 16384], P('tenant'), may hold values from -0.75 to 0.75
- grad_hidden: bfloat16 [2048, 16384], P('dp', 'tenant'), may hold values from -6 to 6
Outputs:
- hidden: bfloat16 [2048, 16384], P('dp', 'tenant')
- grad_tokens: bfloat16 [2048, 8192], P(('dp', 'tenant'))
- grad_in: float32 [32, 32, 8192], P('tenant', None, 'dp')
- grad_out: float32 [32, 2, 16, 16384], P('tenant', None, None, 'dp')
Inputs may be any that keep to these rules, and one draw needn't show every extreme that they name: `tenant_ids`: within each batch the tenant numbers never fall along the row; every tenant has 1 to 16 tokens in each batch, and some tenant exactly 16.
All inputs are finite; a program needn't handle non-finite values.
Results may differ from a plain program's by a relative error of at most 0.019.
Values may be sent and summed in bfloat16 or wider, within the bound.
No kernel may reach another device: no remote copies, remote signals or barrier semaphores. Data moves between devices by JAX's collectives and lax.ppermute only.
A program may use at most 128 MiB of HBM per device.

v0:
```python
import jax
import jax.numpy as jnp
from jax import lax
from jax.sharding import PartitionSpec as P

adapter_scale = 2.0


def on_device(tokens, tenant_ids, gate_weight, up_weight, adapter_in, adapter_out, grad_hidden):
    all_rows, owner_ids = (
        lax.all_gather(tokens, "tenant", axis=0, tiled=True),
        lax.all_gather(tenant_ids, "tenant", axis=1, tiled=True),
    )
    gate_full, up_full = (
        lax.all_gather(gate_weight, "dp", axis=0, tiled=True),
        lax.all_gather(up_weight, "dp", axis=0, tiled=True),
    )
    owner_tenants = owner_ids[0]
    group_rows = all_rows.shape[0]
    number_of_tenants = lax.axis_size("tenant")
    adapter_inner_rank = adapter_out.shape[2]
    capacity = 2 * tokens.shape[0]
    my_index = lax.axis_index("tenant")
    tenant_range = jnp.arange(number_of_tenants, dtype=jnp.int32)
    tenant_indicator = owner_tenants[:, None] == tenant_range[None, :]
    counts = jnp.sum(tenant_indicator.astype(jnp.int32), axis=0)
    offsets = jnp.cumsum(counts) - counts
    row_offsets = jnp.sum(jnp.where(tenant_indicator, offsets[None, :], 0), axis=1)
    row_range = jnp.arange(group_rows, dtype=jnp.int32)
    slots = owner_tenants * capacity + row_range - row_offsets
    my_offset = jnp.sum(jnp.where(tenant_range == my_index, offsets, 0))
    my_count = jnp.sum(jnp.where(tenant_range == my_index, counts, 0))
    slot_range = jnp.arange(capacity, dtype=jnp.int32)
    own_valid = slot_range < my_count
    own_index = jnp.minimum(my_offset + slot_range, group_rows - 1)
    own_rows = jnp.take(all_rows, own_index, axis=0)
    local_adapter = adapter_in[0]
    own_low = lax.dot_general(
        own_rows, local_adapter, (((1,), (1,)), ((), ())), preferred_element_type=jnp.float32
    )
    own_low = jnp.where(own_valid[:, None], own_low, 0.0).astype(jnp.bfloat16)
    own_gate_delta = (
        adapter_scale
        * jnp.dot(
            own_low[:, :adapter_inner_rank], adapter_out[0, 0], preferred_element_type=jnp.float32
        )
    ).astype(jnp.bfloat16)
    own_up_delta = (
        adapter_scale
        * jnp.dot(
            own_low[:, adapter_inner_rank:], adapter_out[0, 1], preferred_element_type=jnp.float32
        )
    ).astype(jnp.bfloat16)
    gate_received, up_received = (
        lax.all_to_all(own_gate_delta, "tenant", split_axis=1, concat_axis=0, tiled=True),
        lax.all_to_all(own_up_delta, "tenant", split_axis=1, concat_axis=0, tiled=True),
    )
    gate_delta = jnp.take(gate_received, slots, axis=0)
    up_delta = jnp.take(up_received, slots, axis=0)
    gate_pre = jnp.dot(all_rows, gate_full, preferred_element_type=jnp.float32) + gate_delta.astype(
        jnp.float32
    )
    up_pre = jnp.dot(all_rows, up_full, preferred_element_type=jnp.float32) + up_delta.astype(
        jnp.float32
    )
    sigmoid_gate = jax.nn.sigmoid(gate_pre)
    silu_gate = gate_pre * sigmoid_gate
    hidden = (silu_gate * up_pre).astype(jnp.bfloat16)
    upstream = grad_hidden.astype(jnp.float32)
    grad_gate = (upstream * up_pre * sigmoid_gate * (1.0 + gate_pre * (1.0 - sigmoid_gate))).astype(
        jnp.bfloat16
    )
    grad_up = (upstream * silu_gate).astype(jnp.bfloat16)
    send_index = jnp.minimum(offsets[:, None] + slot_range[None, :], group_rows - 1).reshape(-1)
    send_valid = (slot_range[None, :] < counts[:, None]).reshape(-1)
    send_gate = jnp.where(
        send_valid[:, None], jnp.take(grad_gate, send_index, axis=0), jnp.zeros((), jnp.bfloat16)
    )
    send_up = jnp.where(
        send_valid[:, None], jnp.take(grad_up, send_index, axis=0), jnp.zeros((), jnp.bfloat16)
    )
    own_grad_gate, own_grad_up = (
        lax.all_to_all(send_gate, "tenant", split_axis=0, concat_axis=1, tiled=True),
        lax.all_to_all(send_up, "tenant", split_axis=0, concat_axis=1, tiled=True),
    )
    rank_pieces = []
    output_pieces = []
    for member, own_grad in enumerate((own_grad_gate, own_grad_up)):
        mapped_result = lax.dot_general(
            own_grad,
            adapter_out[0, member],
            (((1,), (1,)), ((), ())),
            preferred_element_type=jnp.float32,
        )
        rank_pieces.append(adapter_scale * mapped_result)
        matrix_product = lax.dot_general(
            own_low[:, member * adapter_inner_rank : (member + 1) * adapter_inner_rank],
            own_grad,
            (((0,), (0,)), ((), ())),
            preferred_element_type=jnp.float32,
        )
        output_pieces.append(adapter_scale * matrix_product)
    local_rank_gradient = jnp.concatenate(rank_pieces, axis=1).astype(jnp.bfloat16)
    own_grad_out = jnp.stack(output_pieces, axis=0)[None]
    own_grad_in = lax.dot_general(
        local_rank_gradient, own_rows, (((0,), (0,)), ((), ())), preferred_element_type=jnp.float32
    )
    adapter_token_rows = jnp.dot(
        local_rank_gradient, local_adapter, preferred_element_type=jnp.float32
    )
    row_location = jnp.minimum(row_range - row_offsets, capacity - 1)
    mine = owner_tenants == my_index
    summand_term = lax.dot_general(
        grad_gate, gate_full, (((1,), (1,)), ((), ())), preferred_element_type=jnp.float32
    )
    summand_term = summand_term + lax.dot_general(
        grad_up, up_full, (((1,), (1,)), ((), ())), preferred_element_type=jnp.float32
    )
    additional_term = jnp.take(adapter_token_rows, row_location, axis=0)
    grad_tokens = lax.psum_scatter(
        (
            summand_term
            + jnp.where(mine[:, None], additional_term, jnp.zeros_like(additional_term))
        ).astype(jnp.bfloat16),
        "tenant",
        scatter_dimension=0,
        tiled=True,
    )
    grad_in_part, grad_out_part = (
        lax.psum_scatter(
            own_grad_in[None].astype(jnp.bfloat16), "dp", scatter_dimension=2, tiled=True
        ).astype(jnp.float32),
        lax.psum_scatter(
            own_grad_out.astype(jnp.bfloat16), "dp", scatter_dimension=3, tiled=True
        ).astype(jnp.float32),
    )
    return (hidden, grad_tokens, grad_in_part, grad_out_part)


def solution(mesh):
    in_specs = (
        P(("dp", "tenant"), None),
        P("dp", "tenant"),
        P("dp", "tenant"),
        P("dp", "tenant"),
        P("tenant", None, None),
        P("tenant", None, None, None),
        P("dp", "tenant"),
    )
    out_specs = (
        P("dp", "tenant"),
        P(("dp", "tenant"), None),
        P("tenant", None, "dp"),
        P("tenant", None, None, "dp"),
    )
    return jax.shard_map(
        on_device, mesh=mesh, in_specs=in_specs, out_specs=out_specs, check_vma=False
    )
```

profile of v0, /device:TPU:16, one launch (start us, length us, event | category | flops | bytes accessed | tf_op | source)
XLA Modules:
  0.0 475.5 jit_solution(5912488822137609446)
XLA Ops:
  7.2 0.0 all-gather.4.cloned.1.call-start
  7.2 0.7 all-gather.4.cloned.1.call-update
  7.9 0.0 all-gather.6.cloned.1.call-start
  8.0 0.7 all-gather.6.cloned.1.call-update
  8.7 0.0 all-gather.8.cloned.1.call-start
  8.7 0.7 all-gather.8.cloned.1.call-update
  9.4 1.3 dynamic-slice
  11.3 0.8 bitcast_dynamic-update-slice_fusion
  12.1 14.3 %all-reduce = s32[256]{0:T(256)S(1)} all-reduce(s32[256]{0:T(256)S(1)} %bitcast_dynamic-update-slice_fusion), channel_id=1, replica_groups=mesh['dp'=8,'tenant'=32] {'tenant'}, use_global_device_ids=true, to_apply=%add | all-reduce | flops 256 | bytes 2048 | tf_op jit(solution)/shard_map/eq | solution.py:25
  26.4 0.1 convert_reduce_fusion
  26.6 0.1 iota_compare_fusion.1
  26.6 0.1 lt.89
  26.7 0.1 copy.24
  26.8 0.1 reduce-window.7
  26.9 0.1 reduce
  27.0 0.6 fusion.33
  27.6 0.1 add_minimum_fusion
  27.7 0.1 min.49
  27.8 0.7 fusion.34
  28.5 1.3 compare_and_fusion.3
  29.8 0.1 select_reduce_fusion
  29.9 33.6 %all-gather.4.cloned.1.call-done = bf16[256,8192]{1,0:T(8,128)(2,1)} async-done(((bf16[8,8192]{1,0:T(8,128)(2,1)}), bf16[256,8192]{1,0:T(8,128)(2,1)}) %all-gather.4.cloned.1.call-update) | async-done | bytes 4194320 | tf_op jit(solution)/shard_map/all_gather | solution.py:11
  63.5 3.7 gather_fusion
  67.1 0.3 fusion.9
  67.5 1.4 fusion.1
  68.9 0.9 copy.35
  69.7 6.5 %all-to-all-start.1 = ((bf16[16,32,512]{2,0,1:T(8,128)(2,1)}), bf16[16,32,512]{2,0,1:T(8,128)(2,1)S(1)}, u32[]{:S(2)}, u32[]{:S(2)}) async-start(bf16[16,32,512]{2,0,1:T(8,128)(2,1)} %bitcast.61), calls=%async_computation.1 | async-start | bytes 1048576 | tf_op jit(solution)/shard_map/all_to_all | solution.py:56
  76.3 0.3 fusion
  76.6 0.8 copy.36
  77.5 8.0 %all-to-all-done.1 = bf16[16,32,512]{2,0,1:T(8,128)(2,1)S(1)} async-done(((bf16[16,32,512]{2,0,1:T(8,128)(2,1)}), bf16[16,32,512]{2,0,1:T(8,128)(2,1)S(1)}, u32[]{:S(2)}, u32[]{:S(2)}) %all-to-all-start.1) | async-done | bytes 524320 | tf_op jit(solution)/shard_map/all_to_all | solution.py:56
  85.5 6.3 %all-to-all-start = ((bf16[16,32,512]{2,0,1:T(8,128)(2,1)}), bf16[16,32,512]{2,0,1:T(8,128)(2,1)S(1)}, u32[]{:S(2)}, u32[]{:S(2)}) async-start(bf16[16,32,512]{2,0,1:T(8,128)(2,1)} %bitcast.62), calls=%async_computation | async-start | bytes 1048576 | tf_op jit(solution)/shard_map/all_to_all | solution.py:55
  91.8 1.2 gather_fusion.3
  93.0 8.0 %all-to-all-done = bf16[16,32,512]{2,0,1:T(8,128)(2,1)S(1)} async-done(((bf16[16,32,512]{2,0,1:T(8,128)(2,1)}), bf16[16,32,512]{2,0,1:T(8,128)(2,1)S(1)}, u32[]{:S(2)}, u32[]{:S(2)}) %all-to-all-start) | async-done | bytes 524320 | tf_op jit(solution)/shard_map/all_to_all | solution.py:55
  100.9 1.2 gather_fusion.2
  102.1 57.7 %all-gather.6.cloned.1.call-done = bf16[8192,512]{1,0:T(8,128)(2,1)} async-done(((bf16[1024,512]{1,0:T(8,128)(2,1)}), bf16[8192,512]{1,0:T(8,128)(2,1)}) %all-gather.6.cloned.1.call-update) | async-done | bytes 8388624 | tf_op jit(solution)/shard_map/all_gather | solution.py:15
  159.8 7.8 %convolution_add_fusion.2 = f32[256,512]{1,0:T(8,128)} fusion(bf16[256,8192]{1,0:T(8,128)(2,1)} %all-gather.4.cloned.1.call-done, bf16[8192,512]{1,0:T(8,128)(2,1)} %all-gather.6.cloned.1.call-done, bf16[256,512]{1,0:T(8,128)(2,1)S(1)} %gather_fusion.2, pred[256]{0:T(512)(128)(4,1)S(1)} %get-tuple-element.6), kind=kOutput, calls=%fused_computation.22 | convolution fusion | flops 2147876864 | bytes 13369600 | tf_op jit(solution)/shard_map/dot_general | solution.py:60
  167.6 86.7 %all-gather.8.cloned.1.call-done = bf16[8192,512]{1,0:T(8,128)(2,1)} async-done(((bf16[1024,512]{1,0:T(8,128)(2,1)}), bf16[8192,512]{1,0:T(8,128)(2,1)}) %all-gather.8.cloned.1.call-update) | async-done | bytes 8388624 | tf_op jit(solution)/shard_map/all_gather | solution.py:16
  254.3 7.8 %fusion.14 = (bf16[256,512]{1,0:T(8,128)(2,1)S(1)}, bf16[256,512]{1,0:T(8,128)(2,1)}, bf16[256,512]{1,0:T(8,128)(2,1)S(1)}) fusion(bf16[256,512]{1,0:T(8,128)(2,1)S(1)} %copy-done.2, f32[256,512]{1,0:T(8,128)} %convolution_add_fusion.2, bf16[256,512]{1,0:T(8,128)(2,1)S(1)} %gather_fusion.3, pred[256]{0:T(512)(128)(4,1)S(1)} %get-tuple-element.6, ...), kind=kOutput, calls=%fused_computation.34 | convolution fusion | flops 2149974016 | bytes 14418176 | tf_op jit(solution)/shard_map/dot_general | solution.py:63
  262.2 2.0 gather_fusion.4
  264.1 2.0 gather_fusion.5
  266.1 1.0 select_select_fusion.1
  267.1 16.3 %all_to_all.76 = bf16[32,16,512]{2,1,0:T(8,128)(2,1)S(1)} all-to-all(bf16[32,16,512]{2,1,0:T(8,128)(2,1)S(1)} %bitcast.73), channel_id=1, replica_groups=mesh['dp'=8,'tenant'=32] {'tenant'}, dimensions={0} | all-to-all | bytes 1048576 | tf_op jit(solution)/shard_map/all_to_all | solution.py:84
  283.5 6.3 %all-to-all-start.2 = ((bf16[32,16,512]{2,1,0:T(8,128)(2,1)}), bf16[32,16,512]{2,1,0:T(8,128)(2,1)S(1)}, u32[]{:S(2)}, u32[]{:S(2)}) async-start(bf16[32,16,512]{2,1,0:T(8,128)(2,1)} %bitcast.11), calls=%async_computation.2 | async-start | bytes 1048576 | tf_op jit(solution)/shard_map/all_to_all | solution.py:83
  289.8 0.2 reduce-scatter.6.cloned.1.call-start
  290.1 0.4 fusion.4
  290.5 0.3 fusion.11
  290.8 8.1 %all-to-all-done.2 = bf16[32,16,512]{2,1,0:T(8,128)(2,1)S(1)} async-done(((bf16[32,16,512]{2,1,0:T(8,128)(2,1)}), bf16[32,16,512]{2,1,0:T(8,128)(2,1)S(1)}, u32[]{:S(2)}, u32[]{:S(2)}) %all-to-all-start.2) | async-done | bytes 524320 | tf_op jit(solution)/shard_map/all_to_all | solution.py:83
  299.0 0.3 fusion.10
  299.3 0.4 fusion.5
  299.7 1.2 fusion.8
  300.9 0.0 reduce-scatter.6.cloned.1.call-update
  300.9 0.0 reduce-scatter.8.cloned.1.call-start
  300.9 1.1 pad_maximum_fusion
  302.1 0.0 reduce-scatter.8.cloned.1.call-update
  302.1 0.0 reduce-scatter.4.cloned.1.call-start
  302.1 9.0 %fusion.39 = f32[256,8192]{1,0:T(8,128)} fusion(bf16[256,512]{1,0:T(8,128)(2,1)S(1)} %get-tuple-element.10, bf16[8192,512]{1,0:T(8,128)(2,1)} %all-gather.6.cloned.1.call-done), kind=kOutput, calls=%fused_computation.91 | convolution fusion | flops 2147483648 | bytes 17039360 | tf_op jit(solution)/shard_map/dot_general | solution.py:113
  311.1 0.3 fusion.20
  311.4 6.2 %gather_fusion.1 = f32[256,8192]{1,0:T(8,128)} fusion(f32[16,8192]{1,0:T(8,128)S(1)} %fusion.20, s32[1024]{0:T(1024)S(1)} %pad_clamp_fusion), kind=kCustom, calls=%fused_computation.5 | custom fusion | bytes 16778240 | tf_op jit(solution)/shard_map/jit(_take)/gather | solution.py:119
  317.6 12.9 %fusion.7 = bf16[256,8192]{1,0:T(8,128)(2,1)} fusion(f32[256,8192]{1,0:T(8,128)} %fusion.39, bf16[256,512]{1,0:T(8,128)(2,1)S(1)} %get-tuple-element.12, bf16[8192,512]{1,0:T(8,128)(2,1)} %all-gather.8.cloned.1.call-done, f32[256,8192]{1,0:T(8,128)} %gather_fusion.1, pred[256]{0:T(512)(128)(4,1)S(1)} %get-tuple-element.14, ...), kind=kOutput, calls=%fused_computation.18 | convolution fusion | flops 2157969408 | bytes 29622784 | tf_op jit(solution)/shard_map/dot_general | solution.py:116
  330.6 5.6 %reduce-scatter.6.cloned.1.call-done = bf16[1,32,1024]{2,1,0:T(8,128)(2,1)} async-done(((bf16[1,32,8192]{2,1,0:T(8,128)(2,1)}), bf16[1,32,1024]{2,1,0:T(8,128)(2,1)}) %reduce-scatter.6.cloned.1.call-update) | async-done | bytes 65552 | tf_op jit(solution)/shard_map/reduce_scatter | solution.py:130
  336.1 1.5 convert_element_type.68
  337.6 38.4 %reduce-scatter.8.cloned.1.call-done = bf16[1,2,16,2048]{3,2,1,0:T(8,128)(2,1)} async-done(((bf16[1,2,16,16384]{3,2,1,0:T(8,128)(2,1)}), bf16[1,2,16,2048]{3,2,1,0:T(8,128)(2,1)}) %reduce-scatter.8.cloned.1.call-update) | async-done | bytes 131088 | tf_op jit(solution)/shard_map/reduce_scatter | solution.py:133
  376.0 1.6 convert_element_type.69
  377.6 91.0 %reduce-scatter.4.cloned.1.call-done = bf16[8,8192]{1,0:T(8,128)(2,1)} async-done(((bf16[256,8192]{1,0:T(8,128)(2,1)}), bf16[8,8192]{1,0:T(8,128)(2,1)}) %reduce-scatter.4.cloned.1.call-update) | async-done | bytes 131088 | tf_op jit(solution)/shard_map/reduce_scatter | solution.py:120
  (18 shorter events, 0.2 us)
Async XLA Ops:
  7.2 60.0 %copy-start = (bf16[1,32,8192]{2,1,0:T(8,128)(2,1)S(1)}, bf16[1,32,8192]{2,1,0:T(8,128)(2,1)}, u32[]{:S(2)}) copy-start(bf16[1,32,8192]{2,1,0:T(8,128)(2,1)} %param.15) | copy-start | bytes 1572868
  7.2 69.1 %copy-start.1 = (bf16[1,2,16,16384]{3,2,1,0:T(8,128)(2,1)S(1)}, bf16[1,2,16,16384]{3,2,1,0:T(8,128)(2,1)}, u32[]{:S(2)}) copy-start(bf16[1,2,16,16384]{3,2,1,0:T(8,128)(2,1)} %param.16) | copy-start | bytes 3145732
  7.2 56.3 %all-gather.4.cloned.1.call-start = ((), (), s32[]{:S(2)}) async-start(), calls=%async_computation.7 | async-start | bytes 4325376 | tf_op jit(solution)/shard_map/all_gather | solution.py:11
  7.9 151.9 %all-gather.6.cloned.1.call-start = ((), (), s32[]{:S(2)}) async-start(), calls=%async_computation.8 | async-start | bytes 9437184 | tf_op jit(solution)/shard_map/all_gather | solution.py:15
  8.7 245.6 %all-gather.8.cloned.1.call-start = ((), (), s32[]{:S(2)}) async-start(), calls=%async_computation.9 | async-start | bytes 9437184 | tf_op jit(solution)/shard_map/all_gather | solution.py:16
  69.7 15.7 %all-to-all-start.1 = ((bf16[16,32,512]{2,0,1:T(8,128)(2,1)}), bf16[16,32,512]{2,0,1:T(8,128)(2,1)S(1)}, u32[]{:S(2)}, u32[]{:S(2)}) async-start(bf16[16,32,512]{2,0,1:T(8,128)(2,1)} %bitcast.61), calls=%async_computation.1 | async-start | bytes 1048576 | tf_op jit(solution)/shard_map/all_to_all | solution.py:56
  85.5 15.5 %all-to-all-start = ((bf16[16,32,512]{2,0,1:T(8,128)(2,1)}), bf16[16,32,512]{2,0,1:T(8,128)(2,1)S(1)}, u32[]{:S(2)}, u32[]{:S(2)}) async-start(bf16[16,32,512]{2,0,1:T(8,128)(2,1)} %bitcast.62), calls=%async_computation | async-start | bytes 1048576 | tf_op jit(solution)/shard_map/all_to_all | solution.py:55
  159.8 94.5 %copy-start.2 = (bf16[256,512]{1,0:T(8,128)(2,1)S(1)}, bf16[256,512]{1,0:T(8,128)(2,1)}, u32[]{:S(2)}) copy-start(bf16[256,512]{1,0:T(8,128)(2,1)} %param.17) | copy-start | bytes 786436
  283.5 15.5 %all-to-all-start.2 = ((bf16[32,16,512]{2,1,0:T(8,128)(2,1)}), bf16[32,16,512]{2,1,0:T(8,128)(2,1)S(1)}, u32[]{:S(2)}, u32[]{:S(2)}) async-start(bf16[32,16,512]{2,1,0:T(8,128)(2,1)} %bitcast.11), calls=%async_computation.2 | async-start | bytes 1048576 | tf_op jit(solution)/shard_map/all_to_all | solution.py:83
  289.8 46.4 %reduce-scatter.6.cloned.1.call-start = ((), (), s32[]{:S(2)}) async-start(), calls=%async_computation.11 | async-start | bytes 589824 | tf_op jit(solution)/shard_map/reduce_scatter | solution.py:130
  300.9 75.1 %reduce-scatter.8.cloned.1.call-start = ((), (), s32[]{:S(2)}) async-start(), calls=%async_computation.12 | async-start | bytes 1179648 | tf_op jit(solution)/shard_map/reduce_scatter | solution.py:133
  302.1 166.6 %reduce-scatter.4.cloned.1.call-start = ((), (), s32[]{:S(2)}) async-start(), calls=%async_computation.10 | async-start | bytes 4325376 | tf_op jit(solution)/shard_map/reduce_scatter | solution.py:120
Sparse Core Ops, SparseCore 0:
  10.6 52.8 all-gather.3
  65.2 94.5 all-gather.5
  161.6 92.6 all-gather.7
  301.0 35.0 reduce-scatter.5
  338.5 37.4 reduce-scatter.7
  380.4 88.2 reduce-scatter.3
where the time goes:
time: 476 us
  waiting for transfers between devices  339 us (71%)
  matrix products  42.4 us (9%)
  blocking collectives  30.7 us (6%)
  local copies, waits for them, and re-layouts  20.2 us (4%)
  starting transfers between devices  19.6 us (4%)
  between operations  15 us (3%)
  other arithmetic  8.47 us (2%)
    reduce_scatter x1, waiting for transfers between devices, on_device(): lax.psum_scatter((summand_term + jnp.where(mine[:, None], additional_term...  91 us
    all_gather x1, waiting for transfers between devices, on_device(): lax.all_gather(up_weight, 'dp', axis=0, tiled=True)  86.7 us
    all_gather x1, waiting for transfers between devices, on_device(): lax.all_gather(gate_weight, 'dp', axis=0, tiled=True)  57.7 us
    reduce_scatter x1, waiting for transfers between devices, on_device(): lax.psum_scatter(own_grad_out.astype(jnp.bfloat16), 'dp', scatter_dimensi...  38.4 us
    all_gather x1, waiting for transfers between devices, on_device(): lax.all_gather(tokens, 'tenant', axis=0, tiled=True)  33.6 us
    all_to_all x1, blocking collectives, on_device(): lax.all_to_all(send_up, 'tenant', split_axis=0, concat_axis=1, tiled=True)  16.3 us
    eq x1, blocking collectives, on_device(): tenant_indicator = owner_tenants[:, None] == tenant_range[None, :]  14.3 us
    dot_general x1, matrix products, on_device(): lax.dot_general(grad_up, up_full, (((1,), (1,)), ((), ())), preferred_ele...  12.9 us
  transfers between devices with their start and end apart: 9, of which 9 were waited for; matrix products, arithmetic and copies ran while one was open for 12% of the time, Pallas kernels for 0%

commit v1 on v0

v1 whole, which is shorter than its diff:
```python
import jax
import jax.numpy as jnp
from jax import lax
from jax.sharding import Mesh, PartitionSpec as P

adapter_scale = 2.0
bf16 = jnp.bfloat16
f32 = jnp.float32
CHIPS = ("y", "x")
CORE = "c"
GROUP = "z"
ORDER = (4, 3, 5, 2, 6, 1, 7, 0)


def contract(a, b, a_dim, b_dim):
    return lax.dot_general(a, b, (((a_dim,), (b_dim,)), ((), ())), preferred_element_type=f32)


def spread(block, axes, count):
    copies = jnp.broadcast_to(block[None], (count,) + block.shape)
    return lax.all_to_all(copies, axes, split_axis=0, concat_axis=0, tiled=True)


def on_device(tokens, tenant_ids, gate_weight, up_weight, adapter_in, adapter_out, grad_hidden):
    groups = lax.axis_size(GROUP)
    chips = lax.axis_size("y") * lax.axis_size("x")
    own_rows, width = tokens.shape
    depth, columns = gate_weight.shape
    rank = adapter_out.shape[2]
    rows = chips * own_rows
    chip_columns = 2 * columns
    z = lax.axis_index(GROUP)
    c = lax.axis_index(CORE)
    u = lax.axis_index("y") * lax.axis_size("x") + lax.axis_index("x")
    first_core = c == 0
    order = jnp.array(ORDER, jnp.int32)
    place_of = [ORDER.index(d) for d in range(groups)]
    group_at = (z + order) % groups
    place_at = jnp.array(place_of, jnp.int32)[(jnp.arange(groups) - z) % groups]
    swap = [(0, 1), (1, 0)]
    up_ring = [(i, (i + 1) % groups) for i in range(groups)]
    down_ring = [(i, (i - 1) % groups) for i in range(groups)]

    def other_core(value):
        return lax.ppermute(value, CORE, swap)

    def both(own, other):
        return jnp.where(first_core, own, other), jnp.where(first_core, other, own)

    ids = jnp.broadcast_to(tenant_ids.reshape(own_rows, 1, 1).astype(bf16), (own_rows, groups, 128))
    wide = jnp.concatenate([tokens.reshape(own_rows, groups, depth), ids], axis=2)
    sliced = lax.all_to_all(
        wide.reshape(own_rows, groups * (depth + 128)), GROUP, split_axis=1, concat_axis=0, tiled=True
    )
    sliced = jnp.take(sliced.reshape(groups, own_rows, depth + 128), group_at, axis=0)
    sliced = sliced.reshape(groups * own_rows, depth + 128)
    count = groups * own_rows
    id_columns = sliced[:, depth:]
    lane = lax.broadcasted_iota(jnp.int32, (count, 128), 1)
    row = lax.broadcasted_iota(jnp.int32, (count, 128), 0)
    id_lanes = jnp.sum(jnp.where(lane == row, id_columns.astype(f32), 0.0), axis=0, keepdims=True)
    id_block = jnp.broadcast_to(jnp.pad(id_lanes.astype(bf16), ((0, 0), (0, depth - 128))), (8, depth))
    gathered = spread(jnp.concatenate([sliced[:, :depth], id_block], axis=0), CHIPS, chips)
    token_rows = gathered[:, :count].reshape(chips, groups, own_rows, depth)
    token_rows = token_rows.transpose(1, 0, 2, 3).reshape(groups * rows, depth)
    row_ids = gathered[:, count, :count].astype(f32).astype(jnp.int32)
    row_ids = row_ids.reshape(chips, groups, own_rows).transpose(1, 0, 2).reshape(groups, rows)

    gates = both(gate_weight, other_core(gate_weight))
    ups = both(up_weight, other_core(up_weight))
    weight = jnp.concatenate(gates + ups, axis=1)
    by_core = grad_hidden.reshape(chips, 2, own_rows, columns)
    keep = lax.dynamic_index_in_dim(by_core, c, 1, keepdims=False)
    give = lax.dynamic_index_in_dim(by_core, 1 - c, 1, keepdims=False)
    upstream = jnp.concatenate(both(keep, other_core(give)), axis=2).reshape(rows, chip_columns)

    inner = lax.dynamic_slice_in_dim(adapter_in[0], z * depth, depth, axis=1)
    inner = jnp.concatenate([inner, other_core(inner)], axis=0)
    outer = lax.all_to_all(
        adapter_out.reshape(2 * rank, -1), CHIPS, split_axis=1, concat_axis=0, tiled=True
    )
    outers = (outer, other_core(outer))
    chip_range = jnp.arange(chips, dtype=jnp.int32)
    outer_tenants = (2 * chip_range + c, 2 * chip_range + 1 - c)
    my_tenants = (2 * u + c, 2 * u + 1 - c)

    def product(first, last):
        return contract(token_rows[first * rows : last * rows], weight, 1, 0)

    start = product(0, 1).astype(bf16)
    going_up = lax.ppermute(start[:, :chip_columns], GROUP, up_ring)
    going_down = lax.ppermute(start[:, chip_columns:], GROUP, down_ring)
    pair = product(1, 3)
    going_up = pair[:rows] + jnp.pad(going_up.astype(f32), ((0, 0), (0, chip_columns)))
    going_down = pair[rows:] + jnp.pad(going_down.astype(f32), ((0, 0), (chip_columns, 0)))
    going_up = lax.ppermute(going_up.astype(bf16), GROUP, up_ring)
    going_down = lax.ppermute(going_down.astype(bf16), GROUP, down_ring)
    for place in (3, 5):
        pair = product(place, place + 2)
        going_up = lax.ppermute((pair[:rows] + going_up.astype(f32)).astype(bf16), GROUP, up_ring)
        going_down = lax.ppermute((pair[rows:] + going_down.astype(f32)).astype(bf16), GROUP, down_ring)
    projected = product(groups - 1, groups) + going_up.astype(f32) + going_down.astype(f32)

    def mine(values, ids_of_rows):
        first = jnp.where(ids_of_rows == my_tenants[0], values[: 2 * rank], 0.0)
        return first, jnp.where(ids_of_rows == my_tenants[1], values[2 * rank :], 0.0)

    flat_ids = row_ids.reshape(1, groups * rows)
    low_parts = sum(mine(contract(inner, token_rows, 1, 1), flat_ids))
    low_parts = low_parts.reshape(2 * rank, groups, rows).transpose(1, 0, 2)
    low_parts = jnp.take(low_parts, place_at, axis=0)
    low_here = lax.all_to_all(low_parts, GROUP, split_axis=0, concat_axis=0, tiled=True)
    low_here = jnp.sum(low_here, axis=0).astype(bf16)
    low = jnp.sum(spread(low_here, CHIPS, chips).astype(f32), axis=0)

    here = row_ids[groups - 1]
    member_of = lax.broadcasted_iota(jnp.int32, (1, 2 * rank, 1), 1) // rank
    delta = 0.0
    for tenants, table in zip(outer_tenants, outers):
        chosen = (tenants[:, None, None] == here[None, None, :])
        placed = [
            jnp.where(chosen & (member_of == member), low[None], 0.0) for member in range(2)
        ]
        placed = jnp.concatenate(placed, axis=2).reshape(chips * 2 * rank, 2 * rows).astype(bf16)
        delta = delta + contract(placed, table, 0, 0)
    gate = projected[:, :chip_columns] + adapter_scale * delta[:rows]
    up = projected[:, chip_columns:] + adapter_scale * delta[rows:]
    sigmoid = jax.nn.sigmoid(gate)
    silu = gate * sigmoid
    hidden_rows = (silu * up).astype(bf16)
    upstream = upstream.astype(f32)
    grad_gate = (upstream * up * sigmoid * (1.0 + gate * (1.0 - sigmoid))).astype(bf16)
    grad_up = (upstream * silu).astype(bf16)
    grads = jnp.concatenate([grad_gate, grad_up], axis=1)

    halves = hidden_rows.reshape(chips, own_rows, 2, columns)
    keep = lax.dynamic_index_in_dim(halves, c, 2, keepdims=False)
    give = lax.dynamic_index_in_dim(halves, 1 - c, 2, keepdims=False)
    hidden = jnp.stack(both(keep, other_core(give)), axis=1).reshape(chips * 2 * own_rows, columns)

    grad_low = []
    for member, grad in enumerate((grad_gate, grad_up)):
        total = 0.0
        for tenants, table in zip(outer_tenants, outers):
            mapped = contract(table, grad, 1, 1).reshape(chips, 2, rank, rows)[:, member]
            total = total + jnp.sum(
                jnp.where(tenants[:, None, None] == here[None, None, :], mapped, 0.0), axis=0
            )
        grad_low.append(total)
    grad_low = (adapter_scale * jnp.concatenate(grad_low, axis=0)).astype(bf16)
    grad_low = jnp.sum(spread(grad_low, CHIPS, chips).astype(f32), axis=0)
    lows = jnp.concatenate([low, grad_low], axis=0).astype(bf16)
    lows = jnp.take(spread(lows, GROUP, groups), group_at, axis=0)
    lows = lows.transpose(1, 0, 2).reshape(4 * rank, groups * rows)
    all_low, all_grad_low = lows[: 2 * rank], lows[2 * rank :]
    own_grad_low = jnp.concatenate(
        mine(jnp.concatenate([all_grad_low, all_grad_low], axis=0), flat_ids), axis=0
    ).astype(bf16)

    grads_at = {0: grads}
    below = lax.ppermute(grads, GROUP, up_ring)
    above = lax.ppermute(grads, GROUP, down_ring)
    grads_at[7], grads_at[1] = below, above
    for step in (2, 3):
        below = lax.ppermute(below, GROUP, up_ring)
        above = lax.ppermute(above, GROUP, down_ring)
        grads_at[groups - step], grads_at[step] = below, above
    far_gate = lax.ppermute(below[:, :chip_columns], GROUP, up_ring)
    far_up = lax.ppermute(above[:, chip_columns:], GROUP, down_ring)
    grads_at[4] = jnp.concatenate([far_gate, far_up], axis=1)

    def back(first, last):
        parts = jnp.concatenate([grads_at[d] for d in ORDER[first:last]], axis=0)
        total = contract(parts, weight, 1, 1)
        return total + contract(own_grad_low[:, first * rows : last * rows], inner, 0, 0)

    def to_owners(first, last):
        part = back(first, last).astype(bf16).reshape(last - first, chips, own_rows, depth)
        part = part.transpose(1, 0, 2, 3).reshape(chips, (last - first) * own_rows, depth)
        got = lax.all_to_all(part, CHIPS, split_axis=0, concat_axis=0, tiled=True)
        return jnp.sum(got.astype(f32), axis=0).astype(bf16)

    near = to_owners(3, 8)
    far = to_owners(0, 3)
    summed = jnp.concatenate([far, near], axis=0).reshape(groups, own_rows, depth)
    summed = jnp.take(summed, place_at, axis=0).reshape(groups * own_rows, depth)
    grad_tokens = lax.all_to_all(summed, GROUP, split_axis=0, concat_axis=1, tiled=True)

    inner_grads = contract(own_grad_low, token_rows, 1, 0)
    grad_in = inner_grads[: 2 * rank] + other_core(inner_grads[2 * rank :])

    all_grads = jnp.concatenate([grads_at[d] for d in ORDER], axis=0)
    share = 2 * chips // groups
    out_tenants = share * z + jnp.arange(share, dtype=jnp.int32)
    chosen = out_tenants[:, None, None] == flat_ids[None]
    outs = []
    for member in range(2):
        placed = jnp.where(chosen, all_low[None, member * rank : (member + 1) * rank], jnp.zeros((), bf16))
        part = contract(
            placed.reshape(share * rank, groups * rows),
            all_grads[:, member * chip_columns : (member + 1) * chip_columns],
            1,
            0,
        )
        outs.append(part.reshape(share // 2, 2, rank, chip_columns))
    outs = jnp.stack(outs, axis=2)
    keep = lax.dynamic_index_in_dim(outs, c, 1, keepdims=False)
    give = lax.dynamic_index_in_dim(outs, 1 - c, 1, keepdims=False)
    outs = (keep + other_core(give.astype(bf16)).astype(f32)).astype(bf16)
    upper, lower = u // 2, u % 2
    same = lax.dynamic_index_in_dim(outs, lower, 0, keepdims=False)
    cross = lax.dynamic_index_in_dim(outs, 1 - lower, 0, keepdims=False)
    straight, crossed = [], []
    for from_z in range(groups):
        for from_u in range(chips):
            h, low_bit = from_u // 2, from_u % 2
            source = from_z * chips + from_u
            straight.append((source, h * chips + 2 * from_z + low_bit))
            crossed.append((source, h * chips + 2 * from_z + 1 - low_bit))
    same = lax.ppermute(same, (GROUP,) + CHIPS, straight)
    cross = lax.ppermute(cross, (GROUP,) + CHIPS, crossed)
    left = jnp.where(lower == 0, same, cross)
    right = jnp.where(lower == 0, cross, same)
    grad_out = adapter_scale * jnp.concatenate([left, right], axis=2).astype(f32)
    return hidden, grad_tokens, grad_in[None], grad_out[None]


def solution(mesh):
    groups, tenants = mesh.shape["dp"], mesh.shape["tenant"]
    split = Mesh(mesh.devices.reshape(groups, tenants // 8, 4, 2), ("z", "y", "x", "c"))
    tenant = ("y", "x", "c")
    in_specs = (
        P(("z",) + tenant, None),
        P("z", tenant),
        P("z", tenant),
        P("z", tenant),
        P(tenant, None, None),
        P(tenant, None, None, None),
        P("z", tenant),
    )
    out_specs = (
        P("z", tenant),
        P(("z",) + tenant, None),
        P(tenant, None, "z"),
        P(tenant, None, None, "z"),
    )
    return jax.shard_map(
        on_device, mesh=split, in_specs=in_specs, out_specs=out_specs, check_vma=False
    )
```

time: 476 us -> 299 us (0.63)
  waiting for transfers between devices: 339 us -> 79.1 us
  starting transfers between devices: 19.6 us -> 120 us
  blocking collectives: 30.7 us -> 0 us
  other arithmetic: 8.47 us -> 28.3 us
  between operations: 15 us -> 1.92 us
  local copies, waits for them, and re-layouts: 20.2 us -> 32.4 us
  matrix products: 42.4 us -> 32.4 us
    all_gather x3 -> x0, waiting for transfers between devices: 178 us -> none  [the longest x1 86.7 us: on_device(): lax.all_gather(up_weight, 'dp', axis=0, tiled=True)]
    reduce_scatter x3 -> x0, waiting for transfers between devices: 135 us -> none  [the longest x1 91 us: on_device(): lax.psum_scatter((summand_term + jnp.where(mine[:, None], additional_term...]
    all_to_all x3 -> x10, starting transfers between devices: 19.1 us -> 72.3 us  [the longest x4 26.9 us: spread(): return lax.all_to_all(copies, axes, split_axis=0, concat_axis=0, tiled=True)]
    ppermute x0 -> x26, starting transfers between devices: none -> 47.5 us  [the longest x2 13.5 us: on_device(): above = lax.ppermute(above, GROUP, down_ring)]
    all_to_all x3 -> x10, waiting for transfers between devices: 24.1 us -> 55.5 us  [the longest x4 30.6 us: spread(): return lax.all_to_all(copies, axes, split_axis=0, concat_axis=0, tiled=True)]
    ppermute x0 -> x26, waiting for transfers between devices: none -> 23.6 us  [the longest x2 8.3 us: on_device(): above = lax.ppermute(above, GROUP, down_ring)]
    all_to_all x1 -> x0, blocking collectives: 16.3 us -> none  [on_device(): lax.all_to_all(send_up, 'tenant', split_axis=0, concat_axis=1, tiled=True)]
    eq x1 -> x0, blocking collectives: 14.3 us -> none  [on_device(): tenant_indicator = owner_tenants[:, None] == tenant_range[None, :]]
  transfers between devices with their start and end apart: 9 -> 36, of which waited for: 9 -> 13; matrix products, arithmetic and copies ran while one was open for 12% -> 25% of each run, Pallas kernels for 0% -> 0%
where the time goes in v1:
time: 299 us; the launch traced here: 294 us
  starting transfers between devices  120 us (40%)
  waiting for transfers between devices  79.1 us (26%)
  local copies, waits for them, and re-layouts  32.4 us (11%)
  matrix products  32.4 us (11%)
  other arithmetic  28.3 us (9%)
    dot_general x19, matrix products, contract(): lax.dot_general(a, b, (((a_dim,), (b_dim,)), ((), ())), preferred_element...  32.4 us
    all_to_all x4, waiting for transfers between devices, spread(): return lax.all_to_all(copies, axes, split_axis=0, concat_axis=0, tiled=True)  30.6 us
    all_to_all x4, starting transfers between devices, spread(): return lax.all_to_all(copies, axes, split_axis=0, concat_axis=0, tiled=True)  26.9 us
    all_to_all x2, starting transfers between devices, to_owners(): got = lax.all_to_all(part, CHIPS, split_axis=0, concat_axis=0, tiled=True)  14.7 us
    ppermute x2, starting transfers between devices, on_device(): above = lax.ppermute(above, GROUP, down_ring)  13.5 us
    unnamed x97, local copies, waits for them, and re-layouts  11.9 us
    all_to_all x1, waiting for transfers between devices, on_device(): lax.all_to_all(adapter_out.reshape(2 * rank, -1), CHIPS, split_axis=1, co...  11.2 us
    all_to_all x1, starting transfers between devices, on_device(): lax.all_to_all(summed, GROUP, split_axis=0, concat_axis=1, tiled=True)  9.65 us
  transfers between devices with their start and end apart: 36, of which 13 were waited for; matrix products, arithmetic and copies ran while one was open for 25% of the time, Pallas kernels for 0%

profile of v1, /device:TPU:16, one launch (start us, length us, event | category | flops | bytes accessed | tf_op | source)
XLA Modules:
  0.0 293.9 jit_solution(5255583745852306269)
XLA Ops:
  1.5 1.6 pad_maximum_fusion.3
  3.0 8.5 %all-to-all-start = ((bf16[8,8,1152]{2,0,1:T(8,128)(2,1)}), bf16[8,8,1152]{2,0,1:T(8,128)(2,1)S(1)}, u32[]{:S(2)}, u32[]{:S(2)}) async-start(bf16[8,8,1152]{2,0,1:T(8,128)(2,1)} %pad_maximum_fusion.3), calls=%async_computation | async-start | bytes 294912 | tf_op jit(solution)/shard_map/all_to_all | solution.py:52
  11.5 1.8 copy.155
  13.3 1.6 copy.131
  15.6 5.4 %all-to-all-done = bf16[8,8,1152]{2,0,1:T(8,128)(2,1)S(1)} async-done(((bf16[8,8,1152]{2,0,1:T(8,128)(2,1)}), bf16[8,8,1152]{2,0,1:T(8,128)(2,1)S(1)}, u32[]{:S(2)}, u32[]{:S(2)}) %all-to-all-start) | async-done | bytes 147488 | tf_op jit(solution)/shard_map/all_to_all | solution.py:52
  20.9 7.3 %all-to-all-start.4 = ((bf16[32,16,1024]{2,0,1:T(8,128)(2,1)}), bf16[32,16,1024]{2,0,1:T(8,128)(2,1)}, u32[]{:S(2)}, u32[]{:S(2)}) async-start(bf16[32,16,1024]{2,0,1:T(8,128)(2,1)} %copy.131), calls=%async_computation.4 | async-start | bytes 2097152 | tf_op jit(solution)/shard_map/all_to_all | solution.py:79
  30.3 11.2 %all-to-all-done.4 = bf16[32,16,1024]{2,0,1:T(8,128)(2,1)} async-done(((bf16[32,16,1024]{2,0,1:T(8,128)(2,1)}), bf16[32,16,1024]{2,0,1:T(8,128)(2,1)}, u32[]{:S(2)}, u32[]{:S(2)}) %all-to-all-start.4) | async-done | bytes 1048608 | tf_op jit(solution)/shard_map/all_to_all | solution.py:79
  41.5 1.7 broadcast_in_dim.231
  43.2 6.2 %all-to-all-start.1 = ((bf16[16,72,1024]{2,1,0:T(8,128)(2,1)}), bf16[16,72,1024]{2,1,0:T(8,128)(2,1)S(1)}, u32[]{:S(2)}, u32[]{:S(2)}) async-start(bf16[16,72,1024]{2,1,0:T(8,128)(2,1)} %broadcast_in_dim.231), calls=%async_computation.1 | async-start | bytes 4718592 | tf_op jit(solution)/shard_map/all_to_all | solution.py:21
  54.0 1.7 broadcast_select_fusion.3
  55.7 1.4 broadcast_select_fusion.1
  57.0 2.3 pad_maximum_fusion
  59.4 17.8 %all-to-all-done.1 = bf16[16,72,1024]{2,1,0:T(8,128)(2,1)S(1)} async-done(((bf16[16,72,1024]{2,1,0:T(8,128)(2,1)}), bf16[16,72,1024]{2,1,0:T(8,128)(2,1)S(1)}, u32[]{:S(2)}, u32[]{:S(2)}) %all-to-all-start.1) | async-done | bytes 2359328 | tf_op jit(solution)/shard_map/all_to_all | solution.py:21
  77.4 1.2 copy-done.10
  78.7 2.0 slice_bitcast_fusion.4
  83.3 2.6 collective-permute-start.2
  89.7 3.4 %fusion.99 = f32[256,2048]{1,0:T(8,128)S(1)} fusion(bf16[256,1024]{1,0:T(8,128)(2,1)S(1)} %bitcast.255, bf16[1024,2048]{1,0:T(8,128)(2,1)} %pad_maximum_fusion), kind=kOutput, calls=%fused_computation.237 | convolution fusion | flops 1073741824 | bytes 6815744 | tf_op jit(solution)/shard_map/dot_general | solution.py:16
  93.9 1.2 fusion.18
  95.1 1.4 collective-permute-start.3
  96.5 2.2 collective-permute-start.7
  99.4 5.3 %all-to-all-start.2 = ((f32[8,32,128]{2,1,0:T(8,128)}), f32[8,32,128]{2,1,0:T(8,128)S(1)}, u32[]{:S(2)}, u32[]{:S(2)}) async-start(f32[8,32,128]{2,1,0:T(8,128)} %broadcast_select_fusion.5), calls=%async_computation.2 | async-start | bytes 262144 | tf_op jit(solution)/shard_map/all_to_all | solution.py:112
  104.7 3.7 %fusion.98 = f32[256,2048]{1,0:T(8,128)S(1)} fusion(bf16[256,1024]{1,0:T(8,128)(2,1)} %bitcast.254, bf16[1024,2048]{1,0:T(8,128)(2,1)} %pad_maximum_fusion), kind=kOutput, calls=%fused_computation.236 | convolution fusion | flops 1073741824 | bytes 6815744 | tf_op jit(solution)/shard_map/dot_general | solution.py:16
  108.4 2.5 fusion.19
  110.8 2.0 collective-permute-start.4
  112.8 1.2 collective-permute-start.8
  114.1 2.6 fusion.97
  118.3 8.4 %all-to-all-start.3 = ((bf16[16,32,128]{2,1,0:T(8,128)(2,1)}), bf16[16,32,128]{2,1,0:T(8,128)(2,1)S(1)}, u32[]{:S(2)}, u32[]{:S(2)}) async-start(bf16[16,32,128]{2,1,0:T(8,128)(2,1)} %broadcast_in_dim.237), calls=%async_computation.3 | async-start | bytes 262144 | tf_op jit(solution)/shard_map/all_to_all | solution.py:21
  127.4 4.9 %all-to-all-done.3 = bf16[16,32,128]{2,1,0:T(8,128)(2,1)S(1)} async-done(((bf16[16,32,128]{2,1,0:T(8,128)(2,1)}), bf16[16,32,128]{2,1,0:T(8,128)(2,1)S(1)}, u32[]{:S(2)}, u32[]{:S(2)}) %all-to-all-start.3) | async-done | bytes 131104 | tf_op jit(solution)/shard_map/all_to_all | solution.py:21
  133.2 2.0 fusion.20
  135.3 3.2 %collective-permute-start.9 = (bf16[128,2048]{1,0:T(8,128)(2,1)S(1)}, bf16[128,2048]{1,0:T(8,128)(2,1)S(1)}, u32[]{:S(2)}, u32[]{:S(2)}) collective-permute-start(bf16[128,2048]{1,0:T(8,128)(2,1)S(1)} %get-tuple-element.14), channel_id=1, source_target_pairs={{0,224},{32,0},{64,32},{96,64},{128,96},{160,128},{192,160},{224,1... | collective-permute-start | bytes 1572872 | tf_op jit(solution)/shard_map/ppermute | solution.py:101
  138.5 1.7 fusion.38
  140.2 1.7 convolution_add_fusion.1
  141.9 3.7 %collective-permute-done.5 = bf16[128,2048]{1,0:T(8,128)(2,1)S(1)} collective-permute-done((bf16[128,2048]{1,0:T(8,128)(2,1)S(1)}, bf16[128,2048]{1,0:T(8,128)(2,1)S(1)}, u32[]{:S(2)}, u32[]{:S(2)}) %collective-permute-start.5) | collective-permute-done | bytes 524320 | tf_op jit(solution)/shard_map/ppermute | solution.py:100
  146.9 1.7 convolution_bitcast_fusion.3
  149.5 3.2 %collective-permute-start.18 = (bf16[128,2048]{1,0:T(8,128)(2,1)}, bf16[128,2048]{1,0:T(8,128)(2,1)S(1)}, u32[]{:S(2)}, u32[]{:S(2)}) collective-permute-start(bf16[128,2048]{1,0:T(8,128)(2,1)} %pad_maximum_fusion.1), channel_id=1, source_target_pairs={{0,224},{32,0},{64,32},{96,64},{128,96},{160,128},{192,160},{224,1... | collective-permute-start | bytes 1572872 | tf_op jit(solution)/shard_map/ppermute | solution.py:162
  152.8 1.7 convolution_bitcast_fusion.2
  154.7 1.7 convolution_bitcast_fusion
  156.7 1.7 convolution_bitcast_fusion.1
  159.3 5.9 %all-to-all-start.5 = ((bf16[16,32,128]{2,1,0:T(8,128)(2,1)}), bf16[16,32,128]{2,1,0:T(8,128)(2,1)S(1)}, u32[]{:S(2)}, u32[]{:S(2)}) async-start(bf16[16,32,128]{2,1,0:T(8,128)(2,1)} %broadcast_in_dim.246), calls=%async_computation.5 | async-start | bytes 262144 | tf_op jit(solution)/shard_map/all_to_all | solution.py:21
  165.2 13.3 %collective-permute-start.19 = (bf16[128,2048]{1,0:T(8,128)(2,1)S(1)}, bf16[128,2048]{1,0:T(8,128)(2,1)S(1)}, u32[]{:S(2)}, u32[]{:S(2)}) collective-permute-start(bf16[128,2048]{1,0:T(8,128)(2,1)S(1)} %collective-permute-done.18), channel_id=1, source_target_pairs={{0,224},{32,0},{64,32},{96,64},{128,96},{160,128},{192,160},{224,1... | collective-permute-start | bytes 1572872 | tf_op jit(solution)/shard_map/ppermute | solution.py:166
  178.5 1.4 broadcast_compare_fusion
  180.6 6.3 %all-to-all-start.6 = ((bf16[8,64,128]{2,1,0:T(8,128)(2,1)}), bf16[8,64,128]{2,1,0:T(8,128)(2,1)S(1)}, u32[]{:S(2)}, u32[]{:S(2)}) async-start(bf16[8,64,128]{2,1,0:T(8,128)(2,1)} %broadcast_in_dim.247), calls=%async_computation.6 | async-start | bytes 262144 | tf_op jit(solution)/shard_map/all_to_all | solution.py:21
  188.6 7.9 %all-to-all-done.6 = bf16[8,64,128]{2,1,0:T(8,128)(2,1)S(1)} async-done(((bf16[8,64,128]{2,1,0:T(8,128)(2,1)}), bf16[8,64,128]{2,1,0:T(8,128)(2,1)S(1)}, u32[]{:S(2)}, u32[]{:S(2)}) %all-to-all-start.6) | async-done | bytes 131104 | tf_op jit(solution)/shard_map/all_to_all | solution.py:21
  197.5 1.8 collective-permute-start.16
  202.0 8.3 %collective-permute-done.20 = bf16[128,2048]{1,0:T(8,128)(2,1)S(1)} collective-permute-done((bf16[128,2048]{1,0:T(8,128)(2,1)S(1)}, bf16[128,2048]{1,0:T(8,128)(2,1)S(1)}, u32[]{:S(2)}, u32[]{:S(2)}) %collective-permute-start.20) | collective-permute-done | bytes 524320 | tf_op jit(solution)/shard_map/ppermute | solution.py:166
  210.3 1.6 collective-permute-start.21
  212.9 2.0 fusion.67
  214.9 2.0 collective-permute-done.21
  217.0 2.7 collective-permute-done.17
  219.7 1.9 add_convert_fusion.1
  222.6 7.4 %all-to-all-start.7 = ((bf16[16,24,1024]{2,1,0:T(8,128)(2,1)}), bf16[16,24,1024]{2,1,0:T(8,128)(2,1)S(1)}, u32[]{:S(2)}, u32[]{:S(2)}) async-start(bf16[16,24,1024]{2,1,0:T(8,128)(2,1)} %bitcast.236), calls=%async_computation.7 | async-start | bytes 1572864 | tf_op jit(solution)/shard_map/all_to_all | solution.py:180
  230.0 1.0 constant_dynamic-update-slice_fusion.13
  232.2 1.3 constant_dynamic-update-slice_fusion.8
  234.1 2.2 copy-done.7
  236.3 2.9 add_convert_fusion
  239.2 1.2 copy.164
  240.9 7.4 %all-to-all-start.8 = ((bf16[16,40,1024]{2,1,0:T(8,128)(2,1)}), bf16[16,40,1024]{2,1,0:T(8,128)(2,1)}, u32[]{:S(2)}, u32[]{:S(2)}) async-start(bf16[16,40,1024]{2,1,0:T(8,128)(2,1)} %bitcast.241), calls=%async_computation.8 | async-start | bytes 2621440 | tf_op jit(solution)/shard_map/all_to_all | solution.py:180
  248.3 2.1 fusion.13
  252.8 5.8 %collective-permute-start.24 = (bf16[2,16,1024]{2,1,0:T(8,128)(2,1)S(1)}, bf16[2,16,1024]{2,1,0:T(8,128)(2,1)S(1)}, u32[]{:S(2)}, u32[]{:S(2)}) collective-permute-start(bf16[2,16,1024]{2,1,0:T(8,128)(2,1)S(1)} %get-tuple-element.44), channel_id=1, source_target_pairs={{0,0},{2,2},{4,32},{6,34},{8,64},{10,66},{12,96},{14,98},{16,128},... | collective-permute-start | bytes 196616 | tf_op jit(solution)/shard_map/ppermute | solution.py:220
  258.6 5.4 %collective-permute-start.25 = (bf16[2,16,1024]{2,1,0:T(8,128)(2,1)S(1)}, bf16[2,16,1024]{2,1,0:T(8,128)(2,1)S(1)}, u32[]{:S(2)}, u32[]{:S(2)}) collective-permute-start(bf16[2,16,1024]{2,1,0:T(8,128)(2,1)S(1)} %get-tuple-element.45), channel_id=1, source_target_pairs={{0,2},{2,0},{4,34},{6,32},{8,66},{10,64},{12,98},{14,96},{16,130},... | collective-permute-start | bytes 196616 | tf_op jit(solution)/shard_map/ppermute | solution.py:221
  265.3 5.9 %collective-permute-done.25 = bf16[2,16,1024]{2,1,0:T(8,128)(2,1)S(1)} collective-permute-done((bf16[2,16,1024]{2,1,0:T(8,128)(2,1)S(1)}, bf16[2,16,1024]{2,1,0:T(8,128)(2,1)S(1)}, u32[]{:S(2)}, u32[]{:S(2)}) %collective-permute-start.25) | collective-permute-done | bytes 65568 | tf_op jit(solution)/shard_map/ppermute | solution.py:221
  271.3 1.6 reduce_sum.105
  274.3 9.6 %all-to-all-start.9 = ((bf16[8,8,1024]{2,1,0:T(8,128)(2,1)}), bf16[8,8,1024]{2,1,0:T(8,128)(2,1)S(1)}, u32[]{:S(2)}, u32[]{:S(2)}) async-start(bf16[8,8,1024]{2,1,0:T(8,128)(2,1)} %broadcast_select_fusion.4), calls=%async_computation.9 | async-start | bytes 262144 | tf_op jit(solution)/shard_map/all_to_all | solution.py:187
  284.7 8.4 %all-to-all-done.9 = bf16[8,8,1024]{2,1,0:T(8,128)(2,1)S(1)} async-done(((bf16[8,8,1024]{2,1,0:T(8,128)(2,1)}), bf16[8,8,1024]{2,1,0:T(8,128)(2,1)S(1)}, u32[]{:S(2)}, u32[]{:S(2)}) %all-to-all-start.9) | async-done | bytes 131104 | tf_op jit(solution)/shard_map/all_to_all | solution.py:187
  (227 shorter events, 39.4 us)
Async XLA Ops:
  0.6 48.8 %copy-start = (bf16[1,32,8192]{2,1,0:T(8,128)(2,1)S(1)}, bf16[1,32,8192]{2,1,0:T(8,128)(2,1)}, u32[]{:S(2)}) copy-start(bf16[1,32,8192]{2,1,0:T(8,128)(2,1)} %param.13) | copy-start | bytes 1572868
  0.6 14.3 %copy-start.2 = (s32[8]{0:T(128)S(1)}, s32[8]{0:T(128)}, u32[]{:S(2)}) copy-start(s32[8]{0:T(128)} %constant.179.clone) | copy-start | bytes 100
  3.0 17.9 %all-to-all-start = ((bf16[8,8,1152]{2,0,1:T(8,128)(2,1)}), bf16[8,8,1152]{2,0,1:T(8,128)(2,1)S(1)}, u32[]{:S(2)}, u32[]{:S(2)}) async-start(bf16[8,8,1152]{2,0,1:T(8,128)(2,1)} %pad_maximum_fusion.3), calls=%async_computation | async-start | bytes 294912 | tf_op jit(solution)/shard_map/all_to_all | solution.py:52
  11.5 16.7 %copy-start.40 = (s32[8]{0:T(128)S(1)}, s32[8]{0:T(128)}, u32[]{:S(2)}) copy-start(s32[8]{0:T(128)} %constant.178.clone) | copy-start | bytes 100
  20.9 20.6 %all-to-all-start.4 = ((bf16[32,16,1024]{2,0,1:T(8,128)(2,1)}), bf16[32,16,1024]{2,0,1:T(8,128)(2,1)}, u32[]{:S(2)}, u32[]{:S(2)}) async-start(bf16[32,16,1024]{2,0,1:T(8,128)(2,1)} %copy.131), calls=%async_computation.4 | async-start | bytes 2097152 | tf_op jit(solution)/shard_map/all_to_all | solution.py:79
  30.3 19.8 %copy-start.26 = (bf16[256,512]{1,0:T(8,128)(2,1)S(1)}, bf16[256,512]{1,0:T(8,128)(2,1)}, u32[]{:S(2)}) copy-start(bf16[256,512]{1,0:T(8,128)(2,1)} %param.15) | copy-start | bytes 786436
  43.2 34.0 %all-to-all-start.1 = ((bf16[16,72,1024]{2,1,0:T(8,128)(2,1)}), bf16[16,72,1024]{2,1,0:T(8,128)(2,1)S(1)}, u32[]{:S(2)}, u32[]{:S(2)}) async-start(bf16[16,72,1024]{2,1,0:T(8,128)(2,1)} %broadcast_in_dim.231), calls=%async_computation.1 | async-start | bytes 4718592 | tf_op jit(solution)/shard_map/all_to_all | solution.py:21
  49.4 4.6 %collective-permute-start = (bf16[1024,512]{1,0:T(8,128)(2,1)}, bf16[1024,512]{1,0:T(8,128)(2,1)}, u32[]{:S(2)}, u32[]{:S(2)}) collective-permute-start(bf16[1024,512]{1,0:T(8,128)(2,1)} %param.11), channel_id=1, source_target_pairs={{0,1},{1,0},{2,3},{3,2},{4,5},{5,4},{6,7},{7,6},{8,9},{9,8},{10,11... | collective-permute-start | bytes 3145736 | tf_op jit(solution)/shard_map/ppermute | solution.py:45
  49.5 38.8 %collective-permute-start.10 = (bf16[32,1024]{1,0:T(8,128)(2,1)S(1)}, bf16[32,1024]{1,0:T(8,128)(2,1)S(1)}, u32[]{:S(2)}, u32[]{:S(2)}) collective-permute-start(bf16[32,1024]{1,0:T(8,128)(2,1)S(1)} %dynamic-slice_bitcast_fusion.4), channel_id=1, source_target_pairs={{0,1},{1,0},{2,3},{3,2},{4,5},{5,4},{6,7},{7,6},{8,9},{9,8},{10,11... | collective-permute-start | bytes 196616 | tf_op jit(solution)/shard_map/ppermute | solution.py:45
  50.0 3.1 %collective-permute-start.13 = (bf16[16,8,512]{2,1,0:T(8,128)(2,1)S(1)}, bf16[16,8,512]{2,1,0:T(8,128)(2,1)S(1)}, u32[]{:S(2)}, u32[]{:S(2)}) collective-permute-start(bf16[16,8,512]{2,1,0:T(8,128)(2,1)S(1)} %dynamic-slice_bitcast_fusion), channel_id=1, source_target_pairs={{0,1},{1,0},{2,3},{3,2},{4,5},{5,4},{6,7},{7,6},{8,9},{9,8},{10,11... | collective-permute-start | bytes 393224 | tf_op jit(solution)/shard_map/ppermute | solution.py:45
  50.2 5.5 %collective-permute-start.1 = (bf16[1024,512]{1,0:T(8,128)(2,1)}, bf16[1024,512]{1,0:T(8,128)(2,1)}, u32[]{:S(2)}, u32[]{:S(2)}) collective-permute-start(bf16[1024,512]{1,0:T(8,128)(2,1)} %param.12), channel_id=1, source_target_pairs={{0,1},{1,0},{2,3},{3,2},{4,5},{5,4},{6,7},{7,6},{8,9},{9,8},{10,11... | collective-permute-start | bytes 3145736 | tf_op jit(solution)/shard_map/ppermute | solution.py:45
  53.1 36.0 %copy-start.35 = (s32[1024]{0:T(1024)}, s32[1024]{0:T(1024)S(1)}, u32[]{:S(2)}) copy-start(s32[1024]{0:T(1024)S(1)} %pad_clamp_fusion) | copy-start | bytes 12292
  53.9 86.3 %collective-permute-start.11 = (bf16[512,1024]{1,0:T(8,128)(2,1)}, bf16[512,1024]{1,0:T(8,128)(2,1)}, u32[]{:S(2)}, u32[]{:S(2)}) collective-permute-start(bf16[512,1024]{1,0:T(8,128)(2,1)} %bitcast.25), channel_id=1, source_target_pairs={{0,1},{1,0},{2,3},{3,2},{4,5},{5,4},{6,7},{7,6},{8,9},{9,8},{10,11... | collective-permute-start | bytes 3145736 | tf_op jit(solution)/shard_map/ppermute | solution.py:45
  83.1 6.0 %copy-start.32 = (pred[1024]{0:T(1024)(128)(4,1)}, pred[1024]{0:T(1024)(128)(4,1)S(1)}, u32[]{:S(2)}) copy-start(pred[1024]{0:T(1024)(128)(4,1)S(1)} %get-tuple-element.56) | copy-start | bytes 3076
  83.1 6.0 %copy-start.33 = (pred[1024]{0:T(1024)(128)(4,1)}, pred[1024]{0:T(1024)(128)(4,1)S(1)}, u32[]{:S(2)}) copy-start(pred[1024]{0:T(1024)(128)(4,1)S(1)} %get-tuple-element.57) | copy-start | bytes 3076
  83.3 5.0 %copy-start.8 = (bf16[8,16,8,1024]{3,2,1,0:T(8,128)(2,1)}, bf16[8,16,8,1024]{3,2,1,0:T(8,128)(2,1)S(1)}, u32[]{:S(2)}) copy-start(bf16[8,16,8,1024]{3,2,1,0:T(8,128)(2,1)S(1)} %copy.129) | copy-start | bytes 6291460
  83.3 9.9 %collective-permute-start.2 = (bf16[128,1024]{1,0:T(8,128)(2,1)}, bf16[128,1024]{1,0:T(8,128)(2,1)S(1)}, u32[]{:S(2)}, u32[]{:S(2)}) collective-permute-start(bf16[128,1024]{1,0:T(8,128)(2,1)} %get-tuple-element.36), channel_id=1, source_target_pairs={{0,32},{32,64},{64,96},{96,128},{128,160},{160,192},{192,224},{224... | collective-permute-start | bytes 786440 | tf_op jit(solution)/shard_map/ppermute | solution.py:91
  85.9 8.0 %collective-permute-start.6 = (bf16[128,1024]{1,0:T(8,128)(2,1)}, bf16[128,1024]{1,0:T(8,128)(2,1)}, u32[]{:S(2)}, u32[]{:S(2)}) collective-permute-start(bf16[128,1024]{1,0:T(8,128)(2,1)} %get-tuple-element.37), channel_id=1, source_target_pairs={{0,224},{32,0},{64,32},{96,64},{128,96},{160,128},{192,160},{224,1... | collective-permute-start | bytes 786440 | tf_op jit(solution)/shard_map/ppermute | solution.py:92
  93.1 5.5 %copy-start.37 = (pred[8]{0:T(512)(128)(4,1)S(1)}, pred[8]{0:T(512)(128)(4,1)}, u32[]{:S(2)}) copy-start(pred[8]{0:T(512)(128)(4,1)} %get-tuple-element.62) | copy-start | bytes 28
  95.1 13.2 %collective-permute-start.3 = (bf16[128,2048]{1,0:T(8,128)(2,1)S(1)}, bf16[128,2048]{1,0:T(8,128)(2,1)}, u32[]{:S(2)}, u32[]{:S(2)}) collective-permute-start(bf16[128,2048]{1,0:T(8,128)(2,1)S(1)} %get-tuple-element.17), channel_id=1, source_target_pairs={{0,32},{32,64},{64,96},{96,128},{128,160},{160,192},{192,224},{224... | collective-permute-start | bytes 1572872 | tf_op jit(solution)/shard_map/ppermute | solution.py:96
  96.5 11.9 %collective-permute-start.7 = (bf16[128,2048]{1,0:T(8,128)(2,1)S(1)}, bf16[128,2048]{1,0:T(8,128)(2,1)}, u32[]{:S(2)}, u32[]{:S(2)}) collective-permute-start(bf16[128,2048]{1,0:T(8,128)(2,1)S(1)} %get-tuple-element.18), channel_id=1, source_target_pairs={{0,224},{32,0},{64,32},{96,64},{128,96},{160,128},{192,160},{224,1... | collective-permute-start | bytes 1572872 | tf_op jit(solution)/shard_map/ppermute | solution.py:97
  99.4 18.2 %all-to-all-start.2 = ((f32[8,32,128]{2,1,0:T(8,128)}), f32[8,32,128]{2,1,0:T(8,128)S(1)}, u32[]{:S(2)}, u32[]{:S(2)}) async-start(f32[8,32,128]{2,1,0:T(8,128)} %broadcast_select_fusion.5), calls=%async_computation.2 | async-start | bytes 262144 | tf_op jit(solution)/shard_map/all_to_all | solution.py:112
  104.7 9.4 %copy-start.20 = (bf16[2,16,8,1024]{3,2,1,0:T(8,128)(2,1)S(1)}, bf16[2,16,8,1024]{3,2,1,0:T(8,128)(2,1)}, u32[]{:S(2)}) copy-start(bf16[2,16,8,1024]{3,2,1,0:T(8,128)(2,1)} %copy.122) | copy-start | bytes 1572868
  108.3 5.7 %copy-start.4 = (bf16[1024,2048]{1,0:T(8,128)(2,1)S(1)}, bf16[1024,2048]{1,0:T(8,128)(2,1)}, u32[]{:S(2)}) copy-start(bf16[1024,2048]{1,0:T(8,128)(2,1)} %pad_maximum_fusion) | copy-start | bytes 12582916
  110.8 22.4 %collective-permute-start.4 = (bf16[128,2048]{1,0:T(8,128)(2,1)}, bf16[128,2048]{1,0:T(8,128)(2,1)S(1)}, u32[]{:S(2)}, u32[]{:S(2)}) collective-permute-start(bf16[128,2048]{1,0:T(8,128)(2,1)} %get-tuple-element.15), channel_id=1, source_target_pairs={{0,32},{32,64},{64,96},{96,128},{128,160},{160,192},{192,224},{224... | collective-permute-start | bytes 1572872 | tf_op jit(solution)/shard_map/ppermute | solution.py:100
  112.8 20.3 %collective-permute-start.8 = (bf16[128,2048]{1,0:T(8,128)(2,1)S(1)}, bf16[128,2048]{1,0:T(8,128)(2,1)}, u32[]{:S(2)}, u32[]{:S(2)}) collective-permute-start(bf16[128,2048]{1,0:T(8,128)(2,1)S(1)} %get-tuple-element.16), channel_id=1, source_target_pairs={{0,224},{32,0},{64,32},{96,64},{128,96},{160,128},{192,160},{224,1... | collective-permute-start | bytes 1572872 | tf_op jit(solution)/shard_map/ppermute | solution.py:101
  114.1 12.6 %copy-start.41 = (s32[16]{0:T(128)S(1)}, s32[16]{0:T(128)}, u32[]{:S(2)}) copy-start(s32[16]{0:T(128)} %get-tuple-element.60) | copy-start | bytes 196
  114.1 12.6 %copy-start.42 = (s32[16]{0:T(128)S(1)}, s32[16]{0:T(128)}, u32[]{:S(2)}) copy-start(s32[16]{0:T(128)} %get-tuple-element.61) | copy-start | bytes 196
  118.3 14.0 %all-to-all-start.3 = ((bf16[16,32,128]{2,1,0:T(8,128)(2,1)}), bf16[16,32,128]{2,1,0:T(8,128)(2,1)S(1)}, u32[]{:S(2)}, u32[]{:S(2)}) async-start(bf16[16,32,128]{2,1,0:T(8,128)(2,1)} %broadcast_in_dim.237), calls=%async_computation.3 | async-start | bytes 262144 | tf_op jit(solution)/shard_map/all_to_all | solution.py:21
  135.2 10.5 %copy-start.5 = (bf16[1024,2048]{1,0:T(8,128)(2,1)S(1)}, bf16[1024,2048]{1,0:T(8,128)(2,1)}, u32[]{:S(2)}) copy-start(bf16[1024,2048]{1,0:T(8,128)(2,1)} %pad_maximum_fusion) | copy-start | bytes 12582916
  135.2 10.5 %collective-permute-start.5 = (bf16[128,2048]{1,0:T(8,128)(2,1)S(1)}, bf16[128,2048]{1,0:T(8,128)(2,1)S(1)}, u32[]{:S(2)}, u32[]{:S(2)}) collective-permute-start(bf16[128,2048]{1,0:T(8,128)(2,1)S(1)} %get-tuple-element.13), channel_id=1, source_target_pairs={{0,32},{32,64},{64,96},{96,128},{128,160},{160,192},{192,224},{224... | collective-permute-start | bytes 1572872 | tf_op jit(solution)/shard_map/ppermute | solution.py:100
  135.3 10.4 %collective-permute-start.9 = (bf16[128,2048]{1,0:T(8,128)(2,1)S(1)}, bf16[128,2048]{1,0:T(8,128)(2,1)S(1)}, u32[]{:S(2)}, u32[]{:S(2)}) collective-permute-start(bf16[128,2048]{1,0:T(8,128)(2,1)S(1)} %get-tuple-element.14), channel_id=1, source_target_pairs={{0,224},{32,0},{64,32},{96,64},{128,96},{160,128},{192,160},{224,1... | collective-permute-start | bytes 1572872 | tf_op jit(solution)/shard_map/ppermute | solution.py:101
  141.9 4.6 %copy-start.21 = (bf16[16,8,512]{2,1,0:T(8,128)(2,1)S(1)}, bf16[16,8,512]{2,1,0:T(8,128)(2,1)}, u32[]{:S(2)}) copy-start(bf16[16,8,512]{2,1,0:T(8,128)(2,1)} %get-tuple-element.38) | copy-start | bytes 393220
  149.5 15.7 %collective-permute-start.18 = (bf16[128,2048]{1,0:T(8,128)(2,1)}, bf16[128,2048]{1,0:T(8,128)(2,1)S(1)}, u32[]{:S(2)}, u32[]{:S(2)}) collective-permute-start(bf16[128,2048]{1,0:T(8,128)(2,1)} %pad_maximum_fusion.1), channel_id=1, source_target_pairs={{0,224},{32,0},{64,32},{96,64},{128,96},{160,128},{192,160},{224,1... | collective-permute-start | bytes 1572872 | tf_op jit(solution)/shard_map/ppermute | solution.py:162
  152.7 25.8 %collective-permute-start.14 = (bf16[128,2048]{1,0:T(8,128)(2,1)}, bf16[128,2048]{1,0:T(8,128)(2,1)S(1)}, u32[]{:S(2)}, u32[]{:S(2)}) collective-permute-start(bf16[128,2048]{1,0:T(8,128)(2,1)} %pad_maximum_fusion.1), channel_id=1, source_target_pairs={{0,32},{32,64},{64,96},{96,128},{128,160},{160,192},{192,224},{224... | collective-permute-start | bytes 1572872 | tf_op jit(solution)/shard_map/ppermute | solution.py:161
  152.7 5.8 %copy-start.30 = (pred[16,128]{1,0:T(8,128)(4,1)S(1)}, pred[16,128]{1,0:T(8,128)(4,1)}, u32[]{:S(2)}) copy-start(pred[16,128]{1,0:T(8,128)(4,1)} %get-tuple-element.58) | copy-start | bytes 6148
  152.7 34.2 %collective-permute-start.12 = (bf16[16,8,512]{2,1,0:T(8,128)(2,1)S(1)}, bf16[16,8,512]{2,1,0:T(8,128)(2,1)}, u32[]{:S(2)}, u32[]{:S(2)}) collective-permute-start(bf16[16,8,512]{2,1,0:T(8,128)(2,1)S(1)} %dynamic-slice_bitcast_fusion.1), channel_id=1, source_target_pairs={{0,1},{1,0},{2,3},{3,2},{4,5},{5,4},{6,7},{7,6},{8,9},{9,8},{10,11... | collective-permute-start | bytes 393224 | tf_op jit(solution)/shard_map/ppermute | solution.py:45
  159.3 20.6 %all-to-all-start.5 = ((bf16[16,32,128]{2,1,0:T(8,128)(2,1)}), bf16[16,32,128]{2,1,0:T(8,128)(2,1)S(1)}, u32[]{:S(2)}, u32[]{:S(2)}) async-start(bf16[16,32,128]{2,1,0:T(8,128)(2,1)} %broadcast_in_dim.246), calls=%async_computation.5 | async-start | bytes 262144 | tf_op jit(solution)/shard_map/all_to_all | solution.py:21
  165.2 35.5 %copy-start.16 = (bf16[128,2048]{1,0:T(8,128)(2,1)}, bf16[128,2048]{1,0:T(8,128)(2,1)S(1)}, u32[]{:S(2)}) copy-start(bf16[128,2048]{1,0:T(8,128)(2,1)S(1)} %collective-permute-done.18) | copy-start | bytes 1572868
  165.2 32.0 %collective-permute-start.19 = (bf16[128,2048]{1,0:T(8,128)(2,1)S(1)}, bf16[128,2048]{1,0:T(8,128)(2,1)S(1)}, u32[]{:S(2)}, u32[]{:S(2)}) collective-permute-start(bf16[128,2048]{1,0:T(8,128)(2,1)S(1)} %collective-permute-done.18), channel_id=1, source_target_pairs={{0,224},{32,0},{64,32},{96,64},{128,96},{160,128},{192,160},{224,1... | collective-permute-start | bytes 1572872 | tf_op jit(solution)/shard_map/ppermute | solution.py:166
  178.5 19.0 %copy-start.14 = (bf16[128,2048]{1,0:T(8,128)(2,1)}, bf16[128,2048]{1,0:T(8,128)(2,1)S(1)}, u32[]{:S(2)}) copy-start(bf16[128,2048]{1,0:T(8,128)(2,1)S(1)} %collective-permute-done.14) | copy-start | bytes 1572868
  178.5 19.0 %collective-permute-start.15 = (bf16[128,2048]{1,0:T(8,128)(2,1)S(1)}, bf16[128,2048]{1,0:T(8,128)(2,1)}, u32[]{:S(2)}, u32[]{:S(2)}) collective-permute-start(bf16[128,2048]{1,0:T(8,128)(2,1)S(1)} %collective-permute-done.14), channel_id=1, source_target_pairs={{0,32},{32,64},{64,96},{96,128},{128,160},{160,192},{192,224},{224... | collective-permute-start | bytes 1572872 | tf_op jit(solution)/shard_map/ppermute | solution.py:165
  180.6 15.9 %all-to-all-start.6 = ((bf16[8,64,128]{2,1,0:T(8,128)(2,1)}), bf16[8,64,128]{2,1,0:T(8,128)(2,1)S(1)}, u32[]{:S(2)}, u32[]{:S(2)}) async-start(bf16[8,64,128]{2,1,0:T(8,128)(2,1)} %broadcast_in_dim.247), calls=%async_computation.6 | async-start | bytes 262144 | tf_op jit(solution)/shard_map/all_to_all | solution.py:21
  197.2 17.7 %copy-start.18 = (bf16[128,2048]{1,0:T(8,128)(2,1)}, bf16[128,2048]{1,0:T(8,128)(2,1)S(1)}, u32[]{:S(2)}) copy-start(bf16[128,2048]{1,0:T(8,128)(2,1)S(1)} %collective-permute-done.19) | copy-start | bytes 1572868
  197.2 13.1 %collective-permute-start.20 = (bf16[128,2048]{1,0:T(8,128)(2,1)S(1)}, bf16[128,2048]{1,0:T(8,128)(2,1)S(1)}, u32[]{:S(2)}, u32[]{:S(2)}) collective-permute-start(bf16[128,2048]{1,0:T(8,128)(2,1)S(1)} %collective-permute-done.19), channel_id=1, source_target_pairs={{0,224},{32,0},{64,32},{96,64},{128,96},{160,128},{192,160},{224,1... | collective-permute-start | bytes 1572872 | tf_op jit(solution)/shard_map/ppermute | solution.py:166
  197.5 14.5 %collective-permute-start.16 = (bf16[128,2048]{1,0:T(8,128)(2,1)}, bf16[128,2048]{1,0:T(8,128)(2,1)S(1)}, u32[]{:S(2)}, u32[]{:S(2)}) collective-permute-start(bf16[128,2048]{1,0:T(8,128)(2,1)} %collective-permute-done.15), channel_id=1, source_target_pairs={{0,32},{32,64},{64,96},{96,128},{128,160},{160,192},{192,224},{224... | collective-permute-start | bytes 1572872 | tf_op jit(solution)/shard_map/ppermute | solution.py:165
  200.1 19.6 %copy-start.6 = (bf16[1024,2048]{1,0:T(8,128)(2,1)S(1)}, bf16[1024,2048]{1,0:T(8,128)(2,1)}, u32[]{:S(2)}) copy-start(bf16[1024,2048]{1,0:T(8,128)(2,1)} %pad_maximum_fusion) | copy-start | bytes 12582916
  210.3 6.6 %collective-permute-start.21 = (bf16[128,1024]{1,0:T(8,128)(2,1)S(1)}, bf16[128,1024]{1,0:T(8,128)(2,1)S(1)}, u32[]{:S(2)}, u32[]{:S(2)}) collective-permute-start(bf16[128,1024]{1,0:T(8,128)(2,1)S(1)} %slice.222), channel_id=1, source_target_pairs={{0,224},{32,0},{64,32},{96,64},{128,96},{160,128},{192,160},{224,1... | collective-permute-start | bytes 786440 | tf_op jit(solution)/shard_map/ppermute | solution.py:169
  212.0 7.7 %collective-permute-start.17 = (bf16[128,1024]{1,0:T(8,128)(2,1)S(1)}, bf16[128,1024]{1,0:T(8,128)(2,1)S(1)}, u32[]{:S(2)}, u32[]{:S(2)}) collective-permute-start(bf16[128,1024]{1,0:T(8,128)(2,1)S(1)} %slice.221), channel_id=1, source_target_pairs={{0,32},{32,64},{64,96},{96,128},{128,160},{160,192},{192,224},{224... | collective-permute-start | bytes 786440 | tf_op jit(solution)/shard_map/ppermute | solution.py:168
  217.0 4.6 %copy-start.24 = (bf16[128,1024]{1,0:T(8,128)(2,1)}, bf16[128,1024]{1,0:T(8,128)(2,1)S(1)}, u32[]{:S(2)}) copy-start(bf16[128,1024]{1,0:T(8,128)(2,1)S(1)} %collective-permute-done.21) | copy-start | bytes 786436
  222.6 9.5 %copy-start.19 = (bf16[128,2048]{1,0:T(8,128)(2,1)S(1)}, bf16[128,2048]{1,0:T(8,128)(2,1)}, u32[]{:S(2)}) copy-start(bf16[128,2048]{1,0:T(8,128)(2,1)} %copy-done.18) | copy-start | bytes 1572868
  222.6 18.3 %all-to-all-start.7 = ((bf16[16,24,1024]{2,1,0:T(8,128)(2,1)}), bf16[16,24,1024]{2,1,0:T(8,128)(2,1)S(1)}, u32[]{:S(2)}, u32[]{:S(2)}) async-start(bf16[16,24,1024]{2,1,0:T(8,128)(2,1)} %bitcast.236), calls=%async_computation.7 | async-start | bytes 1572864 | tf_op jit(solution)/shard_map/all_to_all | solution.py:180
  233.9 6.5 %copy-start.31 = (bf16[1024,2048]{1,0:T(8,128)(2,1)}, bf16[1024,2048]{1,0:T(8,128)(2,1)S(1)}, u32[]{:S(2)}) copy-start(bf16[1024,2048]{1,0:T(8,128)(2,1)S(1)} %get-tuple-element.26) | copy-start | bytes 12582916
  240.4 7.9 %copy-start.28 = (bf16[8,2,8,128]{3,2,0,1:T(8,128)(2,1)S(1)}, bf16[8,2,8,128]{3,2,0,1:T(8,128)(2,1)}, u32[]{:S(2)}) copy-start(bf16[8,2,8,128]{3,2,0,1:T(8,128)(2,1)} %copy.167) | copy-start | bytes 98308
  240.9 9.5 %copy-start.13 = (f32[2,2,1,16,1024]{4,3,1,0,2:T(8,128)}, f32[2,2,1,16,1024]{4,3,1,0,2:T(8,128)S(1)}, u32[]{:S(2)}) copy-start(f32[2,2,1,16,1024]{4,3,1,0,2:T(8,128)S(1)} %fusion.14) | copy-start | bytes 786436
  240.9 9.6 %copy-start.9 = (bf16[8,16,8,1024]{3,2,1,0:T(8,128)(2,1)S(1)}, bf16[8,16,8,1024]{3,2,1,0:T(8,128)(2,1)}, u32[]{:S(2)}) copy-start(bf16[8,16,8,1024]{3,2,1,0:T(8,128)(2,1)} %copy-done.8) | copy-start | bytes 6291460
  240.9 30.4 %all-to-all-start.8 = ((bf16[16,40,1024]{2,1,0:T(8,128)(2,1)}), bf16[16,40,1024]{2,1,0:T(8,128)(2,1)}, u32[]{:S(2)}, u32[]{:S(2)}) async-start(bf16[16,40,1024]{2,1,0:T(8,128)(2,1)} %bitcast.241), calls=%async_computation.8 | async-start | bytes 2621440 | tf_op jit(solution)/shard_map/all_to_all | solution.py:180
  250.4 23.2 %copy-start.38 = (pred[8]{0:T(512)(128)(4,1)S(1)}, pred[8]{0:T(512)(128)(4,1)}, u32[]{:S(2)}) copy-start(pred[8]{0:T(512)(128)(4,1)} %get-tuple-element.62) | copy-start | bytes 28
  250.4 1.4 collective-permute-start.23
  250.5 43.2 %copy-start.1 = (bf16[1,32,8192]{2,1,0:T(8,128)(2,1)S(1)}, bf16[1,32,8192]{2,1,0:T(8,128)(2,1)}, u32[]{:S(2)}) copy-start(bf16[1,32,8192]{2,1,0:T(8,128)(2,1)} %param.13) | copy-start | bytes 1572868
  251.0 13.0 %collective-permute-start.22 = (f32[32,1024]{1,0:T(8,128)S(1)}, f32[32,1024]{1,0:T(8,128)S(1)}, u32[]{:S(2)}, u32[]{:S(2)}) collective-permute-start(f32[32,1024]{1,0:T(8,128)S(1)} %slice.229), channel_id=1, source_target_pairs={{0,1},{1,0},{2,3},{3,2},{4,5},{5,4},{6,7},{7,6},{8,9},{9,8},{10,11... | collective-permute-start | bytes 393224 | tf_op jit(solution)/shard_map/ppermute | solution.py:45
  252.8 12.5 %collective-permute-start.24 = (bf16[2,16,1024]{2,1,0:T(8,128)(2,1)S(1)}, bf16[2,16,1024]{2,1,0:T(8,128)(2,1)S(1)}, u32[]{:S(2)}, u32[]{:S(2)}) collective-permute-start(bf16[2,16,1024]{2,1,0:T(8,128)(2,1)S(1)} %get-tuple-element.44), channel_id=1, source_target_pairs={{0,0},{2,2},{4,32},{6,34},{8,64},{10,66},{12,96},{14,98},{16,128},... | collective-permute-start | bytes 196616 | tf_op jit(solution)/shard_map/ppermute | solution.py:220
  258.6 12.5 %collective-permute-start.25 = (bf16[2,16,1024]{2,1,0:T(8,128)(2,1)S(1)}, bf16[2,16,1024]{2,1,0:T(8,128)(2,1)S(1)}, u32[]{:S(2)}, u32[]{:S(2)}) collective-permute-start(bf16[2,16,1024]{2,1,0:T(8,128)(2,1)S(1)} %get-tuple-element.45), channel_id=1, source_target_pairs={{0,2},{2,0},{4,34},{6,32},{8,66},{10,64},{12,98},{14,96},{16,130},... | collective-permute-start | bytes 196616 | tf_op jit(solution)/shard_map/ppermute | solution.py:221
  274.3 18.7 %all-to-all-start.9 = ((bf16[8,8,1024]{2,1,0:T(8,128)(2,1)}), bf16[8,8,1024]{2,1,0:T(8,128)(2,1)S(1)}, u32[]{:S(2)}, u32[]{:S(2)}) async-start(bf16[8,8,1024]{2,1,0:T(8,128)(2,1)} %broadcast_select_fusion.4), calls=%async_computation.9 | async-start | bytes 262144 | tf_op jit(solution)/shard_map/all_to_all | solution.py:187
  (15 other events, 38.3 us)

commit v2 on v1

v2 whole, which is shorter than its diff:
```python
import functools

import jax
import jax.numpy as jnp
from jax import lax
from jax.experimental import pallas as pl
from jax.experimental.pallas import tpu as pltpu
from jax.sharding import Mesh, PartitionSpec as P


adapter_scale = 2.0
bf16 = jnp.bfloat16
f32 = jnp.float32
CHIPS = ("y", "x")
CORE = "c"
GROUP = "z"
ORDER = (4, 3, 5, 2, 6, 1, 7, 0)
LATE = 3


def spread(block, axes, count):
    copies = jnp.broadcast_to(block[None], (count,) + block.shape)
    return lax.all_to_all(copies, axes, split_axis=0, concat_axis=0, tiled=True)


def pick(array, places):
    return array.at[places].get(mode="promise_in_bounds")


WIDE = 512
LIMIT = 12 * 2**20


def dot(a, b, a_dim=1, b_dim=0):
    return lax.dot_general(a, b, (((a_dim,), (b_dim,)), ((), ())), preferred_element_type=f32)


VMEM = pl.BlockSpec(memory_space=pltpu.VMEM)


def call(kernel, info, inputs, outputs, scratch=()):
    return pl.pallas_call(
        kernel,
        out_shape=[jax.ShapeDtypeStruct(shape, dtype) for shape, dtype in outputs],
        in_specs=[pl.BlockSpec(memory_space=pltpu.SMEM)] + [VMEM] * len(inputs),
        out_specs=[VMEM] * len(outputs),
        scratch_shapes=scratch,
        compiler_params=pltpu.CompilerParams(vmem_limit_bytes=LIMIT),
    )(info, *inputs)


def rows_at(tokens, place, own_rows):
    start = place * own_rows
    if not isinstance(place, int):
        start = pl.multiple_of(start, own_rows)
    block = tokens[:, pl.ds(start, own_rows), :]
    return block.reshape(block.shape[0] * own_rows, block.shape[2])


def over_columns(width, body):
    wide = min(WIDE, width)

    def one(step, carry):
        body(pl.ds(pl.multiple_of(step * wide, wide), wide))
        return carry

    lax.fori_loop(0, width // wide, one, 0)


def join_kernel(info, gate, up, other_gate, other_up, hidden, other_hidden, weight, upstream):
    columns = gate.shape[1]
    own = pl.ds(pl.multiple_of(info[2] * columns, columns), columns)
    other = pl.ds(pl.multiple_of((1 - info[2]) * columns, columns), columns)
    weight[0, :, own] = gate[...]
    weight[1, :, own] = up[...]
    weight[0, :, other] = other_gate[...]
    weight[1, :, other] = other_up[...]
    rows = upstream.shape[0]
    upstream[:, own] = hidden[:, info[2]].reshape(rows, columns)
    upstream[:, other] = other_hidden[...].reshape(rows, columns)


def first_kernel(own_rows, info, tokens, weight, gate_out, up_out):
    def body(cols):
        block = rows_at(tokens, 0, own_rows)
        gate_out[:, cols] = dot(block, weight[0, :, cols]).astype(bf16)
        up_out[:, cols] = dot(block, weight[1, :, cols]).astype(bf16)

    over_columns(gate_out.shape[1], body)


def step_kernel(place, own_rows, info, tokens, weight, from_below, from_above, up_out, down_out):
    rows = up_out.shape[1]
    half = from_below.shape[0] == 1

    def body(cols):
        block = jnp.concatenate(
            [rows_at(tokens, place, own_rows), rows_at(tokens, place + 1, own_rows)], axis=0
        )
        for member in range(2):
            product = dot(block, weight[member, :, cols])
            up, down = product[:rows], product[rows:]
            if not half or member == 0:
                up = up + from_below[0 if half else member, :, cols].astype(f32)
            if not half or member == 1:
                down = down + from_above[0 if half else member, :, cols].astype(f32)
            up_out[member, :, cols] = up.astype(bf16)
            down_out[member, :, cols] = down.astype(bf16)

    over_columns(up_out.shape[2], body)


def mine(values, ids, info):
    return jnp.concatenate(
        [jnp.where(ids == info[0], values[0], 0.0), jnp.where(ids == info[1], values[1], 0.0)], axis=0
    )


def low_kernel(own_rows, info, tokens, inner, ids, out):
    def one(place, carry):
        values = dot(inner[...], rows_at(tokens, place, own_rows), 1, 1)
        half = values.shape[0] // 2
        masked = mine((values[:half], values[half:]), ids[pl.ds(place, 1), :], info)
        out[info[4 + place]] = masked[:half] + masked[half:]
        return carry

    lax.fori_loop(0, out.shape[0], one, 0)


def slots_of(shape, ids, info, rank):
    slot = lax.broadcasted_iota(jnp.int32, shape, 0) // rank
    half = shape[0] // rank // 2
    tenant = jnp.where(slot < half, 2 * slot + info[2], 2 * (slot - half) + 1 - info[2])
    return tenant == ids


def middle_kernel(
    rank, own_rows, info, tokens, weight, from_below, from_above, outer, other_outer, low, ids, upstream,
    hidden_out, grads_out, low_out, chosen, mapped,
):
    slots = chosen.shape[2]

    def table(member, cols):
        parts = [ref[:, member, :, cols] for ref in (outer, other_outer)]
        return jnp.concatenate([part.reshape(slots // 2, part.shape[2]) for part in parts], axis=0)

    last = ids.shape[0] - 1
    own = ids[last:, :]
    shape = (slots, own.shape[1])
    here = slots_of(shape, own, info, rank)
    for member in range(2):
        values = low[member * rank : (member + 1) * rank, :].astype(f32)
        values = jnp.concatenate([values] * (slots // rank), axis=0)
        chosen[member] = jnp.where(here, values, 0.0).T.astype(bf16)
    mapped[...] = jnp.zeros_like(mapped)

    def body(cols):
        block = rows_at(tokens, last, own_rows)
        tables = (table(0, cols), table(1, cols))
        gate, up = [
            dot(block, weight[member, :, cols])
            + from_below[member, :, cols].astype(f32)
            + from_above[member, :, cols].astype(f32)
            + adapter_scale * dot(chosen[member], tables[member])
            for member in range(2)
        ]
        cotangent = upstream[:, cols].astype(f32)
        sigmoid = 1.0 / (1.0 + jnp.exp(-gate))
        silu = gate * sigmoid
        hidden_out[:, cols] = (silu * up).astype(bf16)
        grad_gate = (cotangent * up * sigmoid * (1.0 + gate * (1.0 - sigmoid))).astype(bf16)
        grad_up = (cotangent * silu).astype(bf16)
        for member, grad in enumerate((grad_gate, grad_up)):
            grads_out[member, :, cols] = grad
            mapped[member] += dot(tables[member], grad, 1, 1)

    over_columns(hidden_out.shape[1], body)
    here = slots_of(shape, own, info, rank)
    for member in range(2):
        total = jnp.where(here, mapped[member], 0.0).reshape(slots // rank, rank, shape[1])
        low_out[member * rank : (member + 1) * rank, :] = (adapter_scale * jnp.sum(total, axis=0)).astype(bf16)


def grad_low_at(info, lows, ids, place):
    values = lows[info[4 + place], lows.shape[1] // 2 :, :].astype(f32)
    return mine((values, values), ids[place : place + 1, :], info)


def back_kernel(first, count, split, info, weight, inner, lows, ids, *refs):
    *chunks, out, adapters = refs
    pairs = [(ref.at[0], ref.at[1]) for ref in chunks[2 if split else 0 :]]
    chunks = ([(chunks[0], chunks[1])] if split else []) + pairs
    adapter = [grad_low_at(info, lows, ids, first + i).T.astype(bf16) for i in range(count)]
    adapters[...] = jnp.concatenate(adapter, axis=0)
    chips, height, width = out.shape
    deep = min(256, width)
    own_rows, rows = height // count, adapters.shape[0] // count

    def one(step, carry):
        cols = pl.ds(pl.multiple_of(step * deep, deep), deep)
        total = dot(adapters[...], inner[:, cols])
        for member in range(2):
            block = jnp.concatenate([chunk[member][...] for chunk in chunks], axis=0)
            total = total + dot(block, weight[member, cols, :], 1, 1)
        for i in range(count):
            part = total[i * rows : (i + 1) * rows].reshape(chips, own_rows, deep)
            out[:, i * own_rows : (i + 1) * own_rows, cols] = part.astype(bf16)
        return carry

    lax.fori_loop(0, width // deep, one, 0)


def inner_kernel(own_rows, info, tokens, lows, ids, out):
    out[...] = jnp.zeros_like(out)

    def one(place, carry):
        values = lows[info[4 + place], lows.shape[1] // 2 :, :].astype(f32)
        masked = mine((values, values), ids[pl.ds(place, 1), :], info)
        out[...] += dot(masked.astype(bf16), rows_at(tokens, place, own_rows))
        return carry

    lax.fori_loop(0, ids.shape[0], one, 0)


def place_kernel(info, near, far, out):
    own_rows = out.shape[1]
    late = far.shape[1] // own_rows
    for place in range(out.shape[0]):
        if place < late:
            block = far[:, place * own_rows : (place + 1) * own_rows, :].astype(f32)
        else:
            block = near[:, (place - late) * own_rows : (place - late + 1) * own_rows, :].astype(f32)
        out[info[4 + place]] = jnp.sum(block, axis=0).astype(bf16)


def outer_kernel(places, rank, share, split, last, info, lows, ids, *refs):
    refs = list(refs)
    outs = [refs.pop() for _ in range(2 if last else 1)][::-1]
    before = refs.pop() if last else None
    chunks = refs
    if split:
        chunks = [(chunks[0][...], chunks[1][...])] + [(ref[0], ref[1]) for ref in chunks[2:]]
    else:
        chunks = [(ref[0], ref[1]) for ref in chunks]
    rows = chunks[0][0].shape[0]
    slot = lax.broadcasted_iota(jnp.int32, (share * rank, rows), 0) // rank
    half = share // 2
    tenant = share * info[3] + jnp.where(slot < half, 2 * slot + info[2], 2 * (slot - half) + 1 - info[2])
    for member in range(2):
        total = before[member] if last else 0.0
        for place, chunk in zip(places, chunks):
            values = lows[info[4 + place], member * rank : (member + 1) * rank, :].astype(f32)
            values = jnp.concatenate([values] * share, axis=0)
            chosen = jnp.where(tenant == ids[place : place + 1, :], values, 0.0).astype(bf16)
            total = total + dot(chosen, chunk[member])
        if last:
            outs[0][member] = total[: half * rank]
            outs[1][member] = total[half * rank :].astype(bf16)
        else:
            outs[0][member] = total


def on_device(tokens, tenant_ids, gate_weight, up_weight, adapter_in, adapter_out, grad_hidden):
    groups = lax.axis_size(GROUP)
    chips = lax.axis_size("y") * lax.axis_size("x")
    own_rows, _ = tokens.shape
    depth, columns = gate_weight.shape
    rank = adapter_out.shape[2]
    rows = chips * own_rows
    chip_columns = 2 * columns
    z = lax.axis_index(GROUP)
    c = lax.axis_index(CORE)
    u = lax.axis_index("y") * lax.axis_size("x") + lax.axis_index("x")
    first_core = c == 0
    order = jnp.array(ORDER, jnp.int32)
    group_at = (z + order) % groups
    swap = [(0, 1), (1, 0)]
    up_ring = [(i, (i + 1) % groups) for i in range(groups)]
    down_ring = [(i, (i - 1) % groups) for i in range(groups)]

    def other_core(value):
        return lax.ppermute(value, CORE, swap)

    def ring(value, pairs):
        return lax.ppermute(value, GROUP, pairs)

    def both(own, other):
        return jnp.where(first_core, own, other), jnp.where(first_core, other, own)

    ids = jnp.broadcast_to(tenant_ids.reshape(own_rows, 1, 1).astype(bf16), (own_rows, groups, 128))
    wide = jnp.concatenate([tokens.reshape(own_rows, groups, depth), ids], axis=2)
    sliced = lax.all_to_all(
        wide.reshape(own_rows, groups * (depth + 128)), GROUP, split_axis=1, concat_axis=0, tiled=True
    )
    sliced = pick(sliced.reshape(groups, own_rows, depth + 128), group_at)
    sliced = sliced.reshape(groups * own_rows, depth + 128)
    count = groups * own_rows
    id_columns = sliced[:, depth:]
    lane = lax.broadcasted_iota(jnp.int32, (count, 128), 1)
    row = lax.broadcasted_iota(jnp.int32, (count, 128), 0)
    id_lanes = jnp.sum(jnp.where(lane == row, id_columns.astype(f32), 0.0), axis=0, keepdims=True)
    id_block = jnp.broadcast_to(jnp.pad(id_lanes.astype(bf16), ((0, 0), (0, depth - 128))), (8, depth))
    gathered = spread(jnp.concatenate([sliced[:, :depth], id_block], axis=0), CHIPS, chips)
    row_ids = gathered[:, count, :count].astype(f32).astype(jnp.int32)
    row_ids = row_ids.reshape(chips, groups, own_rows).transpose(1, 0, 2).reshape(groups, rows)

    info = jnp.concatenate([jnp.stack([2 * u + c, 2 * u + 1 - c, c, z]), group_at]).astype(jnp.int32)
    by_core = grad_hidden.reshape(chips, 2, own_rows, columns)
    give = lax.dynamic_index_in_dim(by_core, 1 - c, 1, keepdims=False)
    weight, upstream = call(
        join_kernel,
        info,
        [gate_weight, up_weight, other_core(gate_weight), other_core(up_weight), by_core, other_core(give)],
        [((2, depth, chip_columns), bf16), ((rows, chip_columns), bf16)],
    )

    inner = lax.dynamic_slice_in_dim(adapter_in[0], z * depth, depth, axis=1)
    inner = jnp.concatenate([inner, other_core(inner)], axis=0)
    outer = adapter_out.reshape(2 * rank, chips, chip_columns).transpose(1, 0, 2)
    outer = lax.all_to_all(outer, CHIPS, split_axis=0, concat_axis=0, tiled=True)
    outer = outer.reshape(chips, 2, rank, chip_columns)
    other_outer = other_core(outer)

    shape = (rows, chip_columns)
    going_up, going_down = call(
        functools.partial(first_kernel, own_rows), info, [gathered, weight], [(shape, bf16)] * 2
    )
    going_up = ring(going_up, up_ring)[None]
    going_down = ring(going_down, down_ring)[None]
    for step, place in enumerate((1, 3, 5), 2):
        going_up, going_down = call(
            functools.partial(step_kernel, place, own_rows),
            info,
            [gathered, weight, going_up, going_down],
            [((2,) + shape, bf16)] * 2,
        )
        going_up = ring(going_up, up_ring)
        going_down = ring(going_down, down_ring)

    (low_parts,) = call(
        functools.partial(low_kernel, own_rows), info, [gathered, inner, row_ids], [((groups, 2 * rank, rows), f32)]
    )
    low_here = lax.all_to_all(low_parts, GROUP, split_axis=0, concat_axis=0, tiled=True)
    low_here = jnp.sum(low_here, axis=0).astype(bf16)
    low = spread(low_here, CHIPS, chips)
    low = jnp.sum(low.astype(f32), axis=0).astype(bf16)

    slots = 2 * chips * rank
    hidden_rows, grads, grad_low = call(
        functools.partial(middle_kernel, rank, own_rows),
        info,
        [gathered, weight, going_up, going_down, outer, other_outer, low, row_ids, upstream],
        [(shape, bf16), ((2,) + shape, bf16), ((2 * rank, rows), bf16)],
        (pltpu.VMEM((2, rows, slots), bf16), pltpu.VMEM((2, slots, rows), f32)),
    )

    grads_at = {0: [grads]}
    below = ring(grads, up_ring)
    above = ring(grads, down_ring)
    grads_at[7], grads_at[1] = [below], [above]
    for step in (2, 3):
        below = ring(below, up_ring)
        above = ring(above, down_ring)
        grads_at[groups - step], grads_at[step] = [below], [above]
    grads_at[4] = [ring(below[0], up_ring), ring(above[1], down_ring)]

    halves = hidden_rows.reshape(chips, own_rows, 2, columns)
    keep = lax.dynamic_index_in_dim(halves, c, 2, keepdims=False)
    give = lax.dynamic_index_in_dim(halves, 1 - c, 2, keepdims=False)
    hidden = jnp.stack(both(keep, other_core(give)), axis=1).reshape(chips * 2 * own_rows, columns)

    grad_low = spread(grad_low, CHIPS, chips)
    grad_low = jnp.sum(grad_low.astype(f32), axis=0).astype(bf16)
    lows = jnp.concatenate([low, grad_low], axis=0)
    lows = spread(lows, GROUP, groups)

    def to_owners(first, last):
        count = last - first
        chunks = [array for d in ORDER[first:last] for array in grads_at[d]]
        (part,) = call(
            functools.partial(back_kernel, first, count, first == 0),
            info,
            [weight, inner, lows, row_ids] + chunks,
            [((chips, count * own_rows, depth), bf16)],
            (pltpu.VMEM((count * rows, inner.shape[0]), bf16),),
        )
        return lax.all_to_all(part, CHIPS, split_axis=0, concat_axis=0, tiled=True)

    near = to_owners(LATE, groups)
    far = to_owners(0, LATE)
    (summed,) = call(place_kernel, info, [near, far], [((groups, own_rows, depth), bf16)])
    grad_tokens = lax.all_to_all(
        summed.reshape(groups * own_rows, depth), GROUP, split_axis=0, concat_axis=1, tiled=True
    )

    (inner_grads,) = call(
        functools.partial(inner_kernel, own_rows), info, [gathered, lows, row_ids], [((4 * rank, depth), f32)]
    )
    grad_in = inner_grads[: 2 * rank] + other_core(inner_grads[2 * rank :])

    share = 2 * chips // groups

    def outer_grads(places, before):
        chunks = [array for place in places for array in grads_at[ORDER[place]]]
        arrays = [lows, row_ids] + chunks + ([] if before is None else [before])
        full = (2, share * rank, chip_columns)
        part = (2, share // 2 * rank, chip_columns)
        outs = [(full, f32)] if before is None else [(part, f32), (part, bf16)]
        return call(
            functools.partial(outer_kernel, places, rank, share, 0 in places, before is not None), info, arrays, outs
        )

    (outs,) = outer_grads(tuple(range(LATE, groups)), None)
    keep, give = outer_grads(tuple(range(LATE)), outs)
    outs = (keep + other_core(give).astype(f32)).astype(bf16)
    outs = outs.reshape(2, share // 2, rank, chip_columns)
    lower = u % 2
    same = lax.dynamic_index_in_dim(outs, lower, 1, keepdims=False)
    cross = lax.dynamic_index_in_dim(outs, 1 - lower, 1, keepdims=False)
    straight, crossed = [], []
    for from_z in range(groups):
        for from_u in range(chips):
            source, low_bit = from_z * chips + from_u, from_u % 2
            target = (from_u // 2) * chips + 2 * from_z
            straight.append((source, target + low_bit))
            crossed.append((source, target + 1 - low_bit))
    same = lax.ppermute(same, (GROUP,) + CHIPS, straight)
    cross = lax.ppermute(cross, (GROUP,) + CHIPS, crossed)
    left = jnp.where(lower == 0, same, cross)
    right = jnp.where(lower == 0, cross, same)
    grad_out = adapter_scale * jnp.concatenate([left, right], axis=2).astype(f32)
    return hidden, grad_tokens, grad_in[None], grad_out[None]


def solution(mesh):
    groups, tenants = mesh.shape["dp"], mesh.shape["tenant"]
    split = Mesh(mesh.devices.reshape(groups, tenants // 8, 4, 2), ("z", "y", "x", "c"))
    tenant = ("y", "x", "c")
    in_specs = (
        P(("z",) + tenant, None),
        P("z", tenant),
        P("z", tenant),
        P("z", tenant),
        P(tenant, None, None),
        P(tenant, None, None, None),
        P("z", tenant),
    )
    out_specs = (
        P("z", tenant),
        P(("z",) + tenant, None),
        P(tenant, None, "z"),
        P(tenant, None, None, "z"),
    )
    return jax.shard_map(on_device, mesh=split, in_specs=in_specs, out_specs=out_specs, check_vma=False)
```

time: 299 us -> 301 us (level)
  Pallas kernels: 0 us -> 36.9 us
  matrix products: 32.4 us -> 0 us
  blocking collectives: 0 us -> 25 us
  starting transfers between devices: 120 us -> 95 us
  other arithmetic: 28.3 us -> 9.8 us
  waiting for transfers between devices: 79.1 us -> 94.7 us
    pallas_call x0 -> x13, Pallas kernels: none -> 36.9 us  [call(): pl.pallas_call(kernel, out_shape=[jax.ShapeDtypeStruct(shape, dtype) for...]
    dot_general x19 -> x0, matrix products: 32.4 us -> none  [contract(): lax.dot_general(a, b, (((a_dim,), (b_dim,)), ((), ())), preferred_element...]
    all_to_all x0 -> x2, blocking collectives: none -> 25 us  [the longest x1 12.7 us: spread(): return lax.all_to_all(copies, axes, split_axis=0, concat_axis=0, tiled=True)]
    ppermute x16, waiting for transfers between devices: 16.9 us -> 38.1 us  [ring(): return lax.ppermute(value, GROUP, pairs)]
    all_to_all x5 -> x4, waiting for transfers between devices: 19.6 us -> 8.37 us  [the longest x1 8.36 us: on_device(): lax.all_to_all(summed.reshape(groups * own_rows, depth), GROUP, split_axi...]
    all_to_all x4 -> x3, starting transfers between devices: 26.9 us -> 17.1 us  [spread(): return lax.all_to_all(copies, axes, split_axis=0, concat_axis=0, tiled=True)]
    unnamed x97 -> x56, local copies, waits for them, and re-layouts: 11.9 us -> 21.6 us
    ppermute x16, starting transfers between devices: 34.2 us -> 26 us  [ring(): return lax.ppermute(value, GROUP, pairs)]
  transfers between devices with their start and end apart: 36 -> 34, of which waited for: 13 -> 14; matrix products, arithmetic and copies ran while one was open for 25% -> 7% of each run, Pallas kernels for 0% -> 10%
where the time goes in v2:
time: 301 us; the launch traced here: 297 us
  starting transfers between devices  95 us (32%)
  waiting for transfers between devices  94.7 us (31%)
  Pallas kernels  36.9 us (12%)
  local copies, waits for them, and re-layouts  34.8 us (12%)
  blocking collectives  25 us (8%)
  other arithmetic  9.8 us (3%)
    ppermute x16, waiting for transfers between devices, ring(): return lax.ppermute(value, GROUP, pairs)  38.1 us
    pallas_call x13, Pallas kernels, call(): pl.pallas_call(kernel, out_shape=[jax.ShapeDtypeStruct(shape, dtype) for...  36.9 us
    all_to_all x3, waiting for transfers between devices, spread(): return lax.all_to_all(copies, axes, split_axis=0, concat_axis=0, tiled=True)  33.4 us
    ppermute x16, starting transfers between devices, ring(): return lax.ppermute(value, GROUP, pairs)  26 us
    unnamed x56, local copies, waits for them, and re-layouts  21.6 us
    all_to_all x3, starting transfers between devices, spread(): return lax.all_to_all(copies, axes, split_axis=0, concat_axis=0, tiled=True)  17.1 us
    all_to_all x2, starting transfers between devices, to_owners(): return lax.all_to_all(part, CHIPS, split_axis=0, concat_axis=0, tiled=True)  14.1 us
    all_to_all x1, blocking collectives, spread(): return lax.all_to_all(copies, axes, split_axis=0, concat_axis=0, tiled=True)  12.7 us
  transfers between devices with their start and end apart: 34, of which 14 were waited for; matrix products, arithmetic and copies ran while one was open for 7% of the time, Pallas kernels for 10%

profile of v2, /device:TPU:16, one launch (start us, length us, event | category | flops | bytes accessed | tf_op | source)
XLA Modules:
  0.0 297.2 jit_solution(10066349360659163367)
XLA Ops:
  1.4 1.6 pad_maximum_fusion.1
  3.0 8.5 %all-to-all-start = ((bf16[8,8,1152]{2,0,1:T(8,128)(2,1)}), bf16[8,8,1152]{2,0,1:T(8,128)(2,1)S(1)}, u32[]{:S(2)}, u32[]{:S(2)}) async-start(bf16[8,8,1152]{2,0,1:T(8,128)(2,1)} %pad_maximum_fusion.1), calls=%async_computation | async-start | bytes 294912 | tf_op jit(solution)/shard_map/all_to_all | solution.py:292
  12.2 8.7 %all-to-all-done = bf16[8,8,1152]{2,0,1:T(8,128)(2,1)S(1)} async-done(((bf16[8,8,1152]{2,0,1:T(8,128)(2,1)}), bf16[8,8,1152]{2,0,1:T(8,128)(2,1)S(1)}, u32[]{:S(2)}, u32[]{:S(2)}) %all-to-all-start) | async-done | bytes 147488 | tf_op jit(solution)/shard_map/all_to_all | solution.py:292
  21.6 1.7 broadcast_in_dim.59
  23.3 7.3 %all-to-all-start.1 = ((bf16[16,72,1024]{2,1,0:T(8,128)(2,1)}), bf16[16,72,1024]{2,1,0:T(8,128)(2,1)S(1)}, u32[]{:S(2)}, u32[]{:S(2)}) async-start(bf16[16,72,1024]{2,1,0:T(8,128)(2,1)} %broadcast_in_dim.59), calls=%async_computation.1 | async-start | bytes 4718592 | tf_op jit(solution)/shard_map/all_to_all | solution.py:23
  31.1 1.8 copy.27
  32.9 1.6 copy.29
  34.5 25.4 %all-to-all-done.1.tokens = bf16[16,72,1024]{2,1,0:T(8,128)(2,1)S(1)} async-done(((bf16[16,72,1024]{2,1,0:T(8,128)(2,1)}), bf16[16,72,1024]{2,1,0:T(8,128)(2,1)S(1)}, u32[]{:S(2)}, u32[]{:S(2)}) %all-to-all-start.1) | async-done | bytes 2359328 | tf_op jit(solution)/shard_map/all_to_all | solution.py:23
  59.8 6.8 %all-to-all-start.2 = ((bf16[16,32,1024]{2,1,0:T(8,128)(2,1)}), bf16[16,32,1024]{2,1,0:T(8,128)(2,1)}, u32[]{:S(2)}, u32[]{:S(2)}) async-start(bf16[16,32,1024]{2,1,0:T(8,128)(2,1)} %bitcast.71), calls=%async_computation.2 | async-start | bytes 2097152 | tf_op jit(solution)/shard_map/all_to_all | solution.py:320
  66.9 1.2 collective-permute-done.2.other_hidden
  68.1 1.2 copy-done.16
  69.3 1.2 copy-done.17
  70.6 1.9 shard_map.111
  72.5 1.5 shard_map.112
  74.0 1.3 collective-permute-start.3
  75.3 2.0 collective-permute-start.4
  77.3 6.3 %collective-permute-done.3 = bf16[128,1024]{1,0:T(8,128)(2,1)S(1)} collective-permute-done((bf16[128,1024]{1,0:T(8,128)(2,1)S(1)}, bf16[128,1024]{1,0:T(8,128)(2,1)S(1)}, u32[]{:S(2)}, u32[]{:S(2)}) %collective-permute-start.3) | collective-permute-done | bytes 262176 | tf_op jit(solution)/shard_map/ppermute | solution.py:285
  83.6 2.0 shard_map.113
  85.8 3.1 %collective-permute-start.6 = (bf16[2,128,1024]{2,1,0:T(8,128)(2,1)S(1)}, bf16[2,128,1024]{2,1,0:T(8,128)(2,1)S(1)}, u32[]{:S(2)}, u32[]{:S(2)}) collective-permute-start(bf16[2,128,1024]{2,1,0:T(8,128)(2,1)S(1)} %get-tuple-element.23), channel_id=1, source_target_pairs={{0,224},{32,0},{64,32},{96,64},{128,96},{160,128},{192,160},{224,1... | collective-permute-start | bytes 1572872 | tf_op jit(solution)/shard_map/ppermute | solution.py:285
  88.9 11.1 %collective-permute-done.5.from_below = bf16[2,128,1024]{2,1,0:T(8,128)(2,1)S(1)} collective-permute-done((bf16[2,128,1024]{2,1,0:T(8,128)(2,1)S(1)}, bf16[2,128,1024]{2,1,0:T(8,128)(2,1)S(1)}, u32[]{:S(2)}, u32[]{:S(2)}) %collective-permute-start.5) | collective-permute-done | bytes 524320 | tf_op jit(solution)/shard_map/ppermute | solution.py:285
  100.0 3.0 %shard_map.114 = (bf16[2,128,1024]{2,1,0:T(8,128)(2,1)}, bf16[2,128,1024]{2,1,0:T(8,128)(2,1)}) custom-call(s32[12]{0:T(128)S(1)} %concatenate.29.info, bf16[16,72,1024]{2,1,0:T(8,128)(2,1)S(1)} %all-to-all-done.1.tokens, bf16[2,1024,1024]{2,1,0:T(8,128)(2,1)S(1)} %get-tuple-element.19.weight, bf16[2,128,1024]{2,1,0:T(8,128)(2,1)S(1)} %collective-permute-done.5.from_below, ...), custom_call_target="tpu_custom_call" | custom-call | tf_op jit(solution)/shard_map/pallas_call | solution.py:42
  103.1 3.2 %collective-permute-start.8 = (bf16[2,128,1024]{2,1,0:T(8,128)(2,1)}, bf16[2,128,1024]{2,1,0:T(8,128)(2,1)}, u32[]{:S(2)}, u32[]{:S(2)}) collective-permute-start(bf16[2,128,1024]{2,1,0:T(8,128)(2,1)} %get-tuple-element.25), channel_id=1, source_target_pairs={{0,224},{32,0},{64,32},{96,64},{128,96},{160,128},{192,160},{224,1... | collective-permute-start | bytes 1572872 | tf_op jit(solution)/shard_map/ppermute | solution.py:285
  106.9 2.4 collective-permute-done.12
  109.3 7.4 %collective-permute-done.7.from_below = bf16[2,128,1024]{2,1,0:T(8,128)(2,1)S(1)} collective-permute-done((bf16[2,128,1024]{2,1,0:T(8,128)(2,1)}, bf16[2,128,1024]{2,1,0:T(8,128)(2,1)S(1)}, u32[]{:S(2)}, u32[]{:S(2)}) %collective-permute-start.7) | collective-permute-done | bytes 524320 | tf_op jit(solution)/shard_map/ppermute | solution.py:285
  116.8 2.2 copy-done.2
  119.0 3.5 %shard_map.115 = (bf16[2,128,1024]{2,1,0:T(8,128)(2,1)}, bf16[2,128,1024]{2,1,0:T(8,128)(2,1)}) custom-call(s32[12]{0:T(128)S(1)} %concatenate.29.info, bf16[16,72,1024]{2,1,0:T(8,128)(2,1)S(1)} %all-to-all-done.1.tokens, bf16[2,1024,1024]{2,1,0:T(8,128)(2,1)S(1)} %copy-done.2, bf16[2,128,1024]{2,1,0:T(8,128)(2,1)S(1)} %collective-permute-done.7.from_below, ...), custom_call_target="tpu_custom_call" | custom-call | tf_op jit(solution)/shard_map/pallas_call | solution.py:42
  122.7 3.1 %collective-permute-start.10 = (bf16[2,128,1024]{2,1,0:T(8,128)(2,1)}, bf16[2,128,1024]{2,1,0:T(8,128)(2,1)}, u32[]{:S(2)}, u32[]{:S(2)}) collective-permute-start(bf16[2,128,1024]{2,1,0:T(8,128)(2,1)} %get-tuple-element.27), channel_id=1, source_target_pairs={{0,224},{32,0},{64,32},{96,64},{128,96},{160,128},{192,160},{224,1... | collective-permute-start | bytes 1572872 | tf_op jit(solution)/shard_map/ppermute | solution.py:285
  126.4 1.5 copy.25
  128.9 2.2 shard_map.116
  131.1 12.3 %all_to_all.69 = f32[8,32,128]{2,1,0:T(8,128)S(1)} all-to-all(f32[8,32,128]{2,1,0:T(8,128)S(1)} %shard_map.116), channel_id=1, replica_groups=mesh['z'=8,'y'=4,'x'=4,'c'=2] {'z'}, dimensions={0} | all-to-all | bytes 262144 | tf_op jit(solution)/shard_map/all_to_all | solution.py:343
  143.5 12.7 %all_to_all.70 = bf16[16,32,128]{2,1,0:T(8,128)(2,1)} all-to-all(bf16[16,32,128]{2,1,0:T(8,128)(2,1)S(1)} %broadcast_in_dim.62), channel_id=1, replica_groups=mesh['z'=8,'y'=4,'x'=4,'c'=2] {'y','x'}, dimensions={0} | all-to-all | bytes 262144 | tf_op jit(solution)/shard_map/all_to_all | solution.py:23
  157.2 2.2 copy-done.3
  160.3 4.2 %shard_map.117 = (bf16[128,1024]{1,0:T(8,128)(2,1)S(1)}, bf16[2,128,1024]{2,1,0:T(8,128)(2,1)S(1)}, bf16[32,128]{1,0:T(8,128)(2,1)S(1)}) custom-call(s32[12]{0:T(128)S(1)} %concatenate.29.info, bf16[16,72,1024]{2,1,0:T(8,128)(2,1)S(1)} %all-to-all-done.1.tokens, bf16[2,1024,1024]{2,1,0:T(8,128)(2,1)S(1)} %copy-done.3, ...), custom_call_target="tpu_custom_call" | custom-call | tf_op jit(solution)/shard_map/pallas_call | solution.py:42
  165.8 2.7 collective-permute-start.14
  169.3 9.7 %collective-permute-done.16.refs_3_ = bf16[2,128,1024]{2,1,0:T(8,128)(2,1)S(1)} collective-permute-done((bf16[2,128,1024]{2,1,0:T(8,128)(2,1)S(1)}, bf16[2,128,1024]{2,1,0:T(8,128)(2,1)S(1)}, u32[]{:S(2)}, u32[]{:S(2)}) %collective-permute-start.16) | collective-permute-done | bytes 524320 | tf_op jit(solution)/shard_map/ppermute | solution.py:285
  179.8 3.2 %collective-permute-start.15 = (bf16[2,128,1024]{2,1,0:T(8,128)(2,1)}, bf16[2,128,1024]{2,1,0:T(8,128)(2,1)}, u32[]{:S(2)}, u32[]{:S(2)}) collective-permute-start(bf16[2,128,1024]{2,1,0:T(8,128)(2,1)} %collective-permute-done.14.refs_2_), channel_id=1, source_target_pairs={{0,224},{32,0},{64,32},{96,64},{128,96},{160,128},{192,160},{224,1... | collective-permute-start | bytes 1572872 | tf_op jit(solution)/shard_map/ppermute | solution.py:285
  183.7 6.5 %all-to-all-start.5 = ((bf16[16,32,128]{2,1,0:T(8,128)(2,1)}), bf16[16,32,128]{2,1,0:T(8,128)(2,1)}, u32[]{:S(2)}, u32[]{:S(2)}) async-start(bf16[16,32,128]{2,1,0:T(8,128)(2,1)} %broadcast_in_dim.63), calls=%async_computation.5 | async-start | bytes 262144 | tf_op jit(solution)/shard_map/all_to_all | solution.py:23
  190.2 3.5 %collective-permute-done.17.refs_1_ = bf16[2,128,1024]{2,1,0:T(8,128)(2,1)} collective-permute-done((bf16[2,128,1024]{2,1,0:T(8,128)(2,1)S(1)}, bf16[2,128,1024]{2,1,0:T(8,128)(2,1)}, u32[]{:S(2)}, u32[]{:S(2)}) %collective-permute-start.17) | collective-permute-done | bytes 524320 | tf_op jit(solution)/shard_map/ppermute | solution.py:285
  193.7 2.2 all-to-all-done.5
  197.5 3.4 %all-to-all-start.6 = ((bf16[8,64,128]{2,1,0:T(8,128)(2,1)}), bf16[8,64,128]{2,1,0:T(8,128)(2,1)S(1)}, u32[]{:S(2)}, u32[]{:S(2)}) async-start(bf16[8,64,128]{2,1,0:T(8,128)(2,1)} %broadcast_in_dim.64), calls=%async_computation.6 | async-start | bytes 262144 | tf_op jit(solution)/shard_map/all_to_all | solution.py:23
  200.9 3.2 %collective-permute-start.20 = (bf16[2,128,1024]{2,1,0:T(8,128)(2,1)}, bf16[2,128,1024]{2,1,0:T(8,128)(2,1)}, u32[]{:S(2)}, u32[]{:S(2)}) collective-permute-start(bf16[2,128,1024]{2,1,0:T(8,128)(2,1)} %collective-permute-done.15.refs_0_), channel_id=1, source_target_pairs={{0,224},{32,0},{64,32},{96,64},{128,96},{160,128},{192,160},{224,1... | collective-permute-start | bytes 1572872 | tf_op jit(solution)/shard_map/ppermute | solution.py:285
  204.1 5.8 %all-to-all-done.6.lows = bf16[8,64,128]{2,1,0:T(8,128)(2,1)S(1)} async-done(((bf16[8,64,128]{2,1,0:T(8,128)(2,1)}), bf16[8,64,128]{2,1,0:T(8,128)(2,1)S(1)}, u32[]{:S(2)}, u32[]{:S(2)}) %all-to-all-start.6) | async-done | bytes 131104 | tf_op jit(solution)/shard_map/all_to_all | solution.py:23
  209.9 2.2 copy-done.4
  214.0 1.0 copy-done.14
  215.1 5.2 %shard_map.118 = bf16[16,40,1024]{2,1,0:T(8,128)(2,1)S(1)} custom-call(s32[12]{0:T(128)S(1)} %concatenate.29.info, bf16[2,1024,1024]{2,1,0:T(8,128)(2,1)S(1)} %copy-done.4, bf16[64,1024]{1,0:T(8,128)(2,1)S(1)} %copy-done.8, bf16[8,64,128]{2,1,0:T(8,128)(2,1)S(1)} %all-to-all-done.6.lows, s32[8,128]{1,0:T(8,128)S(1)} %reshape.113.ids, ...), custom_call_target="tpu_custom_call" | custom-call | tf_op jit(solution)/shard_map/pallas_call | solution.py:42
  220.3 1.1 copy-done.6
  221.3 6.7 %all-to-all-start.7 = ((bf16[16,40,1024]{2,1,0:T(8,128)(2,1)}), bf16[16,40,1024]{2,1,0:T(8,128)(2,1)}, u32[]{:S(2)}, u32[]{:S(2)}) async-start(bf16[16,40,1024]{2,1,0:T(8,128)(2,1)} %copy-done.6), calls=%async_computation.7 | async-start | bytes 2621440 | tf_op jit(solution)/shard_map/all_to_all | solution.py:387
  229.3 1.7 slice_bitcast_fusion
  231.0 2.7 collective-permute-start.21
  233.7 1.6 dynamic-slice_bitcast_fusion
  235.2 1.0 copy-done.12
  237.3 1.9 shard_map.122.refs_4_
  239.2 2.4 shard_map.123
  243.8 2.0 shard_map.121
  247.3 4.8 %shard_map.119 = bf16[16,24,1024]{2,1,0:T(8,128)(2,1)} custom-call(s32[12]{0:T(128)S(1)} %concatenate.29.info, bf16[2,1024,1024]{2,1,0:T(8,128)(2,1)S(1)} %copy-done.5, bf16[64,1024]{1,0:T(8,128)(2,1)S(1)} %copy-done.9, bf16[8,64,128]{2,1,0:T(8,128)(2,1)S(1)} %all-to-all-done.6.lows, s32[8,128]{1,0:T(8,128)S(1)} %reshape.113.ids, ...), custom_call_target="tpu_custom_call" | custom-call | tf_op jit(solution)/shard_map/pallas_call | solution.py:42
  252.1 7.4 %all-to-all-start.8 = ((bf16[16,24,1024]{2,1,0:T(8,128)(2,1)}), bf16[16,24,1024]{2,1,0:T(8,128)(2,1)S(1)}, u32[]{:S(2)}, u32[]{:S(2)}) async-start(bf16[16,24,1024]{2,1,0:T(8,128)(2,1)} %shard_map.119), calls=%async_computation.8 | async-start | bytes 1572864 | tf_op jit(solution)/shard_map/all_to_all | solution.py:387
  260.4 2.0 collective-permute-start.24
  262.4 9.2 %collective-permute-start.25 = (bf16[2,16,1024]{2,1,0:T(8,128)(2,1)S(1)}, bf16[2,16,1024]{2,1,0:T(8,128)(2,1)S(1)}, u32[]{:S(2)}, u32[]{:S(2)}) collective-permute-start(bf16[2,16,1024]{2,1,0:T(8,128)(2,1)S(1)} %get-tuple-element.41), channel_id=1, source_target_pairs={{0,2},{2,0},{4,34},{6,32},{8,66},{10,64},{12,98},{14,96},{16,130},... | collective-permute-start | bytes 196616 | tf_op jit(solution)/shard_map/ppermute | solution.py:428
  271.6 1.6 fusion
  273.2 1.2 collective-permute-done.24
  274.4 1.3 collective-permute-done.25
  275.7 2.3 shard_map.120
  278.0 9.5 %all-to-all-start.9 = ((bf16[8,8,1024]{2,1,0:T(8,128)(2,1)}), bf16[8,8,1024]{2,1,0:T(8,128)(2,1)S(1)}, u32[]{:S(2)}, u32[]{:S(2)}) async-start(bf16[8,8,1024]{2,1,0:T(8,128)(2,1)} %shard_map.120), calls=%async_computation.9 | async-start | bytes 262144 | tf_op jit(solution)/shard_map/all_to_all | solution.py:392
  288.2 8.4 %all-to-all-done.9 = bf16[8,8,1024]{2,1,0:T(8,128)(2,1)S(1)} async-done(((bf16[8,8,1024]{2,1,0:T(8,128)(2,1)}), bf16[8,8,1024]{2,1,0:T(8,128)(2,1)S(1)}, u32[]{:S(2)}, u32[]{:S(2)}) %all-to-all-start.9) | async-done | bytes 131104 | tf_op jit(solution)/shard_map/all_to_all | solution.py:392
  (114 shorter events, 22.9 us)
Async XLA Ops:
  0.6 105.7 %copy-start = (bf16[1,32,8192]{2,1,0:T(8,128)(2,1)S(1)}, bf16[1,32,8192]{2,1,0:T(8,128)(2,1)}, u32[]{:S(2)}) copy-start(bf16[1,32,8192]{2,1,0:T(8,128)(2,1)} %param.12) | copy-start | bytes 1572868
  3.0 17.9 %all-to-all-start = ((bf16[8,8,1152]{2,0,1:T(8,128)(2,1)}), bf16[8,8,1152]{2,0,1:T(8,128)(2,1)S(1)}, u32[]{:S(2)}, u32[]{:S(2)}) async-start(bf16[8,8,1152]{2,0,1:T(8,128)(2,1)} %pad_maximum_fusion.1), calls=%async_computation | async-start | bytes 294912 | tf_op jit(solution)/shard_map/all_to_all | solution.py:292
  23.3 36.5 %all-to-all-start.1 = ((bf16[16,72,1024]{2,1,0:T(8,128)(2,1)}), bf16[16,72,1024]{2,1,0:T(8,128)(2,1)S(1)}, u32[]{:S(2)}, u32[]{:S(2)}) async-start(bf16[16,72,1024]{2,1,0:T(8,128)(2,1)} %broadcast_in_dim.59), calls=%async_computation.1 | async-start | bytes 4718592 | tf_op jit(solution)/shard_map/all_to_all | solution.py:23
  30.6 37.5 %collective-permute-start = (bf16[1024,512]{1,0:T(8,128)(2,1)}, bf16[1024,512]{1,0:T(8,128)(2,1)}, u32[]{:S(2)}, u32[]{:S(2)}) collective-permute-start(bf16[1024,512]{1,0:T(8,128)(2,1)} %gate.1), channel_id=1, source_target_pairs={{0,1},{1,0},{2,3},{3,2},{4,5},{5,4},{6,7},{7,6},{8,9},{9,8},{10,11... | collective-permute-start | bytes 3145736 | tf_op jit(solution)/shard_map/ppermute | solution.py:282
  30.6 37.5 %collective-permute-start.1 = (bf16[1024,512]{1,0:T(8,128)(2,1)}, bf16[1024,512]{1,0:T(8,128)(2,1)}, u32[]{:S(2)}, u32[]{:S(2)}) collective-permute-start(bf16[1024,512]{1,0:T(8,128)(2,1)} %up.1), channel_id=1, source_target_pairs={{0,1},{1,0},{2,3},{3,2},{4,5},{5,4},{6,7},{7,6},{8,9},{9,8},{10,11... | collective-permute-start | bytes 3145736 | tf_op jit(solution)/shard_map/ppermute | solution.py:282
  32.9 33.7 %copy-start.20 = (bf16[256,512]{1,0:T(8,128)(2,1)S(1)}, bf16[256,512]{1,0:T(8,128)(2,1)}, u32[]{:S(2)}) copy-start(bf16[256,512]{1,0:T(8,128)(2,1)} %param.14) | copy-start | bytes 786436
  59.8 46.5 %all-to-all-start.2 = ((bf16[16,32,1024]{2,1,0:T(8,128)(2,1)}), bf16[16,32,1024]{2,1,0:T(8,128)(2,1)}, u32[]{:S(2)}, u32[]{:S(2)}) async-start(bf16[16,32,1024]{2,1,0:T(8,128)(2,1)} %bitcast.71), calls=%async_computation.2 | async-start | bytes 2097152 | tf_op jit(solution)/shard_map/all_to_all | solution.py:320
  66.7 1.4 collective-permute-start.2
  68.1 1.2 copy-start.16
  69.3 1.2 copy-start.17
  72.5 1.5 copy-start.21
  72.5 27.6 %copy-start.1 = (bf16[2,1024,1024]{2,1,0:T(8,128)(2,1)}, bf16[2,1024,1024]{2,1,0:T(8,128)(2,1)S(1)}, u32[]{:S(2)}) copy-start(bf16[2,1024,1024]{2,1,0:T(8,128)(2,1)S(1)} %get-tuple-element.19.weight) | copy-start | bytes 12582916
  74.0 9.7 %collective-permute-start.3 = (bf16[128,1024]{1,0:T(8,128)(2,1)S(1)}, bf16[128,1024]{1,0:T(8,128)(2,1)S(1)}, u32[]{:S(2)}, u32[]{:S(2)}) collective-permute-start(bf16[128,1024]{1,0:T(8,128)(2,1)S(1)} %get-tuple-element.20), channel_id=1, source_target_pairs={{0,32},{32,64},{64,96},{96,128},{128,160},{160,192},{192,224},{224... | collective-permute-start | bytes 786440 | tf_op jit(solution)/shard_map/ppermute | solution.py:285
  75.3 8.3 %collective-permute-start.4 = (bf16[128,1024]{1,0:T(8,128)(2,1)S(1)}, bf16[128,1024]{1,0:T(8,128)(2,1)S(1)}, u32[]{:S(2)}, u32[]{:S(2)}) collective-permute-start(bf16[128,1024]{1,0:T(8,128)(2,1)S(1)} %get-tuple-element.21), channel_id=1, source_target_pairs={{0,224},{32,0},{64,32},{96,64},{128,96},{160,128},{192,160},{224,1... | collective-permute-start | bytes 786440 | tf_op jit(solution)/shard_map/ppermute | solution.py:285
  85.6 14.4 %collective-permute-start.5 = (bf16[2,128,1024]{2,1,0:T(8,128)(2,1)S(1)}, bf16[2,128,1024]{2,1,0:T(8,128)(2,1)S(1)}, u32[]{:S(2)}, u32[]{:S(2)}) collective-permute-start(bf16[2,128,1024]{2,1,0:T(8,128)(2,1)S(1)} %get-tuple-element.22), channel_id=1, source_target_pairs={{0,32},{32,64},{64,96},{96,128},{128,160},{160,192},{192,224},{224... | collective-permute-start | bytes 1572872 | tf_op jit(solution)/shard_map/ppermute | solution.py:285
  85.8 14.2 %collective-permute-start.6 = (bf16[2,128,1024]{2,1,0:T(8,128)(2,1)S(1)}, bf16[2,128,1024]{2,1,0:T(8,128)(2,1)S(1)}, u32[]{:S(2)}, u32[]{:S(2)}) collective-permute-start(bf16[2,128,1024]{2,1,0:T(8,128)(2,1)S(1)} %get-tuple-element.23), channel_id=1, source_target_pairs={{0,224},{32,0},{64,32},{96,64},{128,96},{160,128},{192,160},{224,1... | collective-permute-start | bytes 1572872 | tf_op jit(solution)/shard_map/ppermute | solution.py:285
  103.1 13.7 %collective-permute-start.7 = (bf16[2,128,1024]{2,1,0:T(8,128)(2,1)}, bf16[2,128,1024]{2,1,0:T(8,128)(2,1)S(1)}, u32[]{:S(2)}, u32[]{:S(2)}) collective-permute-start(bf16[2,128,1024]{2,1,0:T(8,128)(2,1)} %get-tuple-element.24), channel_id=1, source_target_pairs={{0,32},{32,64},{64,96},{96,128},{128,160},{160,192},{192,224},{224... | collective-permute-start | bytes 1572872 | tf_op jit(solution)/shard_map/ppermute | solution.py:285
  103.1 13.7 %collective-permute-start.8 = (bf16[2,128,1024]{2,1,0:T(8,128)(2,1)}, bf16[2,128,1024]{2,1,0:T(8,128)(2,1)}, u32[]{:S(2)}, u32[]{:S(2)}) collective-permute-start(bf16[2,128,1024]{2,1,0:T(8,128)(2,1)} %get-tuple-element.25), channel_id=1, source_target_pairs={{0,224},{32,0},{64,32},{96,64},{128,96},{160,128},{192,160},{224,1... | collective-permute-start | bytes 1572872 | tf_op jit(solution)/shard_map/ppermute | solution.py:285
  106.3 50.8 %collective-permute-start.11 = (bf16[16,2,16,1024]{3,2,1,0:T(8,128)(2,1)}, bf16[16,2,16,1024]{3,2,1,0:T(8,128)(2,1)}, u32[]{:S(2)}, u32[]{:S(2)}) collective-permute-start(bf16[16,2,16,1024]{3,2,1,0:T(8,128)(2,1)} %bitcast.14.outer), channel_id=1, source_target_pairs={{0,1},{1,0},{2,3},{3,2},{4,5},{5,4},{6,7},{7,6},{8,9},{9,8},{10,11... | collective-permute-start | bytes 3145736 | tf_op jit(solution)/shard_map/ppermute | solution.py:282
  106.3 3.0 %collective-permute-start.12 = (bf16[32,1024]{1,0:T(8,128)(2,1)S(1)}, bf16[32,1024]{1,0:T(8,128)(2,1)S(1)}, u32[]{:S(2)}, u32[]{:S(2)}) collective-permute-start(bf16[32,1024]{1,0:T(8,128)(2,1)S(1)} %dynamic-slice_bitcast_fusion.4), channel_id=1, source_target_pairs={{0,1},{1,0},{2,3},{3,2},{4,5},{5,4},{6,7},{7,6},{8,9},{9,8},{10,11... | collective-permute-start | bytes 196616 | tf_op jit(solution)/shard_map/ppermute | solution.py:282
  109.3 19.5 %copy-start.7 = (bf16[64,1024]{1,0:T(8,128)(2,1)}, bf16[64,1024]{1,0:T(8,128)(2,1)S(1)}, u32[]{:S(2)}) copy-start(bf16[64,1024]{1,0:T(8,128)(2,1)S(1)} %pad_maximum_fusion.3.inner) | copy-start | bytes 393220
  116.8 2.2 copy-start.2
  122.5 34.6 %collective-permute-start.9 = (bf16[2,128,1024]{2,1,0:T(8,128)(2,1)}, bf16[2,128,1024]{2,1,0:T(8,128)(2,1)S(1)}, u32[]{:S(2)}, u32[]{:S(2)}) collective-permute-start(bf16[2,128,1024]{2,1,0:T(8,128)(2,1)} %get-tuple-element.26), channel_id=1, source_target_pairs={{0,32},{32,64},{64,96},{96,128},{128,160},{160,192},{192,224},{224... | collective-permute-start | bytes 1572872 | tf_op jit(solution)/shard_map/ppermute | solution.py:285
  122.7 34.5 %collective-permute-start.10 = (bf16[2,128,1024]{2,1,0:T(8,128)(2,1)}, bf16[2,128,1024]{2,1,0:T(8,128)(2,1)}, u32[]{:S(2)}, u32[]{:S(2)}) collective-permute-start(bf16[2,128,1024]{2,1,0:T(8,128)(2,1)} %get-tuple-element.27), channel_id=1, source_target_pairs={{0,224},{32,0},{64,32},{96,64},{128,96},{160,128},{192,160},{224,1... | collective-permute-start | bytes 1572872 | tf_op jit(solution)/shard_map/ppermute | solution.py:285
  157.1 2.2 copy-start.3
  159.3 0.9 copy-start.22
  164.5 0.7 copy-start.25
  165.2 13.7 %collective-permute-start.16 = (bf16[2,128,1024]{2,1,0:T(8,128)(2,1)S(1)}, bf16[2,128,1024]{2,1,0:T(8,128)(2,1)S(1)}, u32[]{:S(2)}, u32[]{:S(2)}) collective-permute-start(bf16[2,128,1024]{2,1,0:T(8,128)(2,1)S(1)} %get-tuple-element.31.refs_4_), channel_id=1, source_target_pairs={{0,32},{32,64},{64,96},{96,128},{128,160},{160,192},{192,224},{224... | collective-permute-start | bytes 1572872 | tf_op jit(solution)/shard_map/ppermute | solution.py:285
  165.8 14.0 %collective-permute-start.14 = (bf16[2,128,1024]{2,1,0:T(8,128)(2,1)S(1)}, bf16[2,128,1024]{2,1,0:T(8,128)(2,1)}, u32[]{:S(2)}, u32[]{:S(2)}) collective-permute-start(bf16[2,128,1024]{2,1,0:T(8,128)(2,1)S(1)} %get-tuple-element.31.refs_4_), channel_id=1, source_target_pairs={{0,224},{32,0},{64,32},{96,64},{128,96},{160,128},{192,160},{224,1... | collective-permute-start | bytes 1572872 | tf_op jit(solution)/shard_map/ppermute | solution.py:285
  168.5 0.8 copy-start.10
  179.0 14.7 %collective-permute-start.17 = (bf16[2,128,1024]{2,1,0:T(8,128)(2,1)S(1)}, bf16[2,128,1024]{2,1,0:T(8,128)(2,1)}, u32[]{:S(2)}, u32[]{:S(2)}) collective-permute-start(bf16[2,128,1024]{2,1,0:T(8,128)(2,1)S(1)} %collective-permute-done.16.refs_3_), channel_id=1, source_target_pairs={{0,32},{32,64},{64,96},{96,128},{128,160},{160,192},{192,224},{224... | collective-permute-start | bytes 1572872 | tf_op jit(solution)/shard_map/ppermute | solution.py:285
  179.0 0.8 copy-start.13
  179.8 21.1 %collective-permute-start.15 = (bf16[2,128,1024]{2,1,0:T(8,128)(2,1)}, bf16[2,128,1024]{2,1,0:T(8,128)(2,1)}, u32[]{:S(2)}, u32[]{:S(2)}) collective-permute-start(bf16[2,128,1024]{2,1,0:T(8,128)(2,1)} %collective-permute-done.14.refs_2_), channel_id=1, source_target_pairs={{0,224},{32,0},{64,32},{96,64},{128,96},{160,128},{192,160},{224,1... | collective-permute-start | bytes 1572872 | tf_op jit(solution)/shard_map/ppermute | solution.py:285
  183.7 12.2 %all-to-all-start.5 = ((bf16[16,32,128]{2,1,0:T(8,128)(2,1)}), bf16[16,32,128]{2,1,0:T(8,128)(2,1)}, u32[]{:S(2)}, u32[]{:S(2)}) async-start(bf16[16,32,128]{2,1,0:T(8,128)(2,1)} %broadcast_in_dim.63), calls=%async_computation.5 | async-start | bytes 262144 | tf_op jit(solution)/shard_map/all_to_all | solution.py:23
  193.7 34.3 %collective-permute-start.18 = (bf16[2,128,1024]{2,1,0:T(8,128)(2,1)}, bf16[2,128,1024]{2,1,0:T(8,128)(2,1)S(1)}, u32[]{:S(2)}, u32[]{:S(2)}) collective-permute-start(bf16[2,128,1024]{2,1,0:T(8,128)(2,1)} %collective-permute-done.17.refs_1_), channel_id=1, source_target_pairs={{0,32},{32,64},{64,96},{96,128},{128,160},{160,192},{192,224},{224... | collective-permute-start | bytes 1572872 | tf_op jit(solution)/shard_map/ppermute | solution.py:285
  197.5 12.4 %all-to-all-start.6 = ((bf16[8,64,128]{2,1,0:T(8,128)(2,1)}), bf16[8,64,128]{2,1,0:T(8,128)(2,1)S(1)}, u32[]{:S(2)}, u32[]{:S(2)}) async-start(bf16[8,64,128]{2,1,0:T(8,128)(2,1)} %broadcast_in_dim.64), calls=%async_computation.6 | async-start | bytes 262144 | tf_op jit(solution)/shard_map/all_to_all | solution.py:23
  200.9 28.4 %collective-permute-start.20 = (bf16[2,128,1024]{2,1,0:T(8,128)(2,1)}, bf16[2,128,1024]{2,1,0:T(8,128)(2,1)}, u32[]{:S(2)}, u32[]{:S(2)}) collective-permute-start(bf16[2,128,1024]{2,1,0:T(8,128)(2,1)} %collective-permute-done.15.refs_0_), channel_id=1, source_target_pairs={{0,224},{32,0},{64,32},{96,64},{128,96},{160,128},{192,160},{224,1... | collective-permute-start | bytes 1572872 | tf_op jit(solution)/shard_map/ppermute | solution.py:285
  209.9 2.2 copy-start.4
  212.1 0.9 copy-start.8
  213.0 1.0 copy-start.11
  214.0 1.0 copy-start.14
  220.3 1.1 copy-start.6
  221.3 30.7 %all-to-all-start.7 = ((bf16[16,40,1024]{2,1,0:T(8,128)(2,1)}), bf16[16,40,1024]{2,1,0:T(8,128)(2,1)}, u32[]{:S(2)}, u32[]{:S(2)}) async-start(bf16[16,40,1024]{2,1,0:T(8,128)(2,1)} %copy-done.6), calls=%async_computation.7 | async-start | bytes 2621440 | tf_op jit(solution)/shard_map/all_to_all | solution.py:387
  228.7 10.5 %collective-permute-start.19 = (bf16[128,1024]{1,0:T(8,128)(2,1)}, bf16[128,1024]{1,0:T(8,128)(2,1)}, u32[]{:S(2)}, u32[]{:S(2)}) collective-permute-start(bf16[128,1024]{1,0:T(8,128)(2,1)} %slice_bitcast_fusion.1), channel_id=1, source_target_pairs={{0,32},{32,64},{64,96},{96,128},{128,160},{160,192},{192,224},{224... | collective-permute-start | bytes 786440 | tf_op jit(solution)/shard_map/ppermute | solution.py:285
  231.0 8.2 %collective-permute-start.21 = (bf16[128,1024]{1,0:T(8,128)(2,1)}, bf16[128,1024]{1,0:T(8,128)(2,1)}, u32[]{:S(2)}, u32[]{:S(2)}) collective-permute-start(bf16[128,1024]{1,0:T(8,128)(2,1)} %slice_bitcast_fusion), channel_id=1, source_target_pairs={{0,224},{32,0},{64,32},{96,64},{128,96},{160,128},{192,160},{224,1... | collective-permute-start | bytes 786440 | tf_op jit(solution)/shard_map/ppermute | solution.py:285
  235.2 6.9 %collective-permute-start.13 = (bf16[16,8,512]{2,1,0:T(8,128)(2,1)}, bf16[16,8,512]{2,1,0:T(8,128)(2,1)}, u32[]{:S(2)}, u32[]{:S(2)}) collective-permute-start(bf16[16,8,512]{2,1,0:T(8,128)(2,1)} %dynamic-slice_bitcast_fusion), channel_id=1, source_target_pairs={{0,1},{1,0},{2,3},{3,2},{4,5},{5,4},{6,7},{7,6},{8,9},{9,8},{10,11... | collective-permute-start | bytes 393224 | tf_op jit(solution)/shard_map/ppermute | solution.py:282
  235.2 1.0 copy-start.12
  236.3 1.0 copy-start.15
  237.3 4.8 %copy-start.26 = (bf16[128,1024]{1,0:T(8,128)(2,1)S(1)}, bf16[128,1024]{1,0:T(8,128)(2,1)}, u32[]{:S(2)}) copy-start(bf16[128,1024]{1,0:T(8,128)(2,1)} %copy-done.25) | copy-start | bytes 786436
  239.2 8.0 %copy-start.5 = (bf16[2,1024,1024]{2,1,0:T(8,128)(2,1)S(1)}, bf16[2,1024,1024]{2,1,0:T(8,128)(2,1)}, u32[]{:S(2)}) copy-start(bf16[2,1024,1024]{2,1,0:T(8,128)(2,1)} %copy-done.1) | copy-start | bytes 12582916
  241.6 5.5 %copy-start.23 = (f32[2,32,1024]{2,1,0:T(8,128)}, f32[2,32,1024]{2,1,0:T(8,128)S(1)}, u32[]{:S(2)}) copy-start(f32[2,32,1024]{2,1,0:T(8,128)S(1)} %get-tuple-element.32) | copy-start | bytes 786436
  241.6 5.7 %copy-start.9 = (bf16[64,1024]{1,0:T(8,128)(2,1)S(1)}, bf16[64,1024]{1,0:T(8,128)(2,1)}, u32[]{:S(2)}) copy-start(bf16[64,1024]{1,0:T(8,128)(2,1)} %copy-done.7) | copy-start | bytes 393220
  241.6 17.8 %collective-permute-start.23 = (bf16[2,32,1024]{2,1,0:T(8,128)(2,1)}, bf16[2,32,1024]{2,1,0:T(8,128)(2,1)}, u32[]{:S(2)}, u32[]{:S(2)}) collective-permute-start(bf16[2,32,1024]{2,1,0:T(8,128)(2,1)} %get-tuple-element.33), channel_id=1, source_target_pairs={{0,1},{1,0},{2,3},{3,2},{4,5},{5,4},{6,7},{7,6},{8,9},{9,8},{10,11... | collective-permute-start | bytes 393224 | tf_op jit(solution)/shard_map/ppermute | solution.py:282
  245.8 0.7 copy-start.18
  247.2 24.5 %collective-permute-start.22 = (f32[32,1024]{1,0:T(8,128)}, f32[32,1024]{1,0:T(8,128)}, u32[]{:S(2)}, u32[]{:S(2)}) collective-permute-start(f32[32,1024]{1,0:T(8,128)} %slice.36), channel_id=1, source_target_pairs={{0,1},{1,0},{2,3},{3,2},{4,5},{5,4},{6,7},{7,6},{8,9},{9,8},{10,11... | collective-permute-start | bytes 393224 | tf_op jit(solution)/shard_map/ppermute | solution.py:282
  247.3 12.2 %copy-start.24 = (f32[2,32,1024]{2,1,0:T(8,128)S(1)}, f32[2,32,1024]{2,1,0:T(8,128)}, u32[]{:S(2)}) copy-start(f32[2,32,1024]{2,1,0:T(8,128)} %copy-done.23) | copy-start | bytes 786436
  252.1 19.6 %copy-start.19 = (f32[64,1024]{1,0:T(8,128)S(1)}, f32[64,1024]{1,0:T(8,128)}, u32[]{:S(2)}) copy-start(f32[64,1024]{1,0:T(8,128)} %copy-done.18) | copy-start | bytes 786436
  252.1 23.7 %all-to-all-start.8 = ((bf16[16,24,1024]{2,1,0:T(8,128)(2,1)}), bf16[16,24,1024]{2,1,0:T(8,128)(2,1)S(1)}, u32[]{:S(2)}, u32[]{:S(2)}) async-start(bf16[16,24,1024]{2,1,0:T(8,128)(2,1)} %shard_map.119), calls=%async_computation.8 | async-start | bytes 1572864 | tf_op jit(solution)/shard_map/all_to_all | solution.py:387
  260.4 14.0 %collective-permute-start.24 = (bf16[2,16,1024]{2,1,0:T(8,128)(2,1)S(1)}, bf16[2,16,1024]{2,1,0:T(8,128)(2,1)S(1)}, u32[]{:S(2)}, u32[]{:S(2)}) collective-permute-start(bf16[2,16,1024]{2,1,0:T(8,128)(2,1)S(1)} %get-tuple-element.40), channel_id=1, source_target_pairs={{0,0},{2,2},{4,32},{6,34},{8,64},{10,66},{12,96},{14,98},{16,128},... | collective-permute-start | bytes 196616 | tf_op jit(solution)/shard_map/ppermute | solution.py:427
  262.4 13.3 %collective-permute-start.25 = (bf16[2,16,1024]{2,1,0:T(8,128)(2,1)S(1)}, bf16[2,16,1024]{2,1,0:T(8,128)(2,1)S(1)}, u32[]{:S(2)}, u32[]{:S(2)}) collective-permute-start(bf16[2,16,1024]{2,1,0:T(8,128)(2,1)S(1)} %get-tuple-element.41), channel_id=1, source_target_pairs={{0,2},{2,0},{4,34},{6,32},{8,66},{10,64},{12,98},{14,96},{16,130},... | collective-permute-start | bytes 196616 | tf_op jit(solution)/shard_map/ppermute | solution.py:428
  278.0 18.6 %all-to-all-start.9 = ((bf16[8,8,1024]{2,1,0:T(8,128)(2,1)}), bf16[8,8,1024]{2,1,0:T(8,128)(2,1)S(1)}, u32[]{:S(2)}, u32[]{:S(2)}) async-start(bf16[8,8,1024]{2,1,0:T(8,128)(2,1)} %shard_map.120), calls=%async_computation.9 | async-start | bytes 262144 | tf_op jit(solution)/shard_map/all_to_all | solution.py:392

commit v3 on v2

--- a/solution.py
+++ b/solution.py
@@ -89,25 +89,20 @@
     over_columns(gate_out.shape[1], body)
 
 
-def step_kernel(place, own_rows, info, tokens, weight, from_below, from_above, up_out, down_out):
-    rows = up_out.shape[1]
-    half = from_below.shape[0] == 1
+def rest_kernel(own_rows, info, tokens, weight, *outs):
+    rows = outs[0].shape[2]
+    held = [(out, i) for out in outs for i in range(out.shape[0])]
 
     def body(cols):
         block = jnp.concatenate(
-            [rows_at(tokens, place, own_rows), rows_at(tokens, place + 1, own_rows)], axis=0
+            [rows_at(tokens, place, own_rows) for place in range(1, len(held) + 1)], axis=0
         )
         for member in range(2):
-            product = dot(block, weight[member, :, cols])
-            up, down = product[:rows], product[rows:]
-            if not half or member == 0:
-                up = up + from_below[0 if half else member, :, cols].astype(f32)
-            if not half or member == 1:
-                down = down + from_above[0 if half else member, :, cols].astype(f32)
-            up_out[member, :, cols] = up.astype(bf16)
-            down_out[member, :, cols] = down.astype(bf16)
-
-    over_columns(up_out.shape[2], body)
+            product = dot(block, weight[member, :, cols]).astype(bf16)
+            for at, (out, i) in enumerate(held):
+                out[i, member, :, cols] = product[at * rows : (at + 1) * rows]
+
+    over_columns(outs[0].shape[3], body)
 
 
 def mine(values, ids, info):
@@ -135,7 +130,7 @@
 
 
 def middle_kernel(
-    rank, own_rows, info, tokens, weight, from_below, from_above, outer, other_outer, low, ids, upstream,
+    rank, info, product, from_below, from_above, outer, other_outer, low, ids, upstream,
     hidden_out, grads_out, low_out, chosen, mapped,
 ):
     slots = chosen.shape[2]
@@ -155,10 +150,9 @@
     mapped[...] = jnp.zeros_like(mapped)
 
     def body(cols):
-        block = rows_at(tokens, last, own_rows)
         tables = (table(0, cols), table(1, cols))
         gate, up = [
-            dot(block, weight[member, :, cols])
+            product[0, member, :, cols].astype(f32)
             + from_below[member, :, cols].astype(f32)
             + from_above[member, :, cols].astype(f32)
             + adapter_scale * dot(chosen[member], tables[member])
@@ -327,13 +321,17 @@
     )
     going_up = ring(going_up, up_ring)[None]
     going_down = ring(going_down, down_ring)[None]
-    for step, place in enumerate((1, 3, 5), 2):
-        going_up, going_down = call(
-            functools.partial(step_kernel, place, own_rows),
-            info,
-            [gathered, weight, going_up, going_down],
-            [((2,) + shape, bf16)] * 2,
-        )
+    going_up = jnp.pad(going_up, ((0, 1), (0, 0), (0, 0)))
+    going_down = jnp.pad(going_down, ((1, 0), (0, 0), (0, 0)))
+    *pairs, product = call(
+        functools.partial(rest_kernel, own_rows),
+        info,
+        [gathered, weight],
+        [((count, 2) + shape, bf16) for count in (2, 2, 2, 1)],
+    )
+    for step, pair in enumerate(pairs, 2):
+        going_up = (pair[0].astype(f32) + going_up.astype(f32)).astype(bf16)
+        going_down = (pair[1].astype(f32) + going_down.astype(f32)).astype(bf16)
         going_up = ring(going_up, up_ring)
         going_down = ring(going_down, down_ring)
 
@@ -347,9 +345,9 @@
 
     slots = 2 * chips * rank
     hidden_rows, grads, grad_low = call(
-        functools.partial(middle_kernel, rank, own_rows),
+        functools.partial(middle_kernel, rank),
         info,
-        [gathered, weight, going_up, going_down, outer, other_outer, low, row_ids, upstream],
+        [product, going_up, going_down, outer, other_outer, low, row_ids, upstream],
         [(shape, bf16), ((2,) + shape, bf16), ((2 * rank, rows), bf16)],
         (pltpu.VMEM((2, rows, slots), bf16), pltpu.VMEM((2, slots, rows), f32)),
     )

time: 301 us -> 286 us (0.950)
  waiting for transfers between devices: 94.7 us -> 72.8 us
  other arithmetic: 9.8 us -> 18.1 us
  Pallas kernels: 36.9 us -> 32.5 us
  blocking collectives: 25 us -> 28.2 us
    ppermute x16, waiting for transfers between devices: 38.1 us -> 17.5 us  [ring(): return lax.ppermute(value, GROUP, pairs)]
    all_to_all x3, waiting for transfers between devices: 33.4 us -> 23.6 us  [spread(): return lax.all_to_all(copies, axes, split_axis=0, concat_axis=0, tiled=True)]
    all_to_all x1, waiting for transfers between devices: 0.01 us -> 7.47 us  [on_device(): lax.all_to_all(outer, CHIPS, split_axis=0, concat_axis=0, tiled=True)]
    convert_element_type x0 -> x3, other arithmetic: none -> 7.01 us  [on_device(): going_down = (pair[1].astype(f32) + going_down.astype(f32)).astype(bf16)]
    pallas_call x13 -> x11, Pallas kernels: 36.9 us -> 32.5 us  [call(): pl.pallas_call(kernel, out_shape=[jax.ShapeDtypeStruct(shape, dtype) for...]
    unnamed x56 -> x62, local copies, waits for them, and re-layouts: 21.6 us -> 20.8 us
  transfers between devices with their start and end apart: 34 -> 34, of which waited for: 14 -> 12; matrix products, arithmetic and copies ran while one was open for 7% -> 9% of each run, Pallas kernels for 10% -> 9%
where the time goes in v3:
time: 286 us; the launch traced here: 282 us
  starting transfers between devices  95.5 us (33%)
  waiting for transfers between devices  72.8 us (25%)
  local copies, waits for them, and re-layouts  33.4 us (12%)
  Pallas kernels  32.5 us (11%)
  blocking collectives  28.2 us (10%)
  other arithmetic  18.1 us (6%)
    pallas_call x11, Pallas kernels, call(): pl.pallas_call(kernel, out_shape=[jax.ShapeDtypeStruct(shape, dtype) for...  32.5 us
    ppermute x16, starting transfers between devices, ring(): return lax.ppermute(value, GROUP, pairs)  25.7 us
    all_to_all x3, waiting for transfers between devices, spread(): return lax.all_to_all(copies, axes, split_axis=0, concat_axis=0, tiled=True)  23.6 us
    unnamed x62, local copies, waits for them, and re-layouts  20.8 us
    all_to_all x3, starting transfers between devices, spread(): return lax.all_to_all(copies, axes, split_axis=0, concat_axis=0, tiled=True)  17.8 us
    ppermute x16, waiting for transfers between devices, ring(): return lax.ppermute(value, GROUP, pairs)  17.5 us
    all_to_all x1, blocking collectives, spread(): return lax.all_to_all(copies, axes, split_axis=0, concat_axis=0, tiled=True)  14.7 us
    all_to_all x2, starting transfers between devices, to_owners(): return lax.all_to_all(part, CHIPS, split_axis=0, concat_axis=0, tiled=True)  14.1 us
  transfers between devices with their start and end apart: 34, of which 12 were waited for; matrix products, arithmetic and copies ran while one was open for 9% of the time, Pallas kernels for 9%

profile of v3, /device:TPU:16, one launch (start us, length us, event | category | flops | bytes accessed | tf_op | source)
XLA Modules:
  0.0 281.6 jit_solution(14021562683222807965)
XLA Ops:
  1.4 1.6 pad_maximum_fusion.1
  3.0 8.5 %all-to-all-start = ((bf16[8,8,1152]{2,0,1:T(8,128)(2,1)}), bf16[8,8,1152]{2,0,1:T(8,128)(2,1)S(1)}, u32[]{:S(2)}, u32[]{:S(2)}) async-start(bf16[8,8,1152]{2,0,1:T(8,128)(2,1)} %pad_maximum_fusion.1), calls=%async_computation | async-start | bytes 294912 | tf_op jit(solution)/shard_map/all_to_all | solution.py:286
  12.2 8.7 %all-to-all-done = bf16[8,8,1152]{2,0,1:T(8,128)(2,1)S(1)} async-done(((bf16[8,8,1152]{2,0,1:T(8,128)(2,1)}), bf16[8,8,1152]{2,0,1:T(8,128)(2,1)S(1)}, u32[]{:S(2)}, u32[]{:S(2)}) %all-to-all-start) | async-done | bytes 147488 | tf_op jit(solution)/shard_map/all_to_all | solution.py:286
  21.6 1.8 broadcast_in_dim.59
  23.3 7.4 %all-to-all-start.1 = ((bf16[16,72,1024]{2,1,0:T(8,128)(2,1)}), bf16[16,72,1024]{2,1,0:T(8,128)(2,1)S(1)}, u32[]{:S(2)}, u32[]{:S(2)}) async-start(bf16[16,72,1024]{2,1,0:T(8,128)(2,1)} %broadcast_in_dim.59), calls=%async_computation.1 | async-start | bytes 4718592 | tf_op jit(solution)/shard_map/all_to_all | solution.py:23
  31.5 3.8 %collective-permute-done.2.other_hidden = bf16[16,8,512]{2,1,0:T(8,128)(2,1)S(1)} collective-permute-done((bf16[16,8,512]{2,1,0:T(8,128)(2,1)S(1)}, bf16[16,8,512]{2,1,0:T(8,128)(2,1)S(1)}, u32[]{:S(2)}, u32[]{:S(2)}) %collective-permute-start.2) | collective-permute-done | bytes 131104 | tf_op jit(solution)/shard_map/ppermute | solution.py:276
  35.3 1.2 copy-done.15
  36.5 1.2 copy-done.16
  37.8 1.9 shard_map.111
  39.7 2.0 copy-done.1
  42.4 17.6 %all-to-all-done.1.tokens = bf16[16,72,1024]{2,1,0:T(8,128)(2,1)S(1)} async-done(((bf16[16,72,1024]{2,1,0:T(8,128)(2,1)}), bf16[16,72,1024]{2,1,0:T(8,128)(2,1)S(1)}, u32[]{:S(2)}, u32[]{:S(2)}) %all-to-all-start.1) | async-done | bytes 2359328 | tf_op jit(solution)/shard_map/all_to_all | solution.py:23
  60.0 2.2 copy-done.2
  62.2 1.5 shard_map.113
  63.7 1.3 collective-permute-start.3
  65.0 2.0 collective-permute-start.7
  67.0 4.7 %shard_map.112 = (bf16[2,2,128,1024]{3,2,1,0:T(8,128)(2,1)S(1)}, bf16[2,2,128,1024]{3,2,1,0:T(8,128)(2,1)S(1)}, bf16[2,2,128,1024]{3,2,1,0:T(8,128)(2,1)S(1)}, bf16[1,2,128,1024]{3,2,1,0:T(8,128)(2,1)S(1)}) custom-call(s32[12]{0:T(128)S(1)} %concatenate.29.info, bf16[16,72,1024]{2,1,0:T(8,128)(2,1)S(1)} %all-to-all-done.1.tokens, ...), custom_call_target="tpu_custom_call" | custom-call | tf_op jit(solution)/shard_map/pallas_call | solution.py:42
  71.7 1.2 fusion
  72.9 3.2 %collective-permute-start.8 = (bf16[2,128,1024]{2,1,0:T(8,128)(2,1)}, bf16[2,128,1024]{2,1,0:T(8,128)(2,1)}, u32[]{:S(2)}, u32[]{:S(2)}) collective-permute-start(bf16[2,128,1024]{2,1,0:T(8,128)(2,1)} %get-tuple-element.36), channel_id=1, source_target_pairs={{0,224},{32,0},{64,32},{96,64},{128,96},{160,128},{192,160},{224,1... | collective-permute-start | bytes 1572872 | tf_op jit(solution)/shard_map/ppermute | solution.py:279
  76.8 1.6 copy.29
  78.3 7.2 %all-to-all-start.2 = ((bf16[16,32,1024]{2,1,0:T(8,128)(2,1)}), bf16[16,32,1024]{2,1,0:T(8,128)(2,1)}, u32[]{:S(2)}, u32[]{:S(2)}) async-start(bf16[16,32,1024]{2,1,0:T(8,128)(2,1)} %bitcast.87), calls=%async_computation.2 | async-start | bytes 2097152 | tf_op jit(solution)/shard_map/all_to_all | solution.py:314
  85.6 2.9 %fusion.1 = (bf16[2,128,1024]{2,1,0:T(8,128)(2,1)}, bf16[2,128,1024]{2,1,0:T(8,128)(2,1)}) fusion(bf16[2,128,1024]{2,1,0:T(8,128)(2,1)} %collective-permute-done.8, bf16[2,2,128,1024]{3,2,1,0:T(8,128)(2,1)} %copy-done.18, bf16[2,128,1024]{2,1,0:T(8,128)(2,1)} %collective-permute-done.4), kind=kLoop, calls=%fused_computation.4 | loop fusion | flops 2097152 | bytes 3145728 | tf_op jit(solution)/shard_map/convert_element_type | solution.py:334
  88.5 3.2 %collective-permute-start.9 = (bf16[2,128,1024]{2,1,0:T(8,128)(2,1)}, bf16[2,128,1024]{2,1,0:T(8,128)(2,1)}, u32[]{:S(2)}, u32[]{:S(2)}) collective-permute-start(bf16[2,128,1024]{2,1,0:T(8,128)(2,1)} %get-tuple-element.34), channel_id=1, source_target_pairs={{0,224},{32,0},{64,32},{96,64},{128,96},{160,128},{192,160},{224,1... | collective-permute-start | bytes 1572872 | tf_op jit(solution)/shard_map/ppermute | solution.py:279
  91.9 7.5 %all-to-all-done.2 = bf16[16,32,1024]{2,1,0:T(8,128)(2,1)} async-done(((bf16[16,32,1024]{2,1,0:T(8,128)(2,1)}), bf16[16,32,1024]{2,1,0:T(8,128)(2,1)}, u32[]{:S(2)}, u32[]{:S(2)}) %all-to-all-start.2) | async-done | bytes 1048608 | tf_op jit(solution)/shard_map/all_to_all | solution.py:314
  100.2 1.6 collective-permute-done.5
  101.9 2.9 %fusion.2 = (bf16[2,128,1024]{2,1,0:T(8,128)(2,1)}, bf16[2,128,1024]{2,1,0:T(8,128)(2,1)}) fusion(bf16[2,128,1024]{2,1,0:T(8,128)(2,1)} %collective-permute-done.9, bf16[2,2,128,1024]{3,2,1,0:T(8,128)(2,1)} %copy-done.17, bf16[2,128,1024]{2,1,0:T(8,128)(2,1)} %collective-permute-done.5), kind=kLoop, calls=%fused_computation.6 | loop fusion | flops 2097152 | bytes 3145728 | tf_op jit(solution)/shard_map/convert_element_type | solution.py:334
  104.8 3.0 %collective-permute-start.10 = (bf16[2,128,1024]{2,1,0:T(8,128)(2,1)}, bf16[2,128,1024]{2,1,0:T(8,128)(2,1)}, u32[]{:S(2)}, u32[]{:S(2)}) collective-permute-start(bf16[2,128,1024]{2,1,0:T(8,128)(2,1)} %get-tuple-element.32), channel_id=1, source_target_pairs={{0,224},{32,0},{64,32},{96,64},{128,96},{160,128},{192,160},{224,1... | collective-permute-start | bytes 1572872 | tf_op jit(solution)/shard_map/ppermute | solution.py:279
  108.4 1.5 copy.25
  110.8 2.3 shard_map.114
  113.1 13.5 %all_to_all.69 = f32[8,32,128]{2,1,0:T(8,128)} all-to-all(f32[8,32,128]{2,1,0:T(8,128)S(1)} %shard_map.114), channel_id=1, replica_groups=mesh['z'=8,'y'=4,'x'=4,'c'=2] {'z'}, dimensions={0} | all-to-all | bytes 262144 | tf_op jit(solution)/shard_map/all_to_all | solution.py:341
  127.6 14.7 %all_to_all.70 = bf16[16,32,128]{2,1,0:T(8,128)(2,1)} all-to-all(bf16[16,32,128]{2,1,0:T(8,128)(2,1)S(1)} %broadcast_in_dim.62), channel_id=1, replica_groups=mesh['z'=8,'y'=4,'x'=4,'c'=2] {'y','x'}, dimensions={0} | all-to-all | bytes 262144 | tf_op jit(solution)/shard_map/all_to_all | solution.py:23
  143.3 0.9 copy-done.23
  144.2 3.8 %shard_map.115 = (bf16[128,1024]{1,0:T(8,128)(2,1)S(1)}, bf16[2,128,1024]{2,1,0:T(8,128)(2,1)S(1)}, bf16[32,128]{1,0:T(8,128)(2,1)S(1)}) custom-call(s32[12]{0:T(128)S(1)} %concatenate.29.info, bf16[1,2,128,1024]{3,2,1,0:T(8,128)(2,1)S(1)} %get-tuple-element.18.product, bf16[2,128,1024]{2,1,0:T(8,128)(2,1)} %collective-permute-done.6.from_below, ...), custom_call_target="tpu_custom_call" | custom-call | tf_op jit(solution)/shard_map/pallas_call | solution.py:42
  149.3 2.7 collective-permute-start.14
  152.8 10.3 %collective-permute-done.16.refs_3_ = bf16[2,128,1024]{2,1,0:T(8,128)(2,1)S(1)} collective-permute-done((bf16[2,128,1024]{2,1,0:T(8,128)(2,1)S(1)}, bf16[2,128,1024]{2,1,0:T(8,128)(2,1)S(1)}, u32[]{:S(2)}, u32[]{:S(2)}) %collective-permute-start.16) | collective-permute-done | bytes 524320 | tf_op jit(solution)/shard_map/ppermute | solution.py:279
  163.9 3.2 %collective-permute-start.15 = (bf16[2,128,1024]{2,1,0:T(8,128)(2,1)}, bf16[2,128,1024]{2,1,0:T(8,128)(2,1)}, u32[]{:S(2)}, u32[]{:S(2)}) collective-permute-start(bf16[2,128,1024]{2,1,0:T(8,128)(2,1)} %collective-permute-done.14.refs_2_), channel_id=1, source_target_pairs={{0,224},{32,0},{64,32},{96,64},{128,96},{160,128},{192,160},{224,1... | collective-permute-start | bytes 1572872 | tf_op jit(solution)/shard_map/ppermute | solution.py:279
  167.8 5.9 %all-to-all-start.5 = ((bf16[16,32,128]{2,1,0:T(8,128)(2,1)}), bf16[16,32,128]{2,1,0:T(8,128)(2,1)S(1)}, u32[]{:S(2)}, u32[]{:S(2)}) async-start(bf16[16,32,128]{2,1,0:T(8,128)(2,1)} %broadcast_in_dim.63), calls=%async_computation.5 | async-start | bytes 262144 | tf_op jit(solution)/shard_map/all_to_all | solution.py:23
  173.7 5.5 %collective-permute-done.17.refs_1_ = bf16[2,128,1024]{2,1,0:T(8,128)(2,1)} collective-permute-done((bf16[2,128,1024]{2,1,0:T(8,128)(2,1)S(1)}, bf16[2,128,1024]{2,1,0:T(8,128)(2,1)}, u32[]{:S(2)}, u32[]{:S(2)}) %collective-permute-start.17) | collective-permute-done | bytes 524320 | tf_op jit(solution)/shard_map/ppermute | solution.py:279
  181.3 4.4 %all-to-all-start.6 = ((bf16[8,64,128]{2,1,0:T(8,128)(2,1)}), bf16[8,64,128]{2,1,0:T(8,128)(2,1)S(1)}, u32[]{:S(2)}, u32[]{:S(2)}) async-start(bf16[8,64,128]{2,1,0:T(8,128)(2,1)} %broadcast_in_dim.64), calls=%async_computation.6 | async-start | bytes 262144 | tf_op jit(solution)/shard_map/all_to_all | solution.py:23
  185.8 3.2 %collective-permute-start.20 = (bf16[2,128,1024]{2,1,0:T(8,128)(2,1)}, bf16[2,128,1024]{2,1,0:T(8,128)(2,1)}, u32[]{:S(2)}, u32[]{:S(2)}) collective-permute-start(bf16[2,128,1024]{2,1,0:T(8,128)(2,1)} %collective-permute-done.15.refs_0_), channel_id=1, source_target_pairs={{0,224},{32,0},{64,32},{96,64},{128,96},{160,128},{192,160},{224,1... | collective-permute-start | bytes 1572872 | tf_op jit(solution)/shard_map/ppermute | solution.py:279
  189.0 5.8 %all-to-all-done.6.lows = bf16[8,64,128]{2,1,0:T(8,128)(2,1)S(1)} async-done(((bf16[8,64,128]{2,1,0:T(8,128)(2,1)}), bf16[8,64,128]{2,1,0:T(8,128)(2,1)S(1)}, u32[]{:S(2)}, u32[]{:S(2)}) %all-to-all-start.6) | async-done | bytes 131104 | tf_op jit(solution)/shard_map/all_to_all | solution.py:23
  194.8 2.2 copy-done.3
  197.9 1.0 copy-done.10
  199.0 1.0 copy-done.13
  200.0 5.2 %shard_map.116 = bf16[16,40,1024]{2,1,0:T(8,128)(2,1)S(1)} custom-call(s32[12]{0:T(128)S(1)} %concatenate.29.info, bf16[2,1024,1024]{2,1,0:T(8,128)(2,1)S(1)} %copy-done.3, bf16[64,1024]{1,0:T(8,128)(2,1)S(1)} %copy-done.7, bf16[8,64,128]{2,1,0:T(8,128)(2,1)S(1)} %all-to-all-done.6.lows, s32[8,128]{1,0:T(8,128)S(1)} %reshape.125.ids, ...), custom_call_target="tpu_custom_call" | custom-call | tf_op jit(solution)/shard_map/pallas_call | solution.py:42
  205.2 1.0 copy-done.5
  206.3 6.7 %all-to-all-start.7 = ((bf16[16,40,1024]{2,1,0:T(8,128)(2,1)}), bf16[16,40,1024]{2,1,0:T(8,128)(2,1)}, u32[]{:S(2)}, u32[]{:S(2)}) async-start(bf16[16,40,1024]{2,1,0:T(8,128)(2,1)} %copy-done.5), calls=%async_computation.7 | async-start | bytes 2621440 | tf_op jit(solution)/shard_map/all_to_all | solution.py:385
  214.3 1.7 slice_bitcast_fusion
  215.9 2.7 collective-permute-start.21
  218.6 1.6 dynamic-slice_bitcast_fusion
  220.2 1.0 copy-done.11
  221.2 1.0 copy-done.14
  222.3 1.9 shard_map.120.refs_4_
  224.2 2.4 shard_map.121
  227.1 0.9 fusion.7
  228.8 2.0 shard_map.119
  231.7 4.7 %shard_map.117 = bf16[16,24,1024]{2,1,0:T(8,128)(2,1)} custom-call(s32[12]{0:T(128)S(1)} %concatenate.29.info, bf16[2,1024,1024]{2,1,0:T(8,128)(2,1)S(1)} %copy-done.4, bf16[64,1024]{1,0:T(8,128)(2,1)S(1)} %copy-done.8, bf16[8,64,128]{2,1,0:T(8,128)(2,1)S(1)} %all-to-all-done.6.lows, s32[8,128]{1,0:T(8,128)S(1)} %reshape.125.ids, ...), custom_call_target="tpu_custom_call" | custom-call | tf_op jit(solution)/shard_map/pallas_call | solution.py:42
  236.4 7.4 %all-to-all-start.8 = ((bf16[16,24,1024]{2,1,0:T(8,128)(2,1)}), bf16[16,24,1024]{2,1,0:T(8,128)(2,1)S(1)}, u32[]{:S(2)}, u32[]{:S(2)}) async-start(bf16[16,24,1024]{2,1,0:T(8,128)(2,1)} %shard_map.117), calls=%async_computation.8 | async-start | bytes 1572864 | tf_op jit(solution)/shard_map/all_to_all | solution.py:385
  244.8 2.0 collective-permute-start.24
  246.8 9.3 %collective-permute-start.25 = (bf16[2,16,1024]{2,1,0:T(8,128)(2,1)S(1)}, bf16[2,16,1024]{2,1,0:T(8,128)(2,1)S(1)}, u32[]{:S(2)}, u32[]{:S(2)}) collective-permute-start(bf16[2,16,1024]{2,1,0:T(8,128)(2,1)S(1)} %get-tuple-element.43), channel_id=1, source_target_pairs={{0,2},{2,0},{4,34},{6,32},{8,66},{10,64},{12,98},{14,96},{16,130},... | collective-permute-start | bytes 196616 | tf_op jit(solution)/shard_map/ppermute | solution.py:426
  256.7 2.1 collective-permute-done.24
  258.8 1.3 collective-permute-done.25
  260.1 2.3 shard_map.118
  262.4 9.5 %all-to-all-start.9 = ((bf16[8,8,1024]{2,1,0:T(8,128)(2,1)}), bf16[8,8,1024]{2,1,0:T(8,128)(2,1)S(1)}, u32[]{:S(2)}, u32[]{:S(2)}) async-start(bf16[8,8,1024]{2,1,0:T(8,128)(2,1)} %shard_map.118), calls=%async_computation.9 | async-start | bytes 262144 | tf_op jit(solution)/shard_map/all_to_all | solution.py:390
  272.6 8.4 %all-to-all-done.9 = bf16[8,8,1024]{2,1,0:T(8,128)(2,1)S(1)} async-done(((bf16[8,8,1024]{2,1,0:T(8,128)(2,1)}), bf16[8,8,1024]{2,1,0:T(8,128)(2,1)S(1)}, u32[]{:S(2)}, u32[]{:S(2)}) %all-to-all-start.9) | async-done | bytes 131104 | tf_op jit(solution)/shard_map/all_to_all | solution.py:390
  (121 shorter events, 21.8 us)
Async XLA Ops:
  0.6 91.1 %copy-start = (bf16[1,32,8192]{2,1,0:T(8,128)(2,1)S(1)}, bf16[1,32,8192]{2,1,0:T(8,128)(2,1)}, u32[]{:S(2)}) copy-start(bf16[1,32,8192]{2,1,0:T(8,128)(2,1)} %param.12) | copy-start | bytes 1572868
  3.0 17.9 %all-to-all-start = ((bf16[8,8,1152]{2,0,1:T(8,128)(2,1)}), bf16[8,8,1152]{2,0,1:T(8,128)(2,1)S(1)}, u32[]{:S(2)}, u32[]{:S(2)}) async-start(bf16[8,8,1152]{2,0,1:T(8,128)(2,1)} %pad_maximum_fusion.1), calls=%async_computation | async-start | bytes 294912 | tf_op jit(solution)/shard_map/all_to_all | solution.py:286
  23.3 7.9 %copy-start.21 = (bf16[256,512]{1,0:T(8,128)(2,1)S(1)}, bf16[256,512]{1,0:T(8,128)(2,1)}, u32[]{:S(2)}) copy-start(bf16[256,512]{1,0:T(8,128)(2,1)} %param.14) | copy-start | bytes 786436
  23.3 36.7 %all-to-all-start.1 = ((bf16[16,72,1024]{2,1,0:T(8,128)(2,1)}), bf16[16,72,1024]{2,1,0:T(8,128)(2,1)S(1)}, u32[]{:S(2)}, u32[]{:S(2)}) async-start(bf16[16,72,1024]{2,1,0:T(8,128)(2,1)} %broadcast_in_dim.59), calls=%async_computation.1 | async-start | bytes 4718592 | tf_op jit(solution)/shard_map/all_to_all | solution.py:23
  30.8 4.6 %collective-permute-start = (bf16[1024,512]{1,0:T(8,128)(2,1)}, bf16[1024,512]{1,0:T(8,128)(2,1)}, u32[]{:S(2)}, u32[]{:S(2)}) collective-permute-start(bf16[1024,512]{1,0:T(8,128)(2,1)} %gate.1), channel_id=1, source_target_pairs={{0,1},{1,0},{2,3},{3,2},{4,5},{5,4},{6,7},{7,6},{8,9},{9,8},{10,11... | collective-permute-start | bytes 3145736 | tf_op jit(solution)/shard_map/ppermute | solution.py:276
  30.8 4.6 %collective-permute-start.1 = (bf16[1024,512]{1,0:T(8,128)(2,1)}, bf16[1024,512]{1,0:T(8,128)(2,1)}, u32[]{:S(2)}, u32[]{:S(2)}) collective-permute-start(bf16[1024,512]{1,0:T(8,128)(2,1)} %up.1), channel_id=1, source_target_pairs={{0,1},{1,0},{2,3},{3,2},{4,5},{5,4},{6,7},{7,6},{8,9},{9,8},{10,11... | collective-permute-start | bytes 3145736 | tf_op jit(solution)/shard_map/ppermute | solution.py:276
  31.3 4.0 %collective-permute-start.2 = (bf16[16,8,512]{2,1,0:T(8,128)(2,1)S(1)}, bf16[16,8,512]{2,1,0:T(8,128)(2,1)S(1)}, u32[]{:S(2)}, u32[]{:S(2)}) collective-permute-start(bf16[16,8,512]{2,1,0:T(8,128)(2,1)S(1)} %dynamic-slice_bitcast_fusion.1), channel_id=1, source_target_pairs={{0,1},{1,0},{2,3},{3,2},{4,5},{5,4},{6,7},{7,6},{8,9},{9,8},{10,11... | collective-permute-start | bytes 393224 | tf_op jit(solution)/shard_map/ppermute | solution.py:276
  35.3 1.2 copy-start.15
  36.5 1.2 copy-start.16
  39.7 2.0 copy-start.1
  41.7 0.7 copy-start.22
  60.0 2.2 copy-start.2
  63.7 8.0 %collective-permute-start.3 = (bf16[128,1024]{1,0:T(8,128)(2,1)S(1)}, bf16[128,1024]{1,0:T(8,128)(2,1)S(1)}, u32[]{:S(2)}, u32[]{:S(2)}) collective-permute-start(bf16[128,1024]{1,0:T(8,128)(2,1)S(1)} %get-tuple-element.22), channel_id=1, source_target_pairs={{0,32},{32,64},{64,96},{96,128},{128,160},{160,192},{192,224},{224... | collective-permute-start | bytes 786440 | tf_op jit(solution)/shard_map/ppermute | solution.py:279
  65.0 6.7 %collective-permute-start.7 = (bf16[128,1024]{1,0:T(8,128)(2,1)S(1)}, bf16[128,1024]{1,0:T(8,128)(2,1)S(1)}, u32[]{:S(2)}, u32[]{:S(2)}) collective-permute-start(bf16[128,1024]{1,0:T(8,128)(2,1)S(1)} %get-tuple-element.23), channel_id=1, source_target_pairs={{0,224},{32,0},{64,32},{96,64},{128,96},{160,128},{192,160},{224,1... | collective-permute-start | bytes 786440 | tf_op jit(solution)/shard_map/ppermute | solution.py:279
  71.7 5.1 %copy-start.17 = (bf16[2,2,128,1024]{3,2,1,0:T(8,128)(2,1)}, bf16[2,2,128,1024]{3,2,1,0:T(8,128)(2,1)S(1)}, u32[]{:S(2)}) copy-start(bf16[2,2,128,1024]{3,2,1,0:T(8,128)(2,1)S(1)} %get-tuple-element.19) | copy-start | bytes 3145732
  71.7 5.1 %copy-start.18 = (bf16[2,2,128,1024]{3,2,1,0:T(8,128)(2,1)}, bf16[2,2,128,1024]{3,2,1,0:T(8,128)(2,1)S(1)}, u32[]{:S(2)}) copy-start(bf16[2,2,128,1024]{3,2,1,0:T(8,128)(2,1)S(1)} %get-tuple-element.20) | copy-start | bytes 3145732
  71.7 4.5 %copy-start.28 = (bf16[1,2,16,16384]{3,2,1,0:T(8,128)(2,1)S(1)}, bf16[1,2,16,16384]{3,2,1,0:T(8,128)(2,1)}, u32[]{:S(2)}) copy-start(bf16[1,2,16,16384]{3,2,1,0:T(8,128)(2,1)} %param.13) | copy-start | bytes 3145732
  72.9 12.7 %collective-permute-start.4 = (bf16[2,128,1024]{2,1,0:T(8,128)(2,1)}, bf16[2,128,1024]{2,1,0:T(8,128)(2,1)}, u32[]{:S(2)}, u32[]{:S(2)}) collective-permute-start(bf16[2,128,1024]{2,1,0:T(8,128)(2,1)} %get-tuple-element.37), channel_id=1, source_target_pairs={{0,32},{32,64},{64,96},{96,128},{128,160},{160,192},{192,224},{224... | collective-permute-start | bytes 1572872 | tf_op jit(solution)/shard_map/ppermute | solution.py:279
  72.9 12.6 %collective-permute-start.8 = (bf16[2,128,1024]{2,1,0:T(8,128)(2,1)}, bf16[2,128,1024]{2,1,0:T(8,128)(2,1)}, u32[]{:S(2)}, u32[]{:S(2)}) collective-permute-start(bf16[2,128,1024]{2,1,0:T(8,128)(2,1)} %get-tuple-element.36), channel_id=1, source_target_pairs={{0,224},{32,0},{64,32},{96,64},{128,96},{160,128},{192,160},{224,1... | collective-permute-start | bytes 1572872 | tf_op jit(solution)/shard_map/ppermute | solution.py:279
  78.3 21.0 %all-to-all-start.2 = ((bf16[16,32,1024]{2,1,0:T(8,128)(2,1)}), bf16[16,32,1024]{2,1,0:T(8,128)(2,1)}, u32[]{:S(2)}, u32[]{:S(2)}) async-start(bf16[16,32,1024]{2,1,0:T(8,128)(2,1)} %bitcast.87), calls=%async_computation.2 | async-start | bytes 2097152 | tf_op jit(solution)/shard_map/all_to_all | solution.py:314
  88.5 13.3 %collective-permute-start.5 = (bf16[2,128,1024]{2,1,0:T(8,128)(2,1)}, bf16[2,128,1024]{2,1,0:T(8,128)(2,1)}, u32[]{:S(2)}, u32[]{:S(2)}) collective-permute-start(bf16[2,128,1024]{2,1,0:T(8,128)(2,1)} %get-tuple-element.35), channel_id=1, source_target_pairs={{0,32},{32,64},{64,96},{96,128},{128,160},{160,192},{192,224},{224... | collective-permute-start | bytes 1572872 | tf_op jit(solution)/shard_map/ppermute | solution.py:279
  88.5 13.3 %collective-permute-start.9 = (bf16[2,128,1024]{2,1,0:T(8,128)(2,1)}, bf16[2,128,1024]{2,1,0:T(8,128)(2,1)}, u32[]{:S(2)}, u32[]{:S(2)}) collective-permute-start(bf16[2,128,1024]{2,1,0:T(8,128)(2,1)} %get-tuple-element.34), channel_id=1, source_target_pairs={{0,224},{32,0},{64,32},{96,64},{128,96},{160,128},{192,160},{224,1... | collective-permute-start | bytes 1572872 | tf_op jit(solution)/shard_map/ppermute | solution.py:279
  91.8 7.6 %copy-start.29 = (bf16[32,1024]{1,0:T(8,128)(2,1)}, bf16[32,1024]{1,0:T(8,128)(2,1)S(1)}, u32[]{:S(2)}) copy-start(bf16[32,1024]{1,0:T(8,128)(2,1)S(1)} %dynamic-slice_bitcast_fusion.4) | copy-start | bytes 196612
  91.8 7.6 %collective-permute-start.12 = (bf16[32,1024]{1,0:T(8,128)(2,1)S(1)}, bf16[32,1024]{1,0:T(8,128)(2,1)}, u32[]{:S(2)}, u32[]{:S(2)}) collective-permute-start(bf16[32,1024]{1,0:T(8,128)(2,1)S(1)} %dynamic-slice_bitcast_fusion.4), channel_id=1, source_target_pairs={{0,1},{1,0},{2,3},{3,2},{4,5},{5,4},{6,7},{7,6},{8,9},{9,8},{10,11... | collective-permute-start | bytes 196616 | tf_op jit(solution)/shard_map/ppermute | solution.py:276
  99.3 43.9 %collective-permute-start.11 = (bf16[16,2,16,1024]{3,2,1,0:T(8,128)(2,1)}, bf16[16,2,16,1024]{3,2,1,0:T(8,128)(2,1)}, u32[]{:S(2)}, u32[]{:S(2)}) collective-permute-start(bf16[16,2,16,1024]{3,2,1,0:T(8,128)(2,1)} %bitcast.20.outer), channel_id=1, source_target_pairs={{0,1},{1,0},{2,3},{3,2},{4,5},{5,4},{6,7},{7,6},{8,9},{9,8},{10,11... | collective-permute-start | bytes 3145736 | tf_op jit(solution)/shard_map/ppermute | solution.py:276
  100.2 12.9 %copy-start.6 = (bf16[64,1024]{1,0:T(8,128)(2,1)}, bf16[64,1024]{1,0:T(8,128)(2,1)S(1)}, u32[]{:S(2)}) copy-start(bf16[64,1024]{1,0:T(8,128)(2,1)S(1)} %pad_maximum_fusion.3.inner) | copy-start | bytes 393220
  104.8 38.5 %collective-permute-start.10 = (bf16[2,128,1024]{2,1,0:T(8,128)(2,1)}, bf16[2,128,1024]{2,1,0:T(8,128)(2,1)}, u32[]{:S(2)}, u32[]{:S(2)}) collective-permute-start(bf16[2,128,1024]{2,1,0:T(8,128)(2,1)} %get-tuple-element.32), channel_id=1, source_target_pairs={{0,224},{32,0},{64,32},{96,64},{128,96},{160,128},{192,160},{224,1... | collective-permute-start | bytes 1572872 | tf_op jit(solution)/shard_map/ppermute | solution.py:279
  107.7 35.5 %collective-permute-start.6 = (bf16[2,128,1024]{2,1,0:T(8,128)(2,1)}, bf16[2,128,1024]{2,1,0:T(8,128)(2,1)}, u32[]{:S(2)}, u32[]{:S(2)}) collective-permute-start(bf16[2,128,1024]{2,1,0:T(8,128)(2,1)} %get-tuple-element.33), channel_id=1, source_target_pairs={{0,32},{32,64},{64,96},{96,128},{128,160},{160,192},{192,224},{224... | collective-permute-start | bytes 1572872 | tf_op jit(solution)/shard_map/ppermute | solution.py:279
  143.3 1.0 copy-start.23
  148.0 0.7 copy-start.26
  148.7 14.3 %collective-permute-start.16 = (bf16[2,128,1024]{2,1,0:T(8,128)(2,1)S(1)}, bf16[2,128,1024]{2,1,0:T(8,128)(2,1)S(1)}, u32[]{:S(2)}, u32[]{:S(2)}) collective-permute-start(bf16[2,128,1024]{2,1,0:T(8,128)(2,1)S(1)} %get-tuple-element.27.refs_4_), channel_id=1, source_target_pairs={{0,32},{32,64},{64,96},{96,128},{128,160},{160,192},{192,224},{224... | collective-permute-start | bytes 1572872 | tf_op jit(solution)/shard_map/ppermute | solution.py:279
  149.3 14.6 %collective-permute-start.14 = (bf16[2,128,1024]{2,1,0:T(8,128)(2,1)S(1)}, bf16[2,128,1024]{2,1,0:T(8,128)(2,1)}, u32[]{:S(2)}, u32[]{:S(2)}) collective-permute-start(bf16[2,128,1024]{2,1,0:T(8,128)(2,1)S(1)} %get-tuple-element.27.refs_4_), channel_id=1, source_target_pairs={{0,224},{32,0},{64,32},{96,64},{128,96},{160,128},{192,160},{224,1... | collective-permute-start | bytes 1572872 | tf_op jit(solution)/shard_map/ppermute | solution.py:279
  152.0 0.8 copy-start.9
  163.1 16.2 %collective-permute-start.17 = (bf16[2,128,1024]{2,1,0:T(8,128)(2,1)S(1)}, bf16[2,128,1024]{2,1,0:T(8,128)(2,1)}, u32[]{:S(2)}, u32[]{:S(2)}) collective-permute-start(bf16[2,128,1024]{2,1,0:T(8,128)(2,1)S(1)} %collective-permute-done.16.refs_3_), channel_id=1, source_target_pairs={{0,32},{32,64},{64,96},{96,128},{128,160},{160,192},{192,224},{224... | collective-permute-start | bytes 1572872 | tf_op jit(solution)/shard_map/ppermute | solution.py:279
  163.1 0.8 copy-start.12
  163.9 21.8 %collective-permute-start.15 = (bf16[2,128,1024]{2,1,0:T(8,128)(2,1)}, bf16[2,128,1024]{2,1,0:T(8,128)(2,1)}, u32[]{:S(2)}, u32[]{:S(2)}) collective-permute-start(bf16[2,128,1024]{2,1,0:T(8,128)(2,1)} %collective-permute-done.14.refs_2_), channel_id=1, source_target_pairs={{0,224},{32,0},{64,32},{96,64},{128,96},{160,128},{192,160},{224,1... | collective-permute-start | bytes 1572872 | tf_op jit(solution)/shard_map/ppermute | solution.py:279
  167.8 11.5 %all-to-all-start.5 = ((bf16[16,32,128]{2,1,0:T(8,128)(2,1)}), bf16[16,32,128]{2,1,0:T(8,128)(2,1)S(1)}, u32[]{:S(2)}, u32[]{:S(2)}) async-start(bf16[16,32,128]{2,1,0:T(8,128)(2,1)} %broadcast_in_dim.63), calls=%async_computation.5 | async-start | bytes 262144 | tf_op jit(solution)/shard_map/all_to_all | solution.py:23
  179.2 33.7 %collective-permute-start.18 = (bf16[2,128,1024]{2,1,0:T(8,128)(2,1)}, bf16[2,128,1024]{2,1,0:T(8,128)(2,1)S(1)}, u32[]{:S(2)}, u32[]{:S(2)}) collective-permute-start(bf16[2,128,1024]{2,1,0:T(8,128)(2,1)} %collective-permute-done.17.refs_1_), channel_id=1, source_target_pairs={{0,32},{32,64},{64,96},{96,128},{128,160},{160,192},{192,224},{224... | collective-permute-start | bytes 1572872 | tf_op jit(solution)/shard_map/ppermute | solution.py:279
  181.3 13.5 %all-to-all-start.6 = ((bf16[8,64,128]{2,1,0:T(8,128)(2,1)}), bf16[8,64,128]{2,1,0:T(8,128)(2,1)S(1)}, u32[]{:S(2)}, u32[]{:S(2)}) async-start(bf16[8,64,128]{2,1,0:T(8,128)(2,1)} %broadcast_in_dim.64), calls=%async_computation.6 | async-start | bytes 262144 | tf_op jit(solution)/shard_map/all_to_all | solution.py:23
  185.8 28.5 %collective-permute-start.20 = (bf16[2,128,1024]{2,1,0:T(8,128)(2,1)}, bf16[2,128,1024]{2,1,0:T(8,128)(2,1)}, u32[]{:S(2)}, u32[]{:S(2)}) collective-permute-start(bf16[2,128,1024]{2,1,0:T(8,128)(2,1)} %collective-permute-done.15.refs_0_), channel_id=1, source_target_pairs={{0,224},{32,0},{64,32},{96,64},{128,96},{160,128},{192,160},{224,1... | collective-permute-start | bytes 1572872 | tf_op jit(solution)/shard_map/ppermute | solution.py:279
  194.8 2.2 copy-start.3
  197.0 0.9 copy-start.7
  197.9 1.0 copy-start.10
  199.0 1.0 copy-start.13
  205.2 1.1 copy-start.5
  206.3 30.2 %all-to-all-start.7 = ((bf16[16,40,1024]{2,1,0:T(8,128)(2,1)}), bf16[16,40,1024]{2,1,0:T(8,128)(2,1)}, u32[]{:S(2)}, u32[]{:S(2)}) async-start(bf16[16,40,1024]{2,1,0:T(8,128)(2,1)} %copy-done.5), calls=%async_computation.7 | async-start | bytes 2621440 | tf_op jit(solution)/shard_map/all_to_all | solution.py:385
  213.7 10.5 %collective-permute-start.19 = (bf16[128,1024]{1,0:T(8,128)(2,1)}, bf16[128,1024]{1,0:T(8,128)(2,1)}, u32[]{:S(2)}, u32[]{:S(2)}) collective-permute-start(bf16[128,1024]{1,0:T(8,128)(2,1)} %slice_bitcast_fusion.1), channel_id=1, source_target_pairs={{0,32},{32,64},{64,96},{96,128},{128,160},{160,192},{192,224},{224... | collective-permute-start | bytes 786440 | tf_op jit(solution)/shard_map/ppermute | solution.py:279
  215.9 8.2 %collective-permute-start.21 = (bf16[128,1024]{1,0:T(8,128)(2,1)}, bf16[128,1024]{1,0:T(8,128)(2,1)}, u32[]{:S(2)}, u32[]{:S(2)}) collective-permute-start(bf16[128,1024]{1,0:T(8,128)(2,1)} %slice_bitcast_fusion), channel_id=1, source_target_pairs={{0,224},{32,0},{64,32},{96,64},{128,96},{160,128},{192,160},{224,1... | collective-permute-start | bytes 786440 | tf_op jit(solution)/shard_map/ppermute | solution.py:279
  220.2 6.9 %collective-permute-start.13 = (bf16[16,8,512]{2,1,0:T(8,128)(2,1)}, bf16[16,8,512]{2,1,0:T(8,128)(2,1)}, u32[]{:S(2)}, u32[]{:S(2)}) collective-permute-start(bf16[16,8,512]{2,1,0:T(8,128)(2,1)} %dynamic-slice_bitcast_fusion), channel_id=1, source_target_pairs={{0,1},{1,0},{2,3},{3,2},{4,5},{5,4},{6,7},{7,6},{8,9},{9,8},{10,11... | collective-permute-start | bytes 393224 | tf_op jit(solution)/shard_map/ppermute | solution.py:276
  220.2 1.0 copy-start.11
  221.2 1.0 copy-start.14
  222.3 4.8 %copy-start.27 = (bf16[128,1024]{1,0:T(8,128)(2,1)S(1)}, bf16[128,1024]{1,0:T(8,128)(2,1)}, u32[]{:S(2)}) copy-start(bf16[128,1024]{1,0:T(8,128)(2,1)} %copy-done.26) | copy-start | bytes 786436
  224.2 7.5 %copy-start.4 = (bf16[2,1024,1024]{2,1,0:T(8,128)(2,1)S(1)}, bf16[2,1024,1024]{2,1,0:T(8,128)(2,1)}, u32[]{:S(2)}) copy-start(bf16[2,1024,1024]{2,1,0:T(8,128)(2,1)} %copy-done.1) | copy-start | bytes 12582916
  226.6 4.9 %copy-start.24 = (f32[2,32,1024]{2,1,0:T(8,128)}, f32[2,32,1024]{2,1,0:T(8,128)S(1)}, u32[]{:S(2)}) copy-start(f32[2,32,1024]{2,1,0:T(8,128)S(1)} %get-tuple-element.28) | copy-start | bytes 786436
  226.6 5.1 %copy-start.8 = (bf16[64,1024]{1,0:T(8,128)(2,1)S(1)}, bf16[64,1024]{1,0:T(8,128)(2,1)}, u32[]{:S(2)}) copy-start(bf16[64,1024]{1,0:T(8,128)(2,1)} %copy-done.6) | copy-start | bytes 393220
  226.6 17.2 %collective-permute-start.23 = (bf16[2,32,1024]{2,1,0:T(8,128)(2,1)}, bf16[2,32,1024]{2,1,0:T(8,128)(2,1)}, u32[]{:S(2)}, u32[]{:S(2)}) collective-permute-start(bf16[2,32,1024]{2,1,0:T(8,128)(2,1)} %get-tuple-element.29), channel_id=1, source_target_pairs={{0,1},{1,0},{2,3},{3,2},{4,5},{5,4},{6,7},{7,6},{8,9},{9,8},{10,11... | collective-permute-start | bytes 393224 | tf_op jit(solution)/shard_map/ppermute | solution.py:276
  230.7 0.7 copy-start.19
  231.5 24.6 %collective-permute-start.22 = (f32[32,1024]{1,0:T(8,128)S(1)}, f32[32,1024]{1,0:T(8,128)S(1)}, u32[]{:S(2)}, u32[]{:S(2)}) collective-permute-start(f32[32,1024]{1,0:T(8,128)S(1)} %slice.60), channel_id=1, source_target_pairs={{0,1},{1,0},{2,3},{3,2},{4,5},{5,4},{6,7},{7,6},{8,9},{9,8},{10,11... | collective-permute-start | bytes 393224 | tf_op jit(solution)/shard_map/ppermute | solution.py:276
  231.7 12.1 %copy-start.25 = (f32[2,32,1024]{2,1,0:T(8,128)S(1)}, f32[2,32,1024]{2,1,0:T(8,128)}, u32[]{:S(2)}) copy-start(f32[2,32,1024]{2,1,0:T(8,128)} %copy-done.24) | copy-start | bytes 786436
  236.4 19.6 %copy-start.20 = (f32[64,1024]{1,0:T(8,128)S(1)}, f32[64,1024]{1,0:T(8,128)}, u32[]{:S(2)}) copy-start(f32[64,1024]{1,0:T(8,128)} %copy-done.19) | copy-start | bytes 786436
  236.4 23.7 %all-to-all-start.8 = ((bf16[16,24,1024]{2,1,0:T(8,128)(2,1)}), bf16[16,24,1024]{2,1,0:T(8,128)(2,1)S(1)}, u32[]{:S(2)}, u32[]{:S(2)}) async-start(bf16[16,24,1024]{2,1,0:T(8,128)(2,1)} %shard_map.117), calls=%async_computation.8 | async-start | bytes 1572864 | tf_op jit(solution)/shard_map/all_to_all | solution.py:385
  244.8 14.1 %collective-permute-start.24 = (bf16[2,16,1024]{2,1,0:T(8,128)(2,1)S(1)}, bf16[2,16,1024]{2,1,0:T(8,128)(2,1)S(1)}, u32[]{:S(2)}, u32[]{:S(2)}) collective-permute-start(bf16[2,16,1024]{2,1,0:T(8,128)(2,1)S(1)} %get-tuple-element.42), channel_id=1, source_target_pairs={{0,0},{2,2},{4,32},{6,34},{8,64},{10,66},{12,96},{14,98},{16,128},... | collective-permute-start | bytes 196616 | tf_op jit(solution)/shard_map/ppermute | solution.py:425
  246.8 13.3 %collective-permute-start.25 = (bf16[2,16,1024]{2,1,0:T(8,128)(2,1)S(1)}, bf16[2,16,1024]{2,1,0:T(8,128)(2,1)S(1)}, u32[]{:S(2)}, u32[]{:S(2)}) collective-permute-start(bf16[2,16,1024]{2,1,0:T(8,128)(2,1)S(1)} %get-tuple-element.43), channel_id=1, source_target_pairs={{0,2},{2,0},{4,34},{6,32},{8,66},{10,64},{12,98},{14,96},{16,130},... | collective-permute-start | bytes 196616 | tf_op jit(solution)/shard_map/ppermute | solution.py:426
  262.4 18.6 %all-to-all-start.9 = ((bf16[8,8,1024]{2,1,0:T(8,128)(2,1)}), bf16[8,8,1024]{2,1,0:T(8,128)(2,1)S(1)}, u32[]{:S(2)}, u32[]{:S(2)}) async-start(bf16[8,8,1024]{2,1,0:T(8,128)(2,1)} %shard_map.118), calls=%async_computation.9 | async-start | bytes 262144 | tf_op jit(solution)/shard_map/all_to_all | solution.py:390

commit v4 on v3

--- a/solution.py
+++ b/solution.py
@@ -50,11 +50,15 @@
 
 
 def rows_at(tokens, place, own_rows):
-    start = place * own_rows
-    if not isinstance(place, int):
-        start = pl.multiple_of(start, own_rows)
-    block = tokens[:, pl.ds(start, own_rows), :]
-    return block.reshape(block.shape[0] * own_rows, block.shape[2])
+    parts = (tokens.shape[1] - 8) // (8 * own_rows)
+    blocks = []
+    for part in range(parts):
+        start = (place * parts + part) * own_rows
+        if not isinstance(place, int):
+            start = pl.multiple_of(start, own_rows)
+        block = tokens[:, pl.ds(start, own_rows), :]
+        blocks.append(block.reshape(block.shape[0] * own_rows, block.shape[2]))
+    return jnp.concatenate(blocks, axis=1)
 
 
 def over_columns(width, body):
@@ -293,9 +297,11 @@
     lane = lax.broadcasted_iota(jnp.int32, (count, 128), 1)
     row = lax.broadcasted_iota(jnp.int32, (count, 128), 0)
     id_lanes = jnp.sum(jnp.where(lane == row, id_columns.astype(f32), 0.0), axis=0, keepdims=True)
-    id_block = jnp.broadcast_to(jnp.pad(id_lanes.astype(bf16), ((0, 0), (0, depth - 128))), (8, depth))
-    gathered = spread(jnp.concatenate([sliced[:, :depth], id_block], axis=0), CHIPS, chips)
-    row_ids = gathered[:, count, :count].astype(f32).astype(jnp.int32)
+    id_block = jnp.broadcast_to(id_lanes.astype(bf16), (8, 128))
+    tiles = sliced[:, :depth].reshape(groups, own_rows, depth // 128, 128).transpose(0, 2, 1, 3)
+    tiles = tiles.reshape(count * (depth // 128), 128)
+    gathered = spread(jnp.concatenate([tiles, id_block], axis=0), CHIPS, chips)
+    row_ids = gathered[:, count * (depth // 128), :count].astype(f32).astype(jnp.int32)
     row_ids = row_ids.reshape(chips, groups, own_rows).transpose(1, 0, 2).reshape(groups, rows)
 
     info = jnp.concatenate([jnp.stack([2 * u + c, 2 * u + 1 - c, c, z]), group_at]).astype(jnp.int32)

time: 286 us -> 275 us (0.962)
  waiting for transfers between devices: 72.8 us -> 67.1 us
  local copies, waits for them, and re-layouts: 33.4 us -> 29.6 us
    ppermute x16, waiting for transfers between devices: 17.5 us -> 13.9 us  [ring(): return lax.ppermute(value, GROUP, pairs)]
    unnamed x62 -> x52, local copies, waits for them, and re-layouts: 20.8 us -> 19.9 us
  transfers between devices with their start and end apart: 34 -> 34, of which waited for: 12 -> 12; matrix products, arithmetic and copies ran while one was open for 9% -> 8% of each run, Pallas kernels for 9% -> 9%
where the time goes in v4:
time: 275 us; the launch traced here: 272 us
  starting transfers between devices  97.5 us (35%)
  waiting for transfers between devices  67.1 us (24%)
  Pallas kernels  32.6 us (12%)
  local copies, waits for them, and re-layouts  29.6 us (11%)
  blocking collectives  27.5 us (10%)
  other arithmetic  16.1 us (6%)
    pallas_call x11, Pallas kernels, call(): pl.pallas_call(kernel, out_shape=[jax.ShapeDtypeStruct(shape, dtype) for...  32.6 us
    ppermute x16, starting transfers between devices, ring(): return lax.ppermute(value, GROUP, pairs)  27.4 us
    all_to_all x3, waiting for transfers between devices, spread(): return lax.all_to_all(copies, axes, split_axis=0, concat_axis=0, tiled=True)  22 us
    unnamed x52, local copies, waits for them, and re-layouts  19.9 us
    all_to_all x3, starting transfers between devices, spread(): return lax.all_to_all(copies, axes, split_axis=0, concat_axis=0, tiled=True)  18 us
    all_to_all x1, blocking collectives, spread(): return lax.all_to_all(copies, axes, split_axis=0, concat_axis=0, tiled=True)  14.2 us
    all_to_all x2, starting transfers between devices, to_owners(): return lax.all_to_all(part, CHIPS, split_axis=0, concat_axis=0, tiled=True)  14.1 us
    ppermute x16, waiting for transfers between devices, ring(): return lax.ppermute(value, GROUP, pairs)  13.9 us
  transfers between devices with their start and end apart: 34, of which 12 were waited for; matrix products, arithmetic and copies ran while one was open for 8% of the time, Pallas kernels for 9%

profile of v4, /device:TPU:16, one launch (start us, length us, event | category | flops | bytes accessed | tf_op | source)
XLA Modules:
  0.0 271.5 jit_solution(16806413425861937258)
XLA Ops:
  1.4 1.6 pad_maximum_fusion.1
  3.0 8.5 %all-to-all-start = ((bf16[8,8,1152]{2,0,1:T(8,128)(2,1)}), bf16[8,8,1152]{2,0,1:T(8,128)(2,1)S(1)}, u32[]{:S(2)}, u32[]{:S(2)}) async-start(bf16[8,8,1152]{2,0,1:T(8,128)(2,1)} %pad_maximum_fusion.1), calls=%async_computation | async-start | bytes 294912 | tf_op jit(solution)/shard_map/all_to_all | solution.py:290
  12.2 8.7 %all-to-all-done = bf16[8,8,1152]{2,0,1:T(8,128)(2,1)S(1)} async-done(((bf16[8,8,1152]{2,0,1:T(8,128)(2,1)}), bf16[8,8,1152]{2,0,1:T(8,128)(2,1)S(1)}, u32[]{:S(2)}, u32[]{:S(2)}) %all-to-all-start) | async-done | bytes 147488 | tf_op jit(solution)/shard_map/all_to_all | solution.py:290
  21.5 1.7 broadcast_in_dim.28
  23.2 7.4 %all-to-all-start.1 = ((bf16[16,520,128]{2,1,0:T(8,128)(2,1)}), bf16[16,520,128]{2,1,0:T(8,128)(2,1)S(1)}, u32[]{:S(2)}, u32[]{:S(2)}) async-start(bf16[16,520,128]{2,1,0:T(8,128)(2,1)} %broadcast_in_dim.28), calls=%async_computation.1 | async-start | bytes 4259840 | tf_op jit(solution)/shard_map/all_to_all | solution.py:23
  31.4 3.8 %collective-permute-done.2.other_hidden = bf16[16,8,512]{2,1,0:T(8,128)(2,1)S(1)} collective-permute-done((bf16[16,8,512]{2,1,0:T(8,128)(2,1)S(1)}, bf16[16,8,512]{2,1,0:T(8,128)(2,1)S(1)}, u32[]{:S(2)}, u32[]{:S(2)}) %collective-permute-start.2) | collective-permute-done | bytes 131104 | tf_op jit(solution)/shard_map/ppermute | solution.py:280
  35.2 1.2 copy-done.12
  36.4 1.2 copy-done.13
  37.6 1.9 shard_map.111
  39.6 2.0 copy-done.1
  42.2 14.7 %all-to-all-done.1.tokens = bf16[16,520,128]{2,1,0:T(8,128)(2,1)S(1)} async-done(((bf16[16,520,128]{2,1,0:T(8,128)(2,1)}), bf16[16,520,128]{2,1,0:T(8,128)(2,1)S(1)}, u32[]{:S(2)}, u32[]{:S(2)}) %all-to-all-start.1) | async-done | bytes 2129952 | tf_op jit(solution)/shard_map/all_to_all | solution.py:23
  57.0 2.2 copy-done.2
  59.1 1.5 shard_map.113
  60.6 1.3 collective-permute-start.3
  61.9 2.0 collective-permute-start.7
  63.9 4.7 %shard_map.112 = (bf16[2,2,128,1024]{3,2,1,0:T(8,128)(2,1)S(1)}, bf16[2,2,128,1024]{3,2,1,0:T(8,128)(2,1)S(1)}, bf16[2,2,128,1024]{3,2,1,0:T(8,128)(2,1)S(1)}, bf16[1,2,128,1024]{3,2,1,0:T(8,128)(2,1)S(1)}) custom-call(s32[12]{0:T(128)S(1)} %concatenate.29.info, bf16[16,520,128]{2,1,0:T(8,128)(2,1)S(1)} %all-to-all-done.1.tokens, ...), custom_call_target="tpu_custom_call" | custom-call | tf_op jit(solution)/shard_map/pallas_call | solution.py:42
  68.7 1.2 fusion
  69.9 3.2 %collective-permute-start.8 = (bf16[2,128,1024]{2,1,0:T(8,128)(2,1)}, bf16[2,128,1024]{2,1,0:T(8,128)(2,1)}, u32[]{:S(2)}, u32[]{:S(2)}) collective-permute-start(bf16[2,128,1024]{2,1,0:T(8,128)(2,1)} %get-tuple-element.36), channel_id=1, source_target_pairs={{0,224},{32,0},{64,32},{96,64},{128,96},{160,128},{192,160},{224,1... | collective-permute-start | bytes 1572872 | tf_op jit(solution)/shard_map/ppermute | solution.py:283
  73.7 1.6 copy.29
  75.4 7.4 %all-to-all-start.2 = ((bf16[16,32,1024]{2,1,0:T(8,128)(2,1)}), bf16[16,32,1024]{2,1,0:T(8,128)(2,1)}, u32[]{:S(2)}, u32[]{:S(2)}) async-start(bf16[16,32,1024]{2,1,0:T(8,128)(2,1)} %bitcast.89), calls=%async_computation.2 | async-start | bytes 2097152 | tf_op jit(solution)/shard_map/all_to_all | solution.py:320
  82.7 2.9 %fusion.1 = (bf16[2,128,1024]{2,1,0:T(8,128)(2,1)}, bf16[2,128,1024]{2,1,0:T(8,128)(2,1)}) fusion(bf16[2,128,1024]{2,1,0:T(8,128)(2,1)} %collective-permute-done.8, bf16[2,2,128,1024]{3,2,1,0:T(8,128)(2,1)} %copy-done.15, bf16[2,128,1024]{2,1,0:T(8,128)(2,1)} %collective-permute-done.4), kind=kLoop, calls=%fused_computation.4 | loop fusion | flops 2097152 | bytes 3145728 | tf_op jit(solution)/shard_map/convert_element_type | solution.py:340
  85.7 3.2 %collective-permute-start.9 = (bf16[2,128,1024]{2,1,0:T(8,128)(2,1)}, bf16[2,128,1024]{2,1,0:T(8,128)(2,1)}, u32[]{:S(2)}, u32[]{:S(2)}) collective-permute-start(bf16[2,128,1024]{2,1,0:T(8,128)(2,1)} %get-tuple-element.34), channel_id=1, source_target_pairs={{0,224},{32,0},{64,32},{96,64},{128,96},{160,128},{192,160},{224,1... | collective-permute-start | bytes 1572872 | tf_op jit(solution)/shard_map/ppermute | solution.py:283
  89.0 7.0 %all-to-all-done.2 = bf16[16,32,1024]{2,1,0:T(8,128)(2,1)} async-done(((bf16[16,32,1024]{2,1,0:T(8,128)(2,1)}), bf16[16,32,1024]{2,1,0:T(8,128)(2,1)}, u32[]{:S(2)}, u32[]{:S(2)}) %all-to-all-start.2) | async-done | bytes 1048608 | tf_op jit(solution)/shard_map/all_to_all | solution.py:320
  96.0 2.5 collective-permute-done.5
  98.5 3.0 %fusion.2 = (bf16[2,128,1024]{2,1,0:T(8,128)(2,1)}, bf16[2,128,1024]{2,1,0:T(8,128)(2,1)}) fusion(bf16[2,128,1024]{2,1,0:T(8,128)(2,1)} %collective-permute-done.9, bf16[2,2,128,1024]{3,2,1,0:T(8,128)(2,1)} %copy-done.14, bf16[2,128,1024]{2,1,0:T(8,128)(2,1)} %collective-permute-done.5), kind=kLoop, calls=%fused_computation.6 | loop fusion | flops 2097152 | bytes 3145728 | tf_op jit(solution)/shard_map/convert_element_type | solution.py:340
  101.5 3.0 %collective-permute-start.10 = (bf16[2,128,1024]{2,1,0:T(8,128)(2,1)}, bf16[2,128,1024]{2,1,0:T(8,128)(2,1)}, u32[]{:S(2)}, u32[]{:S(2)}) collective-permute-start(bf16[2,128,1024]{2,1,0:T(8,128)(2,1)} %get-tuple-element.32), channel_id=1, source_target_pairs={{0,224},{32,0},{64,32},{96,64},{128,96},{160,128},{192,160},{224,1... | collective-permute-start | bytes 1572872 | tf_op jit(solution)/shard_map/ppermute | solution.py:283
  104.7 2.3 shard_map.114
  107.1 13.4 %all_to_all.69 = f32[8,32,128]{2,1,0:T(8,128)S(1)} all-to-all(f32[8,32,128]{2,1,0:T(8,128)S(1)} %shard_map.114), channel_id=1, replica_groups=mesh['z'=8,'y'=4,'x'=4,'c'=2] {'z'}, dimensions={0} | all-to-all | bytes 262144 | tf_op jit(solution)/shard_map/all_to_all | solution.py:347
  120.5 14.2 %all_to_all.70 = bf16[16,32,128]{2,1,0:T(8,128)(2,1)} all-to-all(bf16[16,32,128]{2,1,0:T(8,128)(2,1)S(1)} %broadcast_in_dim.59), channel_id=1, replica_groups=mesh['z'=8,'y'=4,'x'=4,'c'=2] {'y','x'}, dimensions={0} | all-to-all | bytes 262144 | tf_op jit(solution)/shard_map/all_to_all | solution.py:23
  136.6 3.8 %shard_map.115 = (bf16[128,1024]{1,0:T(8,128)(2,1)S(1)}, bf16[2,128,1024]{2,1,0:T(8,128)(2,1)S(1)}, bf16[32,128]{1,0:T(8,128)(2,1)S(1)}) custom-call(s32[12]{0:T(128)S(1)} %concatenate.29.info, bf16[1,2,128,1024]{3,2,1,0:T(8,128)(2,1)S(1)} %get-tuple-element.18.product, bf16[2,128,1024]{2,1,0:T(8,128)(2,1)} %collective-permute-done.6.from_below, ...), custom_call_target="tpu_custom_call" | custom-call | tf_op jit(solution)/shard_map/pallas_call | solution.py:42
  141.1 1.1 collective-permute-start.16
  142.2 2.1 collective-permute-start.14
  145.1 8.8 %collective-permute-done.16.refs_3_ = bf16[2,128,1024]{2,1,0:T(8,128)(2,1)S(1)} collective-permute-done((bf16[2,128,1024]{2,1,0:T(8,128)(2,1)S(1)}, bf16[2,128,1024]{2,1,0:T(8,128)(2,1)S(1)}, u32[]{:S(2)}, u32[]{:S(2)}) %collective-permute-start.16) | collective-permute-done | bytes 524320 | tf_op jit(solution)/shard_map/ppermute | solution.py:283
  155.4 2.6 collective-permute-start.15
  158.6 6.5 %all-to-all-start.5 = ((bf16[16,32,128]{2,1,0:T(8,128)(2,1)}), bf16[16,32,128]{2,1,0:T(8,128)(2,1)}, u32[]{:S(2)}, u32[]{:S(2)}) async-start(bf16[16,32,128]{2,1,0:T(8,128)(2,1)} %broadcast_in_dim.60), calls=%async_computation.5 | async-start | bytes 262144 | tf_op jit(solution)/shard_map/all_to_all | solution.py:23
  165.1 2.6 collective-permute-done.17.refs_1_
  167.6 1.7 collective-permute-start.18
  169.4 1.4 all-to-all-done.5
  172.4 4.1 %all-to-all-start.6 = ((bf16[8,64,128]{2,1,0:T(8,128)(2,1)}), bf16[8,64,128]{2,1,0:T(8,128)(2,1)S(1)}, u32[]{:S(2)}, u32[]{:S(2)}) async-start(bf16[8,64,128]{2,1,0:T(8,128)(2,1)} %broadcast_in_dim.61), calls=%async_computation.6 | async-start | bytes 262144 | tf_op jit(solution)/shard_map/all_to_all | solution.py:23
  176.5 3.2 %collective-permute-start.20 = (bf16[2,128,1024]{2,1,0:T(8,128)(2,1)}, bf16[2,128,1024]{2,1,0:T(8,128)(2,1)}, u32[]{:S(2)}, u32[]{:S(2)}) collective-permute-start(bf16[2,128,1024]{2,1,0:T(8,128)(2,1)} %collective-permute-done.15.refs_0_), channel_id=1, source_target_pairs={{0,224},{32,0},{64,32},{96,64},{128,96},{160,128},{192,160},{224,1... | collective-permute-start | bytes 1572872 | tf_op jit(solution)/shard_map/ppermute | solution.py:283
  179.8 5.8 %all-to-all-done.6.lows = bf16[8,64,128]{2,1,0:T(8,128)(2,1)S(1)} async-done(((bf16[8,64,128]{2,1,0:T(8,128)(2,1)}), bf16[8,64,128]{2,1,0:T(8,128)(2,1)S(1)}, u32[]{:S(2)}, u32[]{:S(2)}) %all-to-all-start.6) | async-done | bytes 131104 | tf_op jit(solution)/shard_map/all_to_all | solution.py:23
  185.6 2.2 copy-done.3
  187.8 1.0 copy-done.7
  188.8 1.0 copy-done.10
  189.9 5.2 %shard_map.116 = bf16[16,40,1024]{2,1,0:T(8,128)(2,1)S(1)} custom-call(s32[12]{0:T(128)S(1)} %concatenate.29.info, bf16[2,1024,1024]{2,1,0:T(8,128)(2,1)S(1)} %copy-done.3, bf16[64,1024]{1,0:T(8,128)(2,1)S(1)} %pad_maximum_fusion.3.inner, bf16[8,64,128]{2,1,0:T(8,128)(2,1)S(1)} %all-to-all-done.6.lows, s32[8,128]{1,0:T(8,128)S(1)} %reshape.128.ids, ...), custom_call_target="tpu_custom_call" | custom-call | tf_op jit(solution)/shard_map/pallas_call | solution.py:42
  195.1 1.0 copy-done.5
  196.1 6.7 %all-to-all-start.7 = ((bf16[16,40,1024]{2,1,0:T(8,128)(2,1)}), bf16[16,40,1024]{2,1,0:T(8,128)(2,1)}, u32[]{:S(2)}, u32[]{:S(2)}) async-start(bf16[16,40,1024]{2,1,0:T(8,128)(2,1)} %copy-done.5), calls=%async_computation.7 | async-start | bytes 2621440 | tf_op jit(solution)/shard_map/all_to_all | solution.py:391
  204.1 1.7 slice_bitcast_fusion
  205.8 2.7 collective-permute-start.21
  208.5 1.6 dynamic-slice_bitcast_fusion
  210.0 1.0 copy-done.8
  211.1 1.0 copy-done.11
  212.1 1.9 shard_map.120.refs_4_
  214.1 2.4 shard_map.121
  218.6 2.1 shard_map.119
  221.6 4.7 %shard_map.117 = bf16[16,24,1024]{2,1,0:T(8,128)(2,1)} custom-call(s32[12]{0:T(128)S(1)} %concatenate.29.info, bf16[2,1024,1024]{2,1,0:T(8,128)(2,1)S(1)} %copy-done.4, bf16[64,1024]{1,0:T(8,128)(2,1)S(1)} %pad_maximum_fusion.3.inner, bf16[8,64,128]{2,1,0:T(8,128)(2,1)S(1)} %all-to-all-done.6.lows, s32[8,128]{1,0:T(8,128)S(1)} %reshape.128.ids, ...), custom_call_target="tpu_custom_call" | custom-call | tf_op jit(solution)/shard_map/pallas_call | solution.py:42
  226.3 7.4 %all-to-all-start.8 = ((bf16[16,24,1024]{2,1,0:T(8,128)(2,1)}), bf16[16,24,1024]{2,1,0:T(8,128)(2,1)S(1)}, u32[]{:S(2)}, u32[]{:S(2)}) async-start(bf16[16,24,1024]{2,1,0:T(8,128)(2,1)} %shard_map.117), calls=%async_computation.8 | async-start | bytes 1572864 | tf_op jit(solution)/shard_map/all_to_all | solution.py:391
  234.7 2.0 collective-permute-start.24
  236.7 9.3 %collective-permute-start.25 = (bf16[2,16,1024]{2,1,0:T(8,128)(2,1)S(1)}, bf16[2,16,1024]{2,1,0:T(8,128)(2,1)S(1)}, u32[]{:S(2)}, u32[]{:S(2)}) collective-permute-start(bf16[2,16,1024]{2,1,0:T(8,128)(2,1)S(1)} %get-tuple-element.43), channel_id=1, source_target_pairs={{0,2},{2,0},{4,34},{6,32},{8,66},{10,64},{12,98},{14,96},{16,130},... | collective-permute-start | bytes 196616 | tf_op jit(solution)/shard_map/ppermute | solution.py:432
  246.7 2.1 collective-permute-done.24
  248.8 1.2 collective-permute-done.25
  250.0 2.3 shard_map.118
  252.2 9.5 %all-to-all-start.9 = ((bf16[8,8,1024]{2,1,0:T(8,128)(2,1)}), bf16[8,8,1024]{2,1,0:T(8,128)(2,1)S(1)}, u32[]{:S(2)}, u32[]{:S(2)}) async-start(bf16[8,8,1024]{2,1,0:T(8,128)(2,1)} %shard_map.118), calls=%async_computation.9 | async-start | bytes 262144 | tf_op jit(solution)/shard_map/all_to_all | solution.py:396
  262.5 8.4 %all-to-all-done.9 = bf16[8,8,1024]{2,1,0:T(8,128)(2,1)S(1)} async-done(((bf16[8,8,1024]{2,1,0:T(8,128)(2,1)}), bf16[8,8,1024]{2,1,0:T(8,128)(2,1)S(1)}, u32[]{:S(2)}, u32[]{:S(2)}) %all-to-all-start.9) | async-done | bytes 131104 | tf_op jit(solution)/shard_map/all_to_all | solution.py:396
  (110 shorter events, 19.3 us)
Async XLA Ops:
  0.6 88.3 %copy-start = (bf16[1,32,8192]{2,1,0:T(8,128)(2,1)S(1)}, bf16[1,32,8192]{2,1,0:T(8,128)(2,1)}, u32[]{:S(2)}) copy-start(bf16[1,32,8192]{2,1,0:T(8,128)(2,1)} %param.12) | copy-start | bytes 1572868
  3.0 17.9 %all-to-all-start = ((bf16[8,8,1152]{2,0,1:T(8,128)(2,1)}), bf16[8,8,1152]{2,0,1:T(8,128)(2,1)S(1)}, u32[]{:S(2)}, u32[]{:S(2)}) async-start(bf16[8,8,1152]{2,0,1:T(8,128)(2,1)} %pad_maximum_fusion.1), calls=%async_computation | async-start | bytes 294912 | tf_op jit(solution)/shard_map/all_to_all | solution.py:290
  23.2 7.9 %copy-start.18 = (bf16[256,512]{1,0:T(8,128)(2,1)S(1)}, bf16[256,512]{1,0:T(8,128)(2,1)}, u32[]{:S(2)}) copy-start(bf16[256,512]{1,0:T(8,128)(2,1)} %param.14) | copy-start | bytes 786436
  23.2 33.8 %all-to-all-start.1 = ((bf16[16,520,128]{2,1,0:T(8,128)(2,1)}), bf16[16,520,128]{2,1,0:T(8,128)(2,1)S(1)}, u32[]{:S(2)}, u32[]{:S(2)}) async-start(bf16[16,520,128]{2,1,0:T(8,128)(2,1)} %broadcast_in_dim.28), calls=%async_computation.1 | async-start | bytes 4259840 | tf_op jit(solution)/shard_map/all_to_all | solution.py:23
  30.6 4.6 %collective-permute-start = (bf16[1024,512]{1,0:T(8,128)(2,1)}, bf16[1024,512]{1,0:T(8,128)(2,1)}, u32[]{:S(2)}, u32[]{:S(2)}) collective-permute-start(bf16[1024,512]{1,0:T(8,128)(2,1)} %gate.1), channel_id=1, source_target_pairs={{0,1},{1,0},{2,3},{3,2},{4,5},{5,4},{6,7},{7,6},{8,9},{9,8},{10,11... | collective-permute-start | bytes 3145736 | tf_op jit(solution)/shard_map/ppermute | solution.py:280
  30.6 4.6 %collective-permute-start.1 = (bf16[1024,512]{1,0:T(8,128)(2,1)}, bf16[1024,512]{1,0:T(8,128)(2,1)}, u32[]{:S(2)}, u32[]{:S(2)}) collective-permute-start(bf16[1024,512]{1,0:T(8,128)(2,1)} %up.1), channel_id=1, source_target_pairs={{0,1},{1,0},{2,3},{3,2},{4,5},{5,4},{6,7},{7,6},{8,9},{9,8},{10,11... | collective-permute-start | bytes 3145736 | tf_op jit(solution)/shard_map/ppermute | solution.py:280
  31.1 4.0 %collective-permute-start.2 = (bf16[16,8,512]{2,1,0:T(8,128)(2,1)S(1)}, bf16[16,8,512]{2,1,0:T(8,128)(2,1)S(1)}, u32[]{:S(2)}, u32[]{:S(2)}) collective-permute-start(bf16[16,8,512]{2,1,0:T(8,128)(2,1)S(1)} %dynamic-slice_bitcast_fusion.1), channel_id=1, source_target_pairs={{0,1},{1,0},{2,3},{3,2},{4,5},{5,4},{6,7},{7,6},{8,9},{9,8},{10,11... | collective-permute-start | bytes 393224 | tf_op jit(solution)/shard_map/ppermute | solution.py:280
  35.2 1.2 copy-start.12
  36.4 1.2 copy-start.13
  39.5 2.0 copy-start.1
  41.5 0.7 copy-start.19
  57.0 2.2 copy-start.2
  60.6 8.0 %collective-permute-start.3 = (bf16[128,1024]{1,0:T(8,128)(2,1)S(1)}, bf16[128,1024]{1,0:T(8,128)(2,1)S(1)}, u32[]{:S(2)}, u32[]{:S(2)}) collective-permute-start(bf16[128,1024]{1,0:T(8,128)(2,1)S(1)} %get-tuple-element.22), channel_id=1, source_target_pairs={{0,32},{32,64},{64,96},{96,128},{128,160},{160,192},{192,224},{224... | collective-permute-start | bytes 786440 | tf_op jit(solution)/shard_map/ppermute | solution.py:283
  61.9 6.7 %collective-permute-start.7 = (bf16[128,1024]{1,0:T(8,128)(2,1)S(1)}, bf16[128,1024]{1,0:T(8,128)(2,1)S(1)}, u32[]{:S(2)}, u32[]{:S(2)}) collective-permute-start(bf16[128,1024]{1,0:T(8,128)(2,1)S(1)} %get-tuple-element.23), channel_id=1, source_target_pairs={{0,224},{32,0},{64,32},{96,64},{128,96},{160,128},{192,160},{224,1... | collective-permute-start | bytes 786440 | tf_op jit(solution)/shard_map/ppermute | solution.py:283
  68.6 5.1 %copy-start.14 = (bf16[2,2,128,1024]{3,2,1,0:T(8,128)(2,1)}, bf16[2,2,128,1024]{3,2,1,0:T(8,128)(2,1)S(1)}, u32[]{:S(2)}) copy-start(bf16[2,2,128,1024]{3,2,1,0:T(8,128)(2,1)S(1)} %get-tuple-element.19) | copy-start | bytes 3145732
  68.6 5.1 %copy-start.15 = (bf16[2,2,128,1024]{3,2,1,0:T(8,128)(2,1)}, bf16[2,2,128,1024]{3,2,1,0:T(8,128)(2,1)S(1)}, u32[]{:S(2)}) copy-start(bf16[2,2,128,1024]{3,2,1,0:T(8,128)(2,1)S(1)} %get-tuple-element.20) | copy-start | bytes 3145732
  68.6 4.5 %copy-start.24 = (bf16[1,2,16,16384]{3,2,1,0:T(8,128)(2,1)S(1)}, bf16[1,2,16,16384]{3,2,1,0:T(8,128)(2,1)}, u32[]{:S(2)}) copy-start(bf16[1,2,16,16384]{3,2,1,0:T(8,128)(2,1)} %param.13) | copy-start | bytes 3145732
  69.9 12.8 %collective-permute-start.4 = (bf16[2,128,1024]{2,1,0:T(8,128)(2,1)}, bf16[2,128,1024]{2,1,0:T(8,128)(2,1)}, u32[]{:S(2)}, u32[]{:S(2)}) collective-permute-start(bf16[2,128,1024]{2,1,0:T(8,128)(2,1)} %get-tuple-element.37), channel_id=1, source_target_pairs={{0,32},{32,64},{64,96},{96,128},{128,160},{160,192},{192,224},{224... | collective-permute-start | bytes 1572872 | tf_op jit(solution)/shard_map/ppermute | solution.py:283
  69.9 12.8 %collective-permute-start.8 = (bf16[2,128,1024]{2,1,0:T(8,128)(2,1)}, bf16[2,128,1024]{2,1,0:T(8,128)(2,1)}, u32[]{:S(2)}, u32[]{:S(2)}) collective-permute-start(bf16[2,128,1024]{2,1,0:T(8,128)(2,1)} %get-tuple-element.36), channel_id=1, source_target_pairs={{0,224},{32,0},{64,32},{96,64},{128,96},{160,128},{192,160},{224,1... | collective-permute-start | bytes 1572872 | tf_op jit(solution)/shard_map/ppermute | solution.py:283
  75.4 20.7 %all-to-all-start.2 = ((bf16[16,32,1024]{2,1,0:T(8,128)(2,1)}), bf16[16,32,1024]{2,1,0:T(8,128)(2,1)}, u32[]{:S(2)}, u32[]{:S(2)}) async-start(bf16[16,32,1024]{2,1,0:T(8,128)(2,1)} %bitcast.89), calls=%async_computation.2 | async-start | bytes 2097152 | tf_op jit(solution)/shard_map/all_to_all | solution.py:320
  85.7 12.8 %collective-permute-start.5 = (bf16[2,128,1024]{2,1,0:T(8,128)(2,1)}, bf16[2,128,1024]{2,1,0:T(8,128)(2,1)}, u32[]{:S(2)}, u32[]{:S(2)}) collective-permute-start(bf16[2,128,1024]{2,1,0:T(8,128)(2,1)} %get-tuple-element.35), channel_id=1, source_target_pairs={{0,32},{32,64},{64,96},{96,128},{128,160},{160,192},{192,224},{224... | collective-permute-start | bytes 1572872 | tf_op jit(solution)/shard_map/ppermute | solution.py:283
  85.7 12.8 %collective-permute-start.9 = (bf16[2,128,1024]{2,1,0:T(8,128)(2,1)}, bf16[2,128,1024]{2,1,0:T(8,128)(2,1)}, u32[]{:S(2)}, u32[]{:S(2)}) collective-permute-start(bf16[2,128,1024]{2,1,0:T(8,128)(2,1)} %get-tuple-element.34), channel_id=1, source_target_pairs={{0,224},{32,0},{64,32},{96,64},{128,96},{160,128},{192,160},{224,1... | collective-permute-start | bytes 1572872 | tf_op jit(solution)/shard_map/ppermute | solution.py:283
  88.9 7.1 %collective-permute-start.12 = (bf16[32,1024]{1,0:T(8,128)(2,1)S(1)}, bf16[32,1024]{1,0:T(8,128)(2,1)S(1)}, u32[]{:S(2)}, u32[]{:S(2)}) collective-permute-start(bf16[32,1024]{1,0:T(8,128)(2,1)S(1)} %dynamic-slice_bitcast_fusion.4), channel_id=1, source_target_pairs={{0,1},{1,0},{2,3},{3,2},{4,5},{5,4},{6,7},{7,6},{8,9},{9,8},{10,11... | collective-permute-start | bytes 196616 | tf_op jit(solution)/shard_map/ppermute | solution.py:280
  96.0 39.6 %collective-permute-start.11 = (bf16[16,2,16,1024]{3,2,1,0:T(8,128)(2,1)}, bf16[16,2,16,1024]{3,2,1,0:T(8,128)(2,1)}, u32[]{:S(2)}, u32[]{:S(2)}) collective-permute-start(bf16[16,2,16,1024]{3,2,1,0:T(8,128)(2,1)} %bitcast.22.outer), channel_id=1, source_target_pairs={{0,1},{1,0},{2,3},{3,2},{4,5},{5,4},{6,7},{7,6},{8,9},{9,8},{10,11... | collective-permute-start | bytes 3145736 | tf_op jit(solution)/shard_map/ppermute | solution.py:280
  101.5 34.1 %collective-permute-start.10 = (bf16[2,128,1024]{2,1,0:T(8,128)(2,1)}, bf16[2,128,1024]{2,1,0:T(8,128)(2,1)}, u32[]{:S(2)}, u32[]{:S(2)}) collective-permute-start(bf16[2,128,1024]{2,1,0:T(8,128)(2,1)} %get-tuple-element.32), channel_id=1, source_target_pairs={{0,224},{32,0},{64,32},{96,64},{128,96},{160,128},{192,160},{224,1... | collective-permute-start | bytes 1572872 | tf_op jit(solution)/shard_map/ppermute | solution.py:283
  104.5 31.1 %collective-permute-start.6 = (bf16[2,128,1024]{2,1,0:T(8,128)(2,1)}, bf16[2,128,1024]{2,1,0:T(8,128)(2,1)}, u32[]{:S(2)}, u32[]{:S(2)}) collective-permute-start(bf16[2,128,1024]{2,1,0:T(8,128)(2,1)} %get-tuple-element.33), channel_id=1, source_target_pairs={{0,32},{32,64},{64,96},{96,128},{128,160},{160,192},{192,224},{224... | collective-permute-start | bytes 1572872 | tf_op jit(solution)/shard_map/ppermute | solution.py:283
  135.6 1.0 copy-start.20
  140.4 0.7 copy-start.22
  141.1 12.8 %collective-permute-start.16 = (bf16[2,128,1024]{2,1,0:T(8,128)(2,1)S(1)}, bf16[2,128,1024]{2,1,0:T(8,128)(2,1)S(1)}, u32[]{:S(2)}, u32[]{:S(2)}) collective-permute-start(bf16[2,128,1024]{2,1,0:T(8,128)(2,1)S(1)} %get-tuple-element.27.refs_4_), channel_id=1, source_target_pairs={{0,32},{32,64},{64,96},{96,128},{128,160},{160,192},{192,224},{224... | collective-permute-start | bytes 1572872 | tf_op jit(solution)/shard_map/ppermute | solution.py:283
  142.2 13.2 %collective-permute-start.14 = (bf16[2,128,1024]{2,1,0:T(8,128)(2,1)S(1)}, bf16[2,128,1024]{2,1,0:T(8,128)(2,1)}, u32[]{:S(2)}, u32[]{:S(2)}) collective-permute-start(bf16[2,128,1024]{2,1,0:T(8,128)(2,1)S(1)} %get-tuple-element.27.refs_4_), channel_id=1, source_target_pairs={{0,224},{32,0},{64,32},{96,64},{128,96},{160,128},{192,160},{224,1... | collective-permute-start | bytes 1572872 | tf_op jit(solution)/shard_map/ppermute | solution.py:283
  144.3 0.8 copy-start.6
  153.9 13.8 %collective-permute-start.17 = (bf16[2,128,1024]{2,1,0:T(8,128)(2,1)S(1)}, bf16[2,128,1024]{2,1,0:T(8,128)(2,1)}, u32[]{:S(2)}, u32[]{:S(2)}) collective-permute-start(bf16[2,128,1024]{2,1,0:T(8,128)(2,1)S(1)} %collective-permute-done.16.refs_3_), channel_id=1, source_target_pairs={{0,32},{32,64},{64,96},{96,128},{128,160},{160,192},{192,224},{224... | collective-permute-start | bytes 1572872 | tf_op jit(solution)/shard_map/ppermute | solution.py:283
  154.6 0.8 copy-start.9
  155.4 21.1 %collective-permute-start.15 = (bf16[2,128,1024]{2,1,0:T(8,128)(2,1)}, bf16[2,128,1024]{2,1,0:T(8,128)(2,1)}, u32[]{:S(2)}, u32[]{:S(2)}) collective-permute-start(bf16[2,128,1024]{2,1,0:T(8,128)(2,1)} %collective-permute-done.14.refs_2_), channel_id=1, source_target_pairs={{0,224},{32,0},{64,32},{96,64},{128,96},{160,128},{192,160},{224,1... | collective-permute-start | bytes 1572872 | tf_op jit(solution)/shard_map/ppermute | solution.py:283
  158.6 12.2 %all-to-all-start.5 = ((bf16[16,32,128]{2,1,0:T(8,128)(2,1)}), bf16[16,32,128]{2,1,0:T(8,128)(2,1)}, u32[]{:S(2)}, u32[]{:S(2)}) async-start(bf16[16,32,128]{2,1,0:T(8,128)(2,1)} %broadcast_in_dim.60), calls=%async_computation.5 | async-start | bytes 262144 | tf_op jit(solution)/shard_map/all_to_all | solution.py:23
  167.6 35.2 %collective-permute-start.18 = (bf16[2,128,1024]{2,1,0:T(8,128)(2,1)}, bf16[2,128,1024]{2,1,0:T(8,128)(2,1)S(1)}, u32[]{:S(2)}, u32[]{:S(2)}) collective-permute-start(bf16[2,128,1024]{2,1,0:T(8,128)(2,1)} %collective-permute-done.17.refs_1_), channel_id=1, source_target_pairs={{0,32},{32,64},{64,96},{96,128},{128,160},{160,192},{192,224},{224... | collective-permute-start | bytes 1572872 | tf_op jit(solution)/shard_map/ppermute | solution.py:283
  172.4 13.2 %all-to-all-start.6 = ((bf16[8,64,128]{2,1,0:T(8,128)(2,1)}), bf16[8,64,128]{2,1,0:T(8,128)(2,1)S(1)}, u32[]{:S(2)}, u32[]{:S(2)}) async-start(bf16[8,64,128]{2,1,0:T(8,128)(2,1)} %broadcast_in_dim.61), calls=%async_computation.6 | async-start | bytes 262144 | tf_op jit(solution)/shard_map/all_to_all | solution.py:23
  176.5 27.6 %collective-permute-start.20 = (bf16[2,128,1024]{2,1,0:T(8,128)(2,1)}, bf16[2,128,1024]{2,1,0:T(8,128)(2,1)}, u32[]{:S(2)}, u32[]{:S(2)}) collective-permute-start(bf16[2,128,1024]{2,1,0:T(8,128)(2,1)} %collective-permute-done.15.refs_0_), channel_id=1, source_target_pairs={{0,224},{32,0},{64,32},{96,64},{128,96},{160,128},{192,160},{224,1... | collective-permute-start | bytes 1572872 | tf_op jit(solution)/shard_map/ppermute | solution.py:283
  185.6 2.2 copy-start.3
  187.8 1.0 copy-start.7
  188.8 1.0 copy-start.10
  195.1 1.1 copy-start.5
  196.1 30.2 %all-to-all-start.7 = ((bf16[16,40,1024]{2,1,0:T(8,128)(2,1)}), bf16[16,40,1024]{2,1,0:T(8,128)(2,1)}, u32[]{:S(2)}, u32[]{:S(2)}) async-start(bf16[16,40,1024]{2,1,0:T(8,128)(2,1)} %copy-done.5), calls=%async_computation.7 | async-start | bytes 2621440 | tf_op jit(solution)/shard_map/all_to_all | solution.py:391
  203.6 10.5 %collective-permute-start.19 = (bf16[128,1024]{1,0:T(8,128)(2,1)}, bf16[128,1024]{1,0:T(8,128)(2,1)}, u32[]{:S(2)}, u32[]{:S(2)}) collective-permute-start(bf16[128,1024]{1,0:T(8,128)(2,1)} %slice_bitcast_fusion.1), channel_id=1, source_target_pairs={{0,32},{32,64},{64,96},{96,128},{128,160},{160,192},{192,224},{224... | collective-permute-start | bytes 786440 | tf_op jit(solution)/shard_map/ppermute | solution.py:283
  205.8 8.2 %collective-permute-start.21 = (bf16[128,1024]{1,0:T(8,128)(2,1)}, bf16[128,1024]{1,0:T(8,128)(2,1)}, u32[]{:S(2)}, u32[]{:S(2)}) collective-permute-start(bf16[128,1024]{1,0:T(8,128)(2,1)} %slice_bitcast_fusion), channel_id=1, source_target_pairs={{0,224},{32,0},{64,32},{96,64},{128,96},{160,128},{192,160},{224,1... | collective-permute-start | bytes 786440 | tf_op jit(solution)/shard_map/ppermute | solution.py:283
  210.0 6.9 %collective-permute-start.13 = (bf16[16,8,512]{2,1,0:T(8,128)(2,1)}, bf16[16,8,512]{2,1,0:T(8,128)(2,1)}, u32[]{:S(2)}, u32[]{:S(2)}) collective-permute-start(bf16[16,8,512]{2,1,0:T(8,128)(2,1)} %dynamic-slice_bitcast_fusion), channel_id=1, source_target_pairs={{0,1},{1,0},{2,3},{3,2},{4,5},{5,4},{6,7},{7,6},{8,9},{9,8},{10,11... | collective-permute-start | bytes 393224 | tf_op jit(solution)/shard_map/ppermute | solution.py:280
  210.0 1.0 copy-start.8
  211.1 1.0 copy-start.11
  212.1 4.8 %copy-start.23 = (bf16[128,1024]{1,0:T(8,128)(2,1)S(1)}, bf16[128,1024]{1,0:T(8,128)(2,1)}, u32[]{:S(2)}) copy-start(bf16[128,1024]{1,0:T(8,128)(2,1)} %copy-done.22) | copy-start | bytes 786436
  214.1 7.6 %copy-start.4 = (bf16[2,1024,1024]{2,1,0:T(8,128)(2,1)S(1)}, bf16[2,1024,1024]{2,1,0:T(8,128)(2,1)}, u32[]{:S(2)}) copy-start(bf16[2,1024,1024]{2,1,0:T(8,128)(2,1)} %copy-done.1) | copy-start | bytes 12582916
  216.4 5.2 %copy-start.21 = (f32[2,32,1024]{2,1,0:T(8,128)}, f32[2,32,1024]{2,1,0:T(8,128)S(1)}, u32[]{:S(2)}) copy-start(f32[2,32,1024]{2,1,0:T(8,128)S(1)} %get-tuple-element.28) | copy-start | bytes 786436
  216.4 17.2 %collective-permute-start.23 = (bf16[2,32,1024]{2,1,0:T(8,128)(2,1)}, bf16[2,32,1024]{2,1,0:T(8,128)(2,1)}, u32[]{:S(2)}, u32[]{:S(2)}) collective-permute-start(bf16[2,32,1024]{2,1,0:T(8,128)(2,1)} %get-tuple-element.29), channel_id=1, source_target_pairs={{0,1},{1,0},{2,3},{3,2},{4,5},{5,4},{6,7},{7,6},{8,9},{9,8},{10,11... | collective-permute-start | bytes 393224 | tf_op jit(solution)/shard_map/ppermute | solution.py:280
  220.7 0.7 copy-start.16
  221.4 24.6 %collective-permute-start.22 = (f32[32,1024]{1,0:T(8,128)S(1)}, f32[32,1024]{1,0:T(8,128)S(1)}, u32[]{:S(2)}, u32[]{:S(2)}) collective-permute-start(f32[32,1024]{1,0:T(8,128)S(1)} %slice.60), channel_id=1, source_target_pairs={{0,1},{1,0},{2,3},{3,2},{4,5},{5,4},{6,7},{7,6},{8,9},{9,8},{10,11... | collective-permute-start | bytes 393224 | tf_op jit(solution)/shard_map/ppermute | solution.py:280
  226.3 19.7 %copy-start.17 = (f32[64,1024]{1,0:T(8,128)S(1)}, f32[64,1024]{1,0:T(8,128)}, u32[]{:S(2)}) copy-start(f32[64,1024]{1,0:T(8,128)} %copy-done.16) | copy-start | bytes 786436
  226.3 23.7 %all-to-all-start.8 = ((bf16[16,24,1024]{2,1,0:T(8,128)(2,1)}), bf16[16,24,1024]{2,1,0:T(8,128)(2,1)S(1)}, u32[]{:S(2)}, u32[]{:S(2)}) async-start(bf16[16,24,1024]{2,1,0:T(8,128)(2,1)} %shard_map.117), calls=%async_computation.8 | async-start | bytes 1572864 | tf_op jit(solution)/shard_map/all_to_all | solution.py:391
  234.7 14.0 %collective-permute-start.24 = (bf16[2,16,1024]{2,1,0:T(8,128)(2,1)S(1)}, bf16[2,16,1024]{2,1,0:T(8,128)(2,1)S(1)}, u32[]{:S(2)}, u32[]{:S(2)}) collective-permute-start(bf16[2,16,1024]{2,1,0:T(8,128)(2,1)S(1)} %get-tuple-element.42), channel_id=1, source_target_pairs={{0,0},{2,2},{4,32},{6,34},{8,64},{10,66},{12,96},{14,98},{16,128},... | collective-permute-start | bytes 196616 | tf_op jit(solution)/shard_map/ppermute | solution.py:431
  236.7 13.2 %collective-permute-start.25 = (bf16[2,16,1024]{2,1,0:T(8,128)(2,1)S(1)}, bf16[2,16,1024]{2,1,0:T(8,128)(2,1)S(1)}, u32[]{:S(2)}, u32[]{:S(2)}) collective-permute-start(bf16[2,16,1024]{2,1,0:T(8,128)(2,1)S(1)} %get-tuple-element.43), channel_id=1, source_target_pairs={{0,2},{2,0},{4,34},{6,32},{8,66},{10,64},{12,98},{14,96},{16,130},... | collective-permute-start | bytes 196616 | tf_op jit(solution)/shard_map/ppermute | solution.py:432
  252.2 18.6 %all-to-all-start.9 = ((bf16[8,8,1024]{2,1,0:T(8,128)(2,1)}), bf16[8,8,1024]{2,1,0:T(8,128)(2,1)S(1)}, u32[]{:S(2)}, u32[]{:S(2)}) async-start(bf16[8,8,1024]{2,1,0:T(8,128)(2,1)} %shard_map.118), calls=%async_computation.9 | async-start | bytes 262144 | tf_op jit(solution)/shard_map/all_to_all | solution.py:396
